TPU v7x, 32 devices: a whole 2x2x4 slice. The times are simulated.
32 devices in a mesh: batch: 8 (over y, x, core), tensor: 4 (over z).
Axes of the slice: x: 2, y: 2, z: 4, core: 2. Of those that a mesh axis runs over, the one named last changes fastest.
Arguments:
- slot_states: bfloat16 [960, 32, 768], P('tensor', 'batch'), may hold values from -6 to 6
- pass_counts: int32 [32], P('batch'), may hold values from 2 to 5
- w_qkv: bfloat16 [768, 3, 768], P(None, None, 'tensor'), may hold values from -0.21875 to 0.21875
- q_bias: bfloat16 [768], P('tensor'), may hold values from -3 to 3
- v_bias: bfloat16 [768], P('tensor'), may hold values from -0.29882812 to 0.29882812
- w_out: bfloat16 [768, 768], P('tensor'), may hold values from -1.75 to 1.75
- out_bias: bfloat16 [768], replicated, may hold values from -3 to 3
- w_up: bfloat16 [768, 3072], P(None, 'tensor'), may hold values from -0.21875 to 0.21875
- up_bias: bfloat16 [3072], P('tensor'), may hold values from -3 to 3
- w_down: bfloat16 [3072, 768], P('tensor'), may hold values from -0.109375 to 0.109375
- down_bias: bfloat16 [768], replicated, may hold values from -3 to 3
- ln1_gain: bfloat16 [768], replicated, may hold values from 0.099609375 to 1.8984375
- ln1_bias: bfloat16 [768], replicated, may hold values from -2 to 2
- ln2_gain: bfloat16 [768], replicated, may hold values from 0.099609375 to 1.8984375
- ln2_bias: bfloat16 [768], replicated, may hold values from -2 to 2
- pass_table: bfloat16 [5, 768], replicated, may hold values from -5 to 5
- cotangent: bfloat16 [960, 32, 768], P('tensor', 'batch'), may hold values from -6 to 6
Outputs:
- layer_out: bfloat16 [960, 32, 768], P('tensor', 'batch')
- grad_states: bfloat16 [960, 32, 768], P('tensor', 'batch')
- grad_qkv: float32 [768, 3, 768], P(None, None, 'tensor')
- grad_q_bias: float32 [768], P('tensor')
- grad_v_bias: float32 [768], P('tensor')
- grad_out: float32 [768, 768], P('tensor')
- grad_out_bias: float32 [768], replicated
- grad_up: float32 [768, 3072], P(None, 'tensor')
- grad_up_bias: float32 [3072], P('tensor')
- grad_down: float32 [3072, 768], P('tensor')
- grad_down_bias: float32 [768], replicated
- grad_ln1_gain: float32 [768], replicated
- grad_ln1_bias: float32 [768], replicated
- grad_ln2_gain: float32 [768], replicated
- grad_ln2_bias: float32 [768], replicated
- grad_pass: float32 [5, 768], replicated
All inputs are finite; a program needn't handle non-finite values.
Results may differ from a plain program's by a relative error of at most 0.02.
Values may be sent and summed in bfloat16 or wider, within the bound.
No kernel may reach another device: no remote copies, remote signals or barrier semaphores. Data moves between devices by JAX's collectives and lax.ppermute only.
A program may use at most 256 MiB of HBM per device.

v0:
```python
import math

import jax
import jax.numpy as jnp
from jax import lax
from jax.sharding import PartitionSpec as P

HEAD_DIM = 64
PASSES = 5
LEN = 192
MICRO = 4
SEQ_DEV = 1


HIGHEST = lax.Precision.HIGHEST
EPSILON = 1e-05
MASKED = -1e30


def norm_rows(values, gain, shift):
    center = values - jnp.mean(values, axis=-1, keepdims=True)
    spread = jnp.mean(center * center, axis=-1, keepdims=True)
    return center * lax.rsqrt(spread + EPSILON) * gain + shift


def gelu_tanh(values):
    return jax.nn.gelu(values, approximate=True)


def block_scores(query, keys, allowed, scale):
    scores = jnp.einsum("qbhd,kbhd->bhqk", query, keys, preferred_element_type=jnp.float32) * scale
    return jnp.where(allowed, scores, MASKED)


def attend_block(query, keys, values, allowed, scale):
    scores = block_scores(query, keys, allowed, scale)
    peak = jnp.max(scores, axis=-1, keepdims=True)
    powers = jnp.exp(scores - peak)
    total = jnp.sum(powers, axis=-1, keepdims=True)
    weights = (powers / total).astype(jnp.bfloat16)
    mixed = jnp.einsum("bhqk,kbhd->qbhd", weights, values, preferred_element_type=jnp.float32)
    return (mixed.astype(jnp.bfloat16), peak + jnp.log(total))


def attend_back(query, keys, values, allowed, log_total, grad_mixed, scale):
    scores = block_scores(query, keys, allowed, scale)
    probs = jnp.exp(scores - log_total)
    grad_weights = jnp.einsum(
        "qbhd,kbhd->bhqk", grad_mixed, values, preferred_element_type=jnp.float32
    )
    inner = jnp.sum(probs * grad_weights, axis=-1, keepdims=True)
    grad_scores = (probs * (grad_weights - inner)).astype(jnp.bfloat16)
    grad_query = (
        jnp.einsum("bhqk,kbhd->qbhd", grad_scores, keys, preferred_element_type=jnp.float32) * scale
    )
    grad_keys = (
        jnp.einsum("bhqk,qbhd->kbhd", grad_scores, query, preferred_element_type=jnp.float32)
        * scale
    )
    grad_values = jnp.einsum(
        "bhqk,qbhd->kbhd",
        probs.astype(jnp.bfloat16),
        grad_mixed,
        preferred_element_type=jnp.float32,
    )
    return (grad_query, grad_keys, grad_values)


def layer_block(states, counts, cot_rows, row_index, slots, weights, norms, links):
    qkv_matrix, q_bias, v_bias, w_out, bias_output, w_up, bias_upward, w_down, bias_downward = (
        weights
    )
    gain_one, shift_one, gain_two, shift_two, table = norms
    (
        gather_first,
        sum_attn,
        gather_second,
        sum_mlp,
        gather_grad,
        sum_upward,
        gather_attn,
        sum_qkv,
    ) = links
    width = states.shape[2]
    nseq = states.shape[1]
    local_width = qkv_matrix.shape[1] // 3
    heads_here = local_width // HEAD_DIM
    scale = 1.0 / math.sqrt(HEAD_DIM)
    full_index = jnp.arange(slots, dtype=jnp.int32)
    bias_query = q_bias.astype(jnp.float32).reshape(heads_here, HEAD_DIM)
    bias_value = v_bias.astype(jnp.float32).reshape(heads_here, HEAD_DIM)
    passes = row_index[:, None] % counts[None, :]
    onehot = (passes[:, :, None] == jnp.arange(PASSES, dtype=jnp.int32)[None, None, :]).astype(
        jnp.float32
    )
    live_rows = row_index[:, None] < counts[None, :] * LEN
    allowed = (full_index[None, None, :] <= full_index[None, :, None]) & (
        full_index[None, None, :] < (counts * LEN)[:, None, None]
    )
    hidden = states + jnp.einsum("rbp,pd->rbd", onehot, table, precision=HIGHEST)
    norm_one, pull_one = jax.vjp(norm_rows, hidden, gain_one, shift_one)
    gathered_one = gather_first(norm_one.astype(jnp.bfloat16))
    projected = jnp.einsum(
        "sbd,dc->sbc", gathered_one, qkv_matrix, preferred_element_type=jnp.float32
    )
    projected = projected.reshape(slots, nseq, 3, heads_here, HEAD_DIM)
    query = (projected[:, :, 0] + bias_query).astype(jnp.bfloat16)
    keys = projected[:, :, 1].astype(jnp.bfloat16)
    values = (projected[:, :, 2] + bias_value).astype(jnp.bfloat16)
    piece_number = 0
    begin = piece_number * slots
    mixed, log_total = attend_block(
        query, keys, values, allowed[:, None, begin : begin + slots], scale
    )
    log_blocks = [log_total]
    mixed_flat = mixed.reshape(slots, nseq, local_width)

    def attn_term(start, count):
        return jnp.einsum("sbc,cd->sbd", mixed_flat, w_out, preferred_element_type=jnp.float32)

    attn_total = sum_attn(attn_term)
    after = hidden + attn_total + bias_output
    norm_two, pull_two = jax.vjp(norm_rows, after, gain_two, shift_two)
    gathered_two = gather_second(norm_two.astype(jnp.bfloat16))
    pre_act = (
        jnp.einsum("sbd,df->sbf", gathered_two, w_up, preferred_element_type=jnp.float32)
        + bias_upward
    )
    activated, pull_act = jax.vjp(gelu_tanh, pre_act)
    act_low = activated.astype(jnp.bfloat16)

    def mlp_term(start, count):
        return jnp.einsum("sbf,fd->sbd", act_low, w_down, preferred_element_type=jnp.float32)

    mlp_total = sum_mlp(mlp_term)
    result = after + mlp_total + bias_downward
    layer_part = jnp.where(live_rows[:, :, None], result, 0.0).astype(jnp.bfloat16)
    grad_result = jnp.where(live_rows[:, :, None], cot_rows.astype(jnp.float32), 0.0)
    grad_branch = gather_grad(grad_result.astype(jnp.bfloat16))
    grad_down_part = jnp.einsum(
        "sbf,sbd->fd", act_low, grad_branch, preferred_element_type=jnp.float32
    )
    grad_act = jnp.einsum("sbd,fd->sbf", grad_branch, w_down, preferred_element_type=jnp.float32)
    grad_pre = pull_act(grad_act)[0].astype(jnp.bfloat16)
    grad_up_part = jnp.einsum(
        "sbd,sbf->df", gathered_two, grad_pre, preferred_element_type=jnp.float32
    )
    grad_up_bias_part = jnp.sum(grad_pre.astype(jnp.float32), axis=(0, 1))

    def upward_term(start, count):
        return jnp.einsum("sbf,df->sbd", grad_pre, w_up, preferred_element_type=jnp.float32)

    grad_norm_two = sum_upward(upward_term)
    grad_after, grad_gain_two, grad_shift_two = pull_two(grad_norm_two)
    grad_after = grad_after + grad_result
    grad_out_bias_part = jnp.sum(grad_after, axis=(0, 1))
    grad_down_bias_part = jnp.sum(grad_result, axis=(0, 1))
    grad_attn = gather_attn(grad_after.astype(jnp.bfloat16))
    grad_out_part = jnp.einsum(
        "sbc,sbd->cd", mixed_flat, grad_attn, preferred_element_type=jnp.float32
    )
    grad_mixed = jnp.einsum("sbd,cd->sbc", grad_attn, w_out, preferred_element_type=jnp.float32)
    grad_mixed = grad_mixed.astype(jnp.bfloat16).reshape(slots, nseq, heads_here, HEAD_DIM)
    piece_number = 0
    begin = piece_number * slots
    grad_query, grad_keys, grad_values = attend_back(
        query,
        keys,
        values,
        allowed[:, None, begin : begin + slots],
        log_blocks[piece_number],
        grad_mixed,
        scale,
    )
    grad_proj = jnp.stack([grad_query, grad_keys, grad_values], axis=2)
    grad_proj = grad_proj.astype(jnp.bfloat16).reshape(slots, nseq, 3 * local_width)
    grad_qkv_part = jnp.einsum(
        "sbd,sbc->dc", gathered_one, grad_proj, preferred_element_type=jnp.float32
    ).reshape(width, 3, local_width)
    rounded_proj = grad_proj.astype(jnp.float32).reshape(slots, nseq, 3, local_width)
    grad_q_bias_part = jnp.sum(rounded_proj[:, :, 0], axis=(0, 1))
    grad_v_bias_part = jnp.sum(rounded_proj[:, :, 2], axis=(0, 1))

    def qkv_term(start, count):
        return jnp.einsum("sbc,dc->sbd", grad_proj, qkv_matrix, preferred_element_type=jnp.float32)

    grad_norm_one = sum_qkv(qkv_term)
    grad_hidden, grad_gain_one, grad_shift_one = pull_one(grad_norm_one)
    grad_hidden = grad_hidden + grad_after
    grad_part = grad_hidden.astype(jnp.bfloat16)
    grad_pass_part = jnp.einsum("rbp,rbd->pd", onehot, grad_hidden, precision=HIGHEST)
    matrices = (grad_qkv_part, grad_out_part, grad_up_part, grad_down_part)
    shared = (
        grad_gain_one,
        grad_shift_one,
        grad_gain_two,
        grad_shift_two,
        grad_out_bias_part,
        grad_down_bias_part,
        grad_pass_part,
    )
    biases = (grad_q_bias_part, grad_v_bias_part, grad_up_bias_part)
    return (layer_part, grad_part, matrices, shared, biases)


def add_tuples(old, new):
    if old is None:
        return new
    return tuple((first + second for first, second in zip(old, new)))


def per_device(
    slot_states,
    pass_counts,
    w_qkv,
    q_bias,
    v_bias,
    w_out,
    out_bias,
    w_up,
    up_bias,
    w_down,
    down_bias,
    ln1_gain,
    ln1_bias,
    ln2_gain,
    ln2_bias,
    pass_table,
    cotangent,
):
    groups = lax.axis_size("tensor")
    rows = slot_states.shape[0]
    slots = rows * groups
    norms = (
        ln1_gain.astype(jnp.float32),
        ln1_bias.astype(jnp.float32),
        ln2_gain.astype(jnp.float32),
        ln2_bias.astype(jnp.float32),
        pass_table.astype(jnp.float32),
    )
    bias_output = out_bias.astype(jnp.float32)
    bias_downward = down_bias.astype(jnp.float32)
    layer_parts = []
    grad_parts = []
    matrix_totals = None
    shared_totals = None
    bias_totals = None
    width = slot_states.shape[2]
    weights = (
        w_qkv.reshape(width, 3 * w_qkv.shape[2]),
        q_bias,
        v_bias,
        w_out,
        bias_output,
        w_up,
        up_bias.astype(jnp.float32),
        w_down,
        bias_downward,
    )
    row_index = lax.axis_index("tensor") * rows + jnp.arange(rows, dtype=jnp.int32)

    def gather_first(values):
        return lax.all_gather(values, "tensor", axis=0, tiled=True)

    def sum_attn(term):
        return lax.psum_scatter(
            term(jnp.int32(0), lax.axis_size("tensor") * rows).astype(jnp.bfloat16),
            "tensor",
            scatter_dimension=0,
            tiled=True,
        ).astype(jnp.float32)

    def gather_second(values):
        return lax.all_gather(values, "tensor", axis=0, tiled=True)

    def sum_mlp(term):
        return lax.psum_scatter(
            term(jnp.int32(0), lax.axis_size("tensor") * rows).astype(jnp.bfloat16),
            "tensor",
            scatter_dimension=0,
            tiled=True,
        ).astype(jnp.float32)

    def gather_grad(values):
        return lax.all_gather(values, "tensor", axis=0, tiled=True)

    def sum_upward(term):
        return lax.psum_scatter(
            term(jnp.int32(0), lax.axis_size("tensor") * rows).astype(jnp.bfloat16),
            "tensor",
            scatter_dimension=0,
            tiled=True,
        ).astype(jnp.float32)

    def gather_attn(values):
        return lax.all_gather(values, "tensor", axis=0, tiled=True)

    def sum_qkv(term):
        return lax.psum_scatter(
            term(jnp.int32(0), lax.axis_size("tensor") * rows).astype(jnp.bfloat16),
            "tensor",
            scatter_dimension=0,
            tiled=True,
        ).astype(jnp.float32)

    links = (
        gather_first,
        sum_attn,
        gather_second,
        sum_mlp,
        gather_grad,
        sum_upward,
        gather_attn,
        sum_qkv,
    )
    for micro in range(MICRO):
        first_seq = micro * SEQ_DEV
        layer_part, grad_part, matrices, shared, biases = layer_block(
            slot_states[:, first_seq : first_seq + SEQ_DEV].astype(jnp.float32),
            pass_counts[first_seq : first_seq + SEQ_DEV],
            cotangent[:, first_seq : first_seq + SEQ_DEV],
            row_index,
            slots,
            weights,
            norms,
            links,
        )
        layer_parts.append(layer_part)
        grad_parts.append(grad_part)
        matrices = (
            lax.psum_scatter(matrices[0], "batch", scatter_dimension=0, tiled=True),
            lax.psum_scatter(matrices[1], "batch", scatter_dimension=0, tiled=True),
            lax.psum_scatter(matrices[2], "batch", scatter_dimension=0, tiled=True),
            lax.psum_scatter(matrices[3], "batch", scatter_dimension=0, tiled=True),
        )
        matrix_totals = add_tuples(matrix_totals, matrices)
        shared_totals = add_tuples(shared_totals, shared)
        bias_totals = add_tuples(bias_totals, biases)
    layer_out = jnp.concatenate(layer_parts, axis=1)
    grad_states = jnp.concatenate(grad_parts, axis=1)
    whole = (
        lax.all_gather(matrix_totals[0].astype(jnp.bfloat16), "batch", axis=0, tiled=True).astype(
            jnp.float32
        ),
        lax.all_gather(matrix_totals[1].astype(jnp.bfloat16), "batch", axis=0, tiled=True).astype(
            jnp.float32
        ),
        lax.all_gather(matrix_totals[2].astype(jnp.bfloat16), "batch", axis=0, tiled=True).astype(
            jnp.float32
        ),
        lax.all_gather(matrix_totals[3].astype(jnp.bfloat16), "batch", axis=0, tiled=True).astype(
            jnp.float32
        ),
    )
    shared_sum = lax.psum(
        (
            shared_totals[0],
            shared_totals[1],
            shared_totals[2],
            shared_totals[3],
            shared_totals[4],
            shared_totals[5],
            shared_totals[6],
        ),
        ("batch", "tensor"),
    )
    bias_sum = lax.psum((bias_totals[0], bias_totals[1], bias_totals[2]), "batch")
    return (
        layer_out,
        grad_states,
        whole[0],
        bias_sum[0],
        bias_sum[1],
        whole[1],
        shared_sum[4],
        whole[2],
        bias_sum[2],
        whole[3],
        shared_sum[5],
        shared_sum[0],
        shared_sum[1],
        shared_sum[2],
        shared_sum[3],
        shared_sum[6],
    )


def solution(mesh):
    in_specs = (
        P("tensor", "batch", None),
        P("batch"),
        P(None, None, "tensor"),
        P("tensor"),
        P("tensor"),
        P("tensor", None),
        P(),
        P(None, "tensor"),
        P("tensor"),
        P("tensor", None),
        P(),
        P(),
        P(),
        P(),
        P(),
        P(),
        P("tensor", "batch", None),
    )
    out_specs = (
        P("tensor", "batch", None),
        P("tensor", "batch", None),
        P(None, None, "tensor"),
        P("tensor"),
        P("tensor"),
        P("tensor", None),
        P(),
        P(None, "tensor"),
        P("tensor"),
        P("tensor", None),
        P(),
        P(),
        P(),
        P(),
        P(),
        P(),
    )
    return jax.shard_map(
        per_device, mesh=mesh, in_specs=in_specs, out_specs=out_specs, check_vma=False
    )
```

profile of v0, /device:TPU:0, one launch (start us, length us, event | category | flops | bytes accessed | tf_op | source)
XLA Modules:
  0.0 1458.4 jit_solution(311594064871290279)
XLA Ops:
  37.1 29.8 %all-gather.19.cloned.1.call-done = bf16[960,1,768]{2,0,1:T(8,128)(2,1)} async-done(((bf16[240,1,768]{2,0,1:T(8,128)(2,1)}), bf16[960,1,768]{2,0,1:T(8,128)(2,1)}) %all-gather.19.cloned.1.call-update) | async-done | bytes 1474576 | tf_op jit(solution)/shard_map/all_gather | solution.py:263
  211.3 35.5 %reduce-scatter.25.cloned.1.call-done = bf16[240,1,768]{2,0,1:T(8,128)(2,1)} async-done(((bf16[960,1,768]{2,0,1:T(8,128)(2,1)}), bf16[240,1,768]{2,0,1:T(8,128)(2,1)}) %reduce-scatter.25.cloned.1.call-update) | async-done | bytes 368656 | tf_op jit(solution)/shard_map/reduce_scatter | solution.py:266
  246.8 35.6 %reduce-scatter.29.cloned.1.call-done = bf16[240,1,768]{2,0,1:T(8,128)(2,1)} async-done(((bf16[960,1,768]{2,0,1:T(8,128)(2,1)}), bf16[240,1,768]{2,0,1:T(8,128)(2,1)}) %reduce-scatter.29.cloned.1.call-update) | async-done | bytes 368656 | tf_op jit(solution)/shard_map/reduce_scatter | solution.py:266
  282.4 35.0 %reduce-scatter.33.cloned.1.call-done = bf16[240,1,768]{2,0,1:T(8,128)(2,1)} async-done(((bf16[960,1,768]{2,0,1:T(8,128)(2,1)}), bf16[240,1,768]{2,0,1:T(8,128)(2,1)}) %reduce-scatter.33.cloned.1.call-update) | async-done | bytes 368656 | tf_op jit(solution)/shard_map/reduce_scatter | solution.py:266
  361.6 31.1 %all-gather.47.cloned.1.call-done = bf16[960,1,768]{2,0,1:T(8,128)(2,1)} async-done(((bf16[240,1,768]{2,0,1:T(8,128)(2,1)}), bf16[960,1,768]{2,0,1:T(8,128)(2,1)}) %all-gather.47.cloned.1.call-update) | async-done | bytes 1474576 | tf_op jit(solution)/shard_map/all_gather | solution.py:285
  402.4 26.7 %all-gather.29.cloned.1.call-done = bf16[960,1,768]{2,0,1:T(8,128)(2,1)} async-done(((bf16[240,1,768]{2,0,1:T(8,128)(2,1)}), bf16[960,1,768]{2,0,1:T(8,128)(2,1)}) %all-gather.29.cloned.1.call-update) | async-done | bytes 1474576 | tf_op jit(solution)/shard_map/all_gather | solution.py:274
  433.8 31.1 %all-gather.43.cloned.1.call-done = bf16[960,1,768]{2,0,1:T(8,128)(2,1)} async-done(((bf16[240,1,768]{2,0,1:T(8,128)(2,1)}), bf16[960,1,768]{2,0,1:T(8,128)(2,1)}) %all-gather.43.cloned.1.call-update) | async-done | bytes 1474576 | tf_op jit(solution)/shard_map/all_gather | solution.py:285
  505.4 31.1 %all-gather.39.cloned.1.call-done = bf16[960,1,768]{2,0,1:T(8,128)(2,1)} async-done(((bf16[240,1,768]{2,0,1:T(8,128)(2,1)}), bf16[960,1,768]{2,0,1:T(8,128)(2,1)}) %all-gather.39.cloned.1.call-update) | async-done | bytes 1474576 | tf_op jit(solution)/shard_map/all_gather | solution.py:285
  546.2 26.7 %all-gather.21.cloned.1.call-done = bf16[960,1,768]{2,0,1:T(8,128)(2,1)} async-done(((bf16[240,1,768]{2,0,1:T(8,128)(2,1)}), bf16[960,1,768]{2,0,1:T(8,128)(2,1)}) %all-gather.21.cloned.1.call-update) | async-done | bytes 1474576 | tf_op jit(solution)/shard_map/all_gather | solution.py:274
  577.5 31.1 %all-gather.35.cloned.1.call-done = bf16[960,1,768]{2,0,1:T(8,128)(2,1)} async-done(((bf16[240,1,768]{2,0,1:T(8,128)(2,1)}), bf16[960,1,768]{2,0,1:T(8,128)(2,1)}) %all-gather.35.cloned.1.call-update) | async-done | bytes 1474576 | tf_op jit(solution)/shard_map/all_gather | solution.py:285
  683.8 31.0 %reduce-scatter.31.cloned.1.call-done = bf16[240,1,768]{2,0,1:T(8,128)(2,1)} async-done(((bf16[960,1,768]{2,0,1:T(8,128)(2,1)}), bf16[240,1,768]{2,0,1:T(8,128)(2,1)}) %reduce-scatter.31.cloned.1.call-update) | async-done | bytes 368656 | tf_op jit(solution)/shard_map/reduce_scatter | solution.py:277
  714.7 34.9 %reduce-scatter.41.cloned.1.call-done = bf16[240,1,768]{2,0,1:T(8,128)(2,1)} async-done(((bf16[960,1,768]{2,0,1:T(8,128)(2,1)}), bf16[240,1,768]{2,0,1:T(8,128)(2,1)}) %reduce-scatter.41.cloned.1.call-update) | async-done | bytes 368656 | tf_op jit(solution)/shard_map/reduce_scatter | solution.py:288
  749.6 35.6 %reduce-scatter.37.cloned.1.call-done = bf16[240,1,768]{2,0,1:T(8,128)(2,1)} async-done(((bf16[960,1,768]{2,0,1:T(8,128)(2,1)}), bf16[240,1,768]{2,0,1:T(8,128)(2,1)}) %reduce-scatter.37.cloned.1.call-update) | async-done | bytes 368656 | tf_op jit(solution)/shard_map/reduce_scatter | solution.py:288
  789.2 31.1 %reduce-scatter.35.cloned.1.call-done = bf16[240,1,768]{2,0,1:T(8,128)(2,1)} async-done(((bf16[960,1,768]{2,0,1:T(8,128)(2,1)}), bf16[240,1,768]{2,0,1:T(8,128)(2,1)}) %reduce-scatter.35.cloned.1.call-update) | async-done | bytes 368656 | tf_op jit(solution)/shard_map/reduce_scatter | solution.py:277
  823.8 31.5 %reduce-scatter.23.cloned.1.call-done = bf16[240,1,768]{2,0,1:T(8,128)(2,1)} async-done(((bf16[960,1,768]{2,0,1:T(8,128)(2,1)}), bf16[240,1,768]{2,0,1:T(8,128)(2,1)}) %reduce-scatter.23.cloned.1.call-update) | async-done | bytes 368656 | tf_op jit(solution)/shard_map/reduce_scatter | solution.py:277
  858.9 31.3 %reduce-scatter.27.cloned.1.call-done = bf16[240,1,768]{2,0,1:T(8,128)(2,1)} async-done(((bf16[960,1,768]{2,0,1:T(8,128)(2,1)}), bf16[240,1,768]{2,0,1:T(8,128)(2,1)}) %reduce-scatter.27.cloned.1.call-update) | async-done | bytes 368656 | tf_op jit(solution)/shard_map/reduce_scatter | solution.py:277
  897.5 37.2 %reduce-scatter.57.cloned.1.call-done = f32[96,768]{1,0:T(8,128)} async-done(((f32[768,768]{1,0:T(8,128)}), f32[96,768]{1,0:T(8,128)}) %reduce-scatter.57.cloned.1.call-update) | async-done | bytes 294928 | tf_op jit(solution)/shard_map/reduce_scatter | solution.py:333
  936.6 43.7 %reduce-scatter.59.cloned.1.call-done = f32[96,768]{1,0:T(8,128)} async-done(((f32[768,768]{1,0:T(8,128)}), f32[96,768]{1,0:T(8,128)}) %reduce-scatter.59.cloned.1.call-update) | async-done | bytes 294928 | tf_op jit(solution)/shard_map/reduce_scatter | solution.py:334
  982.3 35.4 %all-gather.41.cloned.1.call-done = bf16[960,1,768]{2,0,1:T(8,128)(2,1)} async-done(((bf16[240,1,768]{2,0,1:T(8,128)(2,1)}), bf16[960,1,768]{2,0,1:T(8,128)(2,1)}) %all-gather.41.cloned.1.call-update) | async-done | bytes 1474576 | tf_op jit(solution)/shard_map/all_gather | solution.py:296
  1236.2 24.5 %reduce-scatter.53.cloned.1.call-done = f32[96,3,192]{2,0,1:T(8,128)} async-done(((f32[768,3,192]{2,0,1:T(8,128)}), f32[96,3,192]{2,0,1:T(8,128)}) %reduce-scatter.53.cloned.1.call-update) | async-done | bytes 221200 | tf_op jit(solution)/shard_map/reduce_scatter | solution.py:331
  1298.3 33.5 %reduce-scatter.43.cloned.1.call-done = bf16[240,1,768]{2,0,1:T(8,128)(2,1)} async-done(((bf16[960,1,768]{2,0,1:T(8,128)(2,1)}), bf16[240,1,768]{2,0,1:T(8,128)(2,1)}) %reduce-scatter.43.cloned.1.call-update) | async-done | bytes 368656 | tf_op jit(solution)/shard_map/reduce_scatter | solution.py:299
  1331.9 34.9 %reduce-scatter.47.cloned.1.call-done = bf16[240,1,768]{2,0,1:T(8,128)(2,1)} async-done(((bf16[960,1,768]{2,0,1:T(8,128)(2,1)}), bf16[240,1,768]{2,0,1:T(8,128)(2,1)}) %reduce-scatter.47.cloned.1.call-update) | async-done | bytes 368656 | tf_op jit(solution)/shard_map/reduce_scatter | solution.py:299
  1366.8 35.6 %reduce-scatter.39.cloned.1.call-done = bf16[240,1,768]{2,0,1:T(8,128)(2,1)} async-done(((bf16[960,1,768]{2,0,1:T(8,128)(2,1)}), bf16[240,1,768]{2,0,1:T(8,128)(2,1)}) %reduce-scatter.39.cloned.1.call-update) | async-done | bytes 368656 | tf_op jit(solution)/shard_map/reduce_scatter | solution.py:299
  1411.3 40.3 %all-reduce = (f32[768]{0:T(1024)}, f32[768]{0:T(1024)}, f32[768]{0:T(1024)}, f32[768]{0:T(1024)}, f32[768]{0:T(1024)}, /*index=5*/f32[768]{0:T(1024)}, f32[5,768]{1,0:T(8,128)}) all-reduce(f32[768]{0:T(1024)S(1)} %add_add_fusion.33, f32[768]{0:T(1024)S(1)} %add_add_fusion.31, ...), channel_id=1, replica_groups=mesh['batch'=8,'tensor'=4] {'batch','tensor'}, use_global_device_ids=true, to_apply=%region_82.84 | all-reduce | flops 8448 | bytes 67584 | tf_op jit(solution)/shard_map/psum | solution.py:355
  (700 shorter events, 636.4 us)
Async XLA Ops:
  30.8 180.5 %reduce-scatter.21.cloned.1.call-start = ((), (), s32[]{:S(2)}) async-start(), calls=%async_computation.21 | async-start | bytes 1843200 | tf_op jit(solution)/shard_map/reduce_scatter | solution.py:266
  81.6 165.2 %reduce-scatter.25.cloned.1.call-start = ((), (), s32[]{:S(2)}) async-start(), calls=%async_computation.25 | async-start | bytes 1843200 | tf_op jit(solution)/shard_map/reduce_scatter | solution.py:266
  189.9 167.1 %all-gather.33.cloned.1.call-start = ((), (), s32[]{:S(2)}) async-start(), calls=%async_computation.34 | async-start | bytes 1843200 | tf_op jit(solution)/shard_map/all_gather | solution.py:274
  337.5 199.1 %all-gather.39.cloned.1.call-start = ((), (), s32[]{:S(2)}) async-start(), calls=%async_computation.40 | async-start | bytes 1843200 | tf_op jit(solution)/shard_map/all_gather | solution.py:285
  340.8 232.0 %all-gather.21.cloned.1.call-start = ((), (), s32[]{:S(2)}) async-start(), calls=%async_computation.22 | async-start | bytes 1843200 | tf_op jit(solution)/shard_map/all_gather | solution.py:274
  341.4 267.2 %all-gather.35.cloned.1.call-start = ((), (), s32[]{:S(2)}) async-start(), calls=%async_computation.36 | async-start | bytes 1843200 | tf_op jit(solution)/shard_map/all_gather | solution.py:285
  344.8 312.1 %reduce-scatter.49.cloned.1.call-start = ((), (), s32[]{:S(2)}) async-start(), calls=%async_computation.49 | async-start | bytes 1843200 | tf_op jit(solution)/shard_map/reduce_scatter | solution.py:288
  402.4 276.8 %reduce-scatter.45.cloned.1.call-start = ((), (), s32[]{:S(2)}) async-start(), calls=%async_computation.45 | async-start | bytes 1843200 | tf_op jit(solution)/shard_map/reduce_scatter | solution.py:288
  474.6 240.2 %reduce-scatter.31.cloned.1.call-start = ((), (), s32[]{:S(2)}) async-start(), calls=%async_computation.31 | async-start | bytes 1843200 | tf_op jit(solution)/shard_map/reduce_scatter | solution.py:277
  479.6 270.1 %reduce-scatter.41.cloned.1.call-start = ((), (), s32[]{:S(2)}) async-start(), calls=%async_computation.41 | async-start | bytes 1843200 | tf_op jit(solution)/shard_map/reduce_scatter | solution.py:288
  546.1 239.1 %reduce-scatter.37.cloned.1.call-start = ((), (), s32[]{:S(2)}) async-start(), calls=%async_computation.37 | async-start | bytes 1843200 | tf_op jit(solution)/shard_map/reduce_scatter | solution.py:288
  618.2 202.0 %reduce-scatter.35.cloned.1.call-start = ((), (), s32[]{:S(2)}) async-start(), calls=%async_computation.35 | async-start | bytes 1843200 | tf_op jit(solution)/shard_map/reduce_scatter | solution.py:277
  623.3 232.1 %reduce-scatter.23.cloned.1.call-start = ((), (), s32[]{:S(2)}) async-start(), calls=%async_computation.23 | async-start | bytes 1843200 | tf_op jit(solution)/shard_map/reduce_scatter | solution.py:277
  628.3 261.9 %reduce-scatter.27.cloned.1.call-start = ((), (), s32[]{:S(2)}) async-start(), calls=%async_computation.27 | async-start | bytes 1843200 | tf_op jit(solution)/shard_map/reduce_scatter | solution.py:277
  633.8 300.9 %reduce-scatter.57.cloned.1.call-start = ((), (), s32[]{:S(2)}) async-start(), calls=%async_computation.56 | async-start | bytes 2654208 | tf_op jit(solution)/shard_map/reduce_scatter | solution.py:333
  644.1 336.2 %reduce-scatter.59.cloned.1.call-start = ((), (), s32[]{:S(2)}) async-start(), calls=%async_computation.57 | async-start | bytes 2654208 | tf_op jit(solution)/shard_map/reduce_scatter | solution.py:334
  656.9 360.8 %all-gather.41.cloned.1.call-start = ((), (), s32[]{:S(2)}) async-start(), calls=%async_computation.42 | async-start | bytes 1843200 | tf_op jit(solution)/shard_map/all_gather | solution.py:296
  895.8 194.9 %all-gather.45.cloned.1.call-start = ((), (), s32[]{:S(2)}) async-start(), calls=%async_computation.46 | async-start | bytes 1843200 | tf_op jit(solution)/shard_map/all_gather | solution.py:296
  896.6 229.7 %all-gather.37.cloned.1.call-start = ((), (), s32[]{:S(2)}) async-start(), calls=%async_computation.38 | async-start | bytes 1843200 | tf_op jit(solution)/shard_map/all_gather | solution.py:296
  897.5 322.6 %all-gather.51.cloned.1.call-start = ((), (), s32[]{:S(2)}) async-start(), calls=%async_computation.52 | async-start | bytes 1327104 | tf_op jit(solution)/shard_map/all_gather | solution.py:348
  936.4 286.5 %all-gather.53.cloned.1.call-start = ((), (), s32[]{:S(2)}) async-start(), calls=%async_computation.53 | async-start | bytes 1327104 | tf_op jit(solution)/shard_map/all_gather | solution.py:351
  982.0 243.9 %reduce-scatter.55.cloned.1.call-start = ((), (), s32[]{:S(2)}) async-start(), calls=%async_computation.55 | async-start | bytes 663552 | tf_op jit(solution)/shard_map/reduce_scatter | solution.py:332
  1192.8 174.0 %reduce-scatter.47.cloned.1.call-start = ((), (), s32[]{:S(2)}) async-start(), calls=%async_computation.47 | async-start | bytes 1843200 | tf_op jit(solution)/shard_map/reduce_scatter | solution.py:299
  1196.6 205.8 %reduce-scatter.39.cloned.1.call-start = ((), (), s32[]{:S(2)}) async-start(), calls=%async_computation.39 | async-start | bytes 1843200 | tf_op jit(solution)/shard_map/reduce_scatter | solution.py:299
  (209 other events, 7195.7 us)
Sparse Core Ops, SparseCore 0:
  28.8 38.0 all-gather.18
  69.1 34.3 all-gather.22
  105.6 34.2 all-gather.26
  141.3 34.2 all-gather.30
  178.4 32.8 reduce-scatter.20
  322.8 34.0 all-gather.32
  358.4 34.2 all-gather.46
  394.9 34.2 all-gather.28
  430.6 34.2 all-gather.42
  466.5 34.2 all-gather.24
  502.2 34.2 all-gather.38
  538.5 34.2 all-gather.20
  574.3 34.2 all-gather.34
  610.8 32.8 reduce-scatter.48
  893.6 41.1 reduce-scatter.56
  937.9 42.3 reduce-scatter.58
  982.3 35.3 all-gather.40
  1019.8 34.2 all-gather.48
  1056.3 34.2 all-gather.44
  1092.0 34.2 all-gather.36
  1180.5 34.3 reduce-scatter.54
  1218.3 42.3 reduce-scatter.52
  1263.0 33.9 reduce-scatter.50
  1299.1 32.6 reduce-scatter.42
  (14 shorter events, 438.2 us)
where the time goes:
time: 1460 us
  waiting for transfers between devices  952 us (65%)
  matrix products  246 us (17%)
  other arithmetic  98.3 us (7%)
  blocking collectives  74.7 us (5%)
  local copies, waits for them, and re-layouts  56.2 us (4%)
  between operations  27.6 us (2%)
    reduce_scatter x4, waiting for transfers between devices, sum_attn(): lax.psum_scatter(term(jnp.int32(0), lax.axis_size('tensor') * rows).astyp...  127 us
    reduce_scatter x4, waiting for transfers between devices, sum_mlp(): lax.psum_scatter(term(jnp.int32(0), lax.axis_size('tensor') * rows).astyp...  125 us
    reduce_scatter x4, waiting for transfers between devices, sum_qkv(): lax.psum_scatter(term(jnp.int32(0), lax.axis_size('tensor') * rows).astyp...  125 us
    all_gather x4, waiting for transfers between devices, gather_grad(): return lax.all_gather(values, 'tensor', axis=0, tiled=True)  124 us
    all_gather x4, waiting for transfers between devices, gather_first(): return lax.all_gather(values, 'tensor', axis=0, tiled=True)  93.9 us
    reduce_scatter x4, waiting for transfers between devices, sum_upward(): lax.psum_scatter(term(jnp.int32(0), lax.axis_size('tensor') * rows).astyp...  92.7 us
    all_gather x4, waiting for transfers between devices, gather_second(): return lax.all_gather(values, 'tensor', axis=0, tiled=True)  86.3 us
    all_gather x4, waiting for transfers between devices, gather_attn(): return lax.all_gather(values, 'tensor', axis=0, tiled=True)  67.5 us
  transfers between devices with their start and end apart: 38, of which 34 were waited for; matrix products, arithmetic and copies ran while one was open for 23% of the time, Pallas kernels for 0%

commit v1 on v0

v1 whole, which is shorter than its diff:
```python
import functools
import math

import jax
import jax.numpy as jnp
from jax import lax
from jax.experimental import pallas as pl
from jax.experimental.pallas import tpu as pltpu
from jax.sharding import PartitionSpec as P

HEAD_DIM = 64
PASSES = 5
LEN = 192
EPSILON = 1e-05
MASKED = -1e30
QUERY_TILE = 256
LANES = 128
F32 = jnp.float32
BF16 = jnp.bfloat16


def tiles_of(slots):
    return [(q0, min(q0 + QUERY_TILE, slots)) for q0 in range(0, slots, QUERY_TILE)]


def dot_nt(a, b):
    return lax.dot_general(a, b, (((1,), (1,)), ((), ())), preferred_element_type=F32)


def dot_nn(a, b):
    return lax.dot_general(a, b, (((1,), (0,)), ((), ())), preferred_element_type=F32)


def dot_tn(a, b):
    return lax.dot_general(a, b, (((0,), (0,)), ((), ())), preferred_element_type=F32)


def half_lanes(values, half):
    lane = lax.broadcasted_iota(jnp.int32, (1, LANES), 1)
    return jnp.where((lane // HEAD_DIM) == half, values, jnp.zeros_like(values))


def diagonal_mask(q0, rows, live):
    key = lax.broadcasted_iota(jnp.int32, (rows, rows), 0)
    query = lax.broadcasted_iota(jnp.int32, (rows, rows), 1)
    return (key <= query) & (key + q0 < live)


def attend_kernel(live_ref, q_ref, k_ref, v_ref, o_ref, lse_ref, vt_ref):
    slots = q_ref.shape[0]
    live = live_ref[0]
    vt_ref[...] = v_ref[...].T
    for q0, q1 in tiles_of(slots):
        rows = q1 - q0

        @pl.when(q0 >= live)
        def _():
            o_ref[q0:q1, :] = jnp.zeros((rows, LANES), BF16)
            lse_ref[0, :, q0:q1] = jnp.zeros((2, rows), F32)

        @pl.when(q0 < live)
        def _():
            query = q_ref[q0:q1, :] * jnp.asarray(1.0 / math.sqrt(HEAD_DIM), BF16)
            allowed = diagonal_mask(q0, rows, live)
            outs = []
            for half in range(2):
                one = half_lanes(query, half)
                last = dot_nt(k_ref[q0:q1, :], one)
                last = jnp.where(allowed, last, MASKED)
                peak = jnp.max(last, axis=0, keepdims=True)
                if q0:
                    early = dot_nt(k_ref[0:q0, :], one)
                    peak = jnp.maximum(peak, jnp.max(early, axis=0, keepdims=True))
                last = jnp.exp(last - peak)
                total = jnp.sum(last, axis=0, keepdims=True)
                lanes = slice(half * HEAD_DIM, (half + 1) * HEAD_DIM)
                if q0:
                    early = jnp.exp(early - peak)
                    total = total + jnp.sum(early, axis=0, keepdims=True)
                inverse = 1.0 / total
                out = dot_nn(vt_ref[lanes, q0:q1], (last * inverse).astype(BF16))
                if q0:
                    out = out + dot_nn(vt_ref[lanes, 0:q0], (early * inverse).astype(BF16))
                outs.append(out)
                lse_ref[0, half : half + 1, q0:q1] = peak + jnp.log(total)
            o_ref[q0:q1, :] = jnp.concatenate(outs, axis=0).T.astype(BF16)


def attend_back_kernel(
    live_ref, q_ref, k_ref, v_ref, o_ref, g_ref, lse_ref, dq_ref, dk_ref, dv_ref, kt_ref, dk_sum, dv_sum
):
    slots = q_ref.shape[0]
    live = live_ref[0]
    kt_ref[...] = k_ref[...].T
    dk_sum[...] = jnp.zeros_like(dk_sum)
    dv_sum[...] = jnp.zeros_like(dv_sum)
    scale = 1.0 / math.sqrt(HEAD_DIM)
    for q0, q1 in tiles_of(slots):
        rows = q1 - q0

        @pl.when(q0 >= live)
        def _():
            dq_ref[q0:q1, :] = jnp.zeros((rows, LANES), BF16)

        @pl.when(q0 < live)
        def _():
            query = q_ref[q0:q1, :] * jnp.asarray(scale, BF16)
            grad = g_ref[q0:q1, :]
            allowed = diagonal_mask(q0, rows, live)
            both = (grad.astype(F32) * o_ref[q0:q1, :].astype(F32)).T
            parts = []
            for half in range(2):
                lanes = slice(half * HEAD_DIM, (half + 1) * HEAD_DIM)
                one = half_lanes(query, half)
                grad_one = half_lanes(grad, half)
                lse = lse_ref[0, half : half + 1, q0:q1]
                inner = jnp.sum(both[lanes, :], axis=0, keepdims=True)
                turned = None
                for start, stop in ([(0, q0)] if q0 else []) + [(q0, q1)]:
                    scores = dot_nt(k_ref[start:stop, :], one)
                    probs = jnp.exp(scores - lse)
                    if start == q0:
                        probs = jnp.where(allowed, probs, 0.0)
                    grad_weights = dot_nt(v_ref[start:stop, :], grad_one)
                    grad_scores = (probs * (grad_weights - inner)).astype(BF16)
                    dk_sum[start:stop, :] += dot_nn(grad_scores, one)
                    dv_sum[start:stop, :] += dot_nn(probs.astype(BF16), grad_one)
                    piece = dot_nn(kt_ref[lanes, start:stop], grad_scores)
                    turned = piece if turned is None else turned + piece
                parts.append(turned)
            dq_ref[q0:q1, :] = (jnp.concatenate(parts, axis=0).T * scale).astype(BF16)

    dk_ref[...] = dk_sum[...].astype(BF16)
    dv_ref[...] = dv_sum[...].astype(BF16)


def pair_spec(slots):
    return pl.BlockSpec((slots, LANES), lambda p, live: (0, p))


def attend(live, query, keys, values):
    slots, width = query.shape
    pairs = width // LANES
    spec = pair_spec(slots)
    lse_spec = pl.BlockSpec((1, 2, slots), lambda p, live: (p, 0, 0))
    flops = 2 * 2 * slots * slots * width
    return pl.pallas_call(
        attend_kernel,
        out_shape=(
            jax.ShapeDtypeStruct((slots, width), BF16),
            jax.ShapeDtypeStruct((pairs, 2, slots), F32),
        ),
        grid_spec=pltpu.PrefetchScalarGridSpec(
            num_scalar_prefetch=1,
            grid=(pairs,),
            in_specs=[spec, spec, spec],
            out_specs=(spec, lse_spec),
            scratch_shapes=[pltpu.VMEM((LANES, slots), BF16)],
        ),
        cost_estimate=pl.CostEstimate(
            flops=flops, transcendentals=slots * slots * width // HEAD_DIM, bytes_accessed=8 * slots * width
        ),
        name="attend",
    )(live, query, keys, values)


def attend_back(live, query, keys, values, mixed, grad_mixed, lse):
    slots, width = query.shape
    pairs = width // LANES
    spec = pair_spec(slots)
    lse_spec = pl.BlockSpec((1, 2, slots), lambda p, live: (p, 0, 0))
    flops = 5 * 2 * slots * slots * width
    shape = jax.ShapeDtypeStruct((slots, width), BF16)
    return pl.pallas_call(
        attend_back_kernel,
        out_shape=(shape, shape, shape),
        grid_spec=pltpu.PrefetchScalarGridSpec(
            num_scalar_prefetch=1,
            grid=(pairs,),
            in_specs=[spec, spec, spec, spec, spec, lse_spec],
            out_specs=(spec, spec, spec),
            scratch_shapes=[
                pltpu.VMEM((LANES, slots), BF16),
                pltpu.VMEM((slots, LANES), F32),
                pltpu.VMEM((slots, LANES), F32),
            ],
        ),
        cost_estimate=pl.CostEstimate(
            flops=flops, transcendentals=slots * slots * width // HEAD_DIM, bytes_accessed=16 * slots * width
        ),
        name="attend_back",
    )(live, query, keys, values, mixed, grad_mixed, lse)


def ring_pairs(size, shift):
    return [(source, (source + shift) % size) for source in range(size)]


def to_sequence(block):
    size = lax.axis_size("tensor")
    me = lax.axis_index("tensor")
    rows, seqs, width = block.shape
    block = block.transpose(1, 0, 2)
    out = jnp.zeros((size * rows, width), block.dtype)
    for shift in range(size):
        piece = lax.dynamic_index_in_dim(block, (me + shift) % size, 0, keepdims=False)
        if shift:
            piece = lax.ppermute(piece, "tensor", ring_pairs(size, shift))
        out = lax.dynamic_update_slice(out, piece, (((me - shift) % size) * rows, 0))
    return out


def to_slots(values):
    size = lax.axis_size("tensor")
    me = lax.axis_index("tensor")
    slots, width = values.shape
    rows = slots // size
    out = jnp.zeros((size, rows, width), values.dtype)
    for shift in range(size):
        piece = lax.dynamic_slice(values, (((me + shift) % size) * rows, 0), (rows, width))
        if shift:
            piece = lax.ppermute(piece, "tensor", ring_pairs(size, shift))
        out = lax.dynamic_update_slice(out, piece[None], ((me - shift) % size, 0, 0))
    return out.transpose(1, 0, 2)


def share(rows):
    size = lax.axis_size("batch")
    each = rows.shape[0] // size
    return lax.dynamic_slice(rows, (lax.axis_index("batch") * each, 0), (each, rows.shape[1]))


def norm_parts(values):
    mean = jnp.mean(values, axis=-1, keepdims=True)
    center = values - mean
    spread = jnp.mean(center * center, axis=-1, keepdims=True)
    inverse = lax.rsqrt(spread + EPSILON)
    return center * inverse, inverse


def norm_back(grad, xhat, inverse, gain):
    scaled = grad * gain
    first = jnp.mean(scaled, axis=-1, keepdims=True)
    second = jnp.mean(scaled * xhat, axis=-1, keepdims=True)
    return inverse * (scaled - first - xhat * second)


def gelu_parts(values):
    outer = math.sqrt(2.0 / math.pi)
    inside = jnp.tanh(outer * (values + 0.044715 * values * values * values))
    act = 0.5 * values * (1.0 + inside)
    slope = 0.5 * (1.0 + inside) + 0.5 * values * (1.0 - inside * inside) * outer * (
        1.0 + 3.0 * 0.044715 * values * values
    )
    return act, slope


def per_device(
    slot_states,
    pass_counts,
    w_qkv,
    q_bias,
    v_bias,
    w_out,
    out_bias,
    w_up,
    up_bias,
    w_down,
    down_bias,
    ln1_gain,
    ln1_bias,
    ln2_gain,
    ln2_bias,
    pass_table,
    cotangent,
):
    groups = lax.axis_size("tensor")
    spread = lax.axis_size("batch")
    me = lax.axis_index("tensor")
    rows, seqs, width = slot_states.shape
    slots = rows * groups
    hidden_here = w_up.shape[1]
    hidden_units = hidden_here * groups
    assert seqs == groups

    gain_one, shift_one = ln1_gain.astype(F32), ln1_bias.astype(F32)
    gain_two, shift_two = ln2_gain.astype(F32), ln2_bias.astype(F32)
    table = pass_table.astype(F32)

    qkv_rows = w_qkv.transpose(1, 2, 0)
    every = ("tensor", "batch")
    gathered_qkv = lax.all_gather(
        jnp.concatenate([share(qkv_rows[part]) for part in range(3)], axis=0)[None], every, axis=0, tiled=True
    )
    each = width // (groups * spread)
    gathered_qkv = gathered_qkv.reshape(groups * spread, 3, each, width)
    matrix_q, matrix_k, matrix_v = (gathered_qkv[:, part].reshape(width, width) for part in range(3))
    matrix_out = lax.all_gather(share(w_out), every, axis=0, tiled=True)
    mixed_order = ("batch", "tensor")
    matrix_up = lax.all_gather(share(w_up.T), mixed_order, axis=0, tiled=True)
    matrix_down = lax.all_gather(share(w_down), mixed_order, axis=0, tiled=True)
    bias_row = jnp.concatenate([q_bias, v_bias, up_bias]).astype(BF16)
    bias_rows = lax.all_gather(bias_row, "tensor", axis=0)
    here = q_bias.shape[0]
    bias_query = bias_rows[:, :here].reshape(1, width).astype(F32)
    bias_value = bias_rows[:, here : 2 * here].reshape(1, width).astype(F32)
    bias_up = bias_rows[:, 2 * here :].reshape(groups, spread, hidden_here // spread)
    bias_up = bias_up.transpose(1, 0, 2).reshape(1, hidden_units).astype(F32)

    states = to_sequence(slot_states).astype(F32)
    cot = to_sequence(cotangent)
    count = lax.dynamic_index_in_dim(pass_counts, me, 0, keepdims=False)
    index = jnp.arange(slots, dtype=jnp.int32)
    passes = (index % count)[:, None]
    live_count = count * LEN
    live = (index < live_count)[:, None]
    live_arg = live_count.reshape(1).astype(jnp.int32)
    added = jnp.zeros((slots, width), F32)
    for number in range(PASSES):
        added = jnp.where(passes == number, table[number][None, :], added)
    hidden = states + added

    xhat_one, inverse_one = norm_parts(hidden)
    n1 = (xhat_one * gain_one + shift_one).astype(BF16)
    query = (dot_nt(n1, matrix_q) + bias_query).astype(BF16)
    keys = dot_nt(n1, matrix_k).astype(BF16)
    values = (dot_nt(n1, matrix_v) + bias_value).astype(BF16)
    mixed, lse = attend(live_arg, query, keys, values)
    after = hidden + dot_nn(mixed, matrix_out) + out_bias.astype(F32)
    xhat_two, inverse_two = norm_parts(after)
    n2 = (xhat_two * gain_two + shift_two).astype(BF16)
    pre_act = dot_nt(n2, matrix_up) + bias_up
    act, slope = gelu_parts(pre_act)
    act = act.astype(BF16)
    result = after + dot_nn(act, matrix_down) + down_bias.astype(F32)
    layer_out = jnp.where(live, result, 0.0).astype(BF16)
    layer_part = to_slots(layer_out)

    grad_m = jnp.where(live, cot, jnp.zeros_like(cot))
    grad_y = grad_m.astype(F32)
    grad_down = dot_tn(act, grad_m).astype(BF16)
    grad_act = dot_nt(grad_m, matrix_down)
    grad_u = (grad_act * slope).astype(BF16)
    grad_up = dot_tn(grad_u, n2).astype(BF16)
    grad_n2 = dot_nn(grad_u, matrix_up)
    grad_a = grad_y + norm_back(grad_n2, xhat_two, inverse_two, gain_two)
    grad_att = grad_a.astype(BF16)
    grad_out = dot_tn(mixed, grad_att).astype(BF16)
    grad_mixed = dot_nt(grad_att, matrix_out).astype(BF16)
    grad_q, grad_k, grad_v = attend_back(live_arg, query, keys, values, mixed, grad_mixed, lse)
    grad_wq = dot_tn(grad_q, n1).astype(BF16)
    grad_wk = dot_tn(grad_k, n1).astype(BF16)
    grad_wv = dot_tn(grad_v, n1).astype(BF16)
    grad_n1 = dot_nn(grad_q, matrix_q) + dot_nn(grad_k, matrix_k) + dot_nn(grad_v, matrix_v)
    grad_h = grad_a + norm_back(grad_n1, xhat_one, inverse_one, gain_one)
    grad_part = to_slots(grad_h.astype(BF16))

    def reduce_mixed(value):
        value = lax.psum_scatter(value, "batch", scatter_dimension=0, tiled=True)
        value = lax.psum_scatter(value, "tensor", scatter_dimension=0, tiled=True)
        return lax.all_gather(value, "batch", axis=0, tiled=True).astype(F32)

    def reduce_plain(value):
        value = value.reshape(groups, -1, width)
        value = lax.psum_scatter(value, "batch", scatter_dimension=1, tiled=True)
        value = lax.psum_scatter(value, "tensor", scatter_dimension=0, tiled=True)
        return lax.all_gather(value[0], "batch", axis=0, tiled=True).astype(F32)

    out_down = reduce_mixed(grad_down)
    out_up = reduce_mixed(grad_up).T
    out_out = reduce_plain(grad_out)
    out_qkv = jnp.stack([reduce_plain(value) for value in (grad_wq, grad_wk, grad_wv)], axis=0).transpose(2, 0, 1)

    def total(value):
        return jnp.sum(value.astype(F32), axis=0, keepdims=True)

    grad_pass = jnp.concatenate(
        [total(jnp.where(passes == number, grad_h, 0.0)) for number in range(PASSES)], axis=0
    )
    grad_bias_up = total(grad_u).reshape(spread, groups, hidden_here // spread)
    grad_bias_up = grad_bias_up.transpose(1, 0, 2).reshape(groups, width)
    small = jnp.concatenate(
        [
            total(grad_n1 * xhat_one),
            total(grad_n1),
            total(grad_n2 * xhat_two),
            total(grad_n2),
            total(grad_a),
            total(grad_y),
            grad_pass,
            total(grad_q),
            total(grad_v),
            grad_bias_up,
        ],
        axis=0,
    )
    small = lax.psum(small, ("batch", "tensor"))
    lead = 6 + PASSES
    mine = lax.dynamic_slice_in_dim(small[lead : lead + 2], me * here, here, axis=1)
    return (
        layer_part,
        grad_part,
        out_qkv,
        mine[0],
        mine[1],
        out_out,
        small[4],
        out_up,
        lax.dynamic_index_in_dim(small[lead + 2 :], me, 0, keepdims=False),
        out_down,
        small[5],
        small[0],
        small[1],
        small[2],
        small[3],
        small[6:lead],
    )


def solution(mesh):
    in_specs = (
        P("tensor", "batch", None),
        P("batch"),
        P(None, None, "tensor"),
        P("tensor"),
        P("tensor"),
        P("tensor", None),
        P(),
        P(None, "tensor"),
        P("tensor"),
        P("tensor", None),
        P(),
        P(),
        P(),
        P(),
        P(),
        P(),
        P("tensor", "batch", None),
    )
    out_specs = (
        P("tensor", "batch", None),
        P("tensor", "batch", None),
        P(None, None, "tensor"),
        P("tensor"),
        P("tensor"),
        P("tensor", None),
        P(),
        P(None, "tensor"),
        P("tensor"),
        P("tensor", None),
        P(),
        P(),
        P(),
        P(),
        P(),
        P(),
    )
    return jax.shard_map(
        per_device, mesh=mesh, in_specs=in_specs, out_specs=out_specs, check_vma=False
    )
```

time: 1460 us -> 904 us (0.62)
  waiting for transfers between devices: 952 us -> 330 us
  matrix products: 246 us -> 105 us
  local copies, waits for them, and re-layouts: 56.2 us -> 176 us
  blocking collectives: 74.7 us -> 163 us
  other arithmetic: 98.3 us -> 27.7 us
  Pallas kernels: 0 us -> 45.3 us
  starting transfers between devices: 4.3 us -> 26.7 us
    reduce_scatter x20 -> x8, waiting for transfers between devices: 575 us -> 62.5 us  [the longest x2 33.8 us: reduce_mixed(): value = lax.psum_scatter(value, 'batch', scatter_dimension=0, tiled=True)]
    all_gather x18 -> x6, waiting for transfers between devices: 372 us -> 108 us  [the longest x1 56 us: per_device(): matrix_up = lax.all_gather(share(w_up.T), mixed_order, axis=0, tiled=True)]
    unnamed x38 -> x22, waiting for transfers between devices: 4.33 us -> 157 us
    dot_general x80 -> x18, matrix products: 246 us -> 105 us  [the longest x6 36.4 us: dot_nt(): lax.dot_general(a, b, (((1,), (1,)), ((), ())), preferred_element_type=F32)]
    dynamic_update_slice x0 -> x16, local copies, waits for them, and re-layouts: none -> 112 us  [the longest x8 105 us: to_slots(): lax.dynamic_update_slice(out, piece[None], ((me - shift) % size, 0, 0))]
    all_gather x2 -> x5, blocking collectives: 20.6 us -> 106 us  [the longest x1 69.1 us: per_device(): bias_rows = lax.all_gather(bias_row, 'tensor', axis=0)]
    pallas_call x0 -> x2, Pallas kernels: none -> 45.3 us  [the longest x1 23.4 us: attend_back(): pl.pallas_call(attend_back_kernel, out_shape=(shape, shape, shape), grid_...]
    convert_element_type x32 -> x12, other arithmetic: 47.3 us -> 7.7 us  [the longest x1 3.9 us: per_device(): n1 = (xhat_one * gain_one + shift_one).astype(BF16)]
  transfers between devices with their start and end apart: 38 -> 30, of which waited for: 34 -> 10; matrix products, arithmetic and copies ran while one was open for 23% -> 31% of each run, Pallas kernels for 0% -> 5%
where the time goes in v1:
time: 904 us; the launch traced here: 891 us
  waiting for transfers between devices  330 us (37%)
  local copies, waits for them, and re-layouts  176 us (19%)
  blocking collectives  163 us (18%)
  matrix products  105 us (12%)
  Pallas kernels  45.3 us (5%)
  other arithmetic  27.7 us (3%)
  starting transfers between devices  26.7 us (3%)
  between operations  17.6 us (2%)
    unnamed x22, waiting for transfers between devices  157 us
    dynamic_update_slice x8, local copies, waits for them, and re-layouts, to_slots(): lax.dynamic_update_slice(out, piece[None], ((me - shift) % size, 0, 0))  105 us
    all_gather x1, blocking collectives, per_device(): bias_rows = lax.all_gather(bias_row, 'tensor', axis=0)  69.1 us
    psum x1, blocking collectives, per_device(): small = lax.psum(small, ('batch', 'tensor'))  57.7 us
    all_gather x1, waiting for transfers between devices, per_device(): matrix_up = lax.all_gather(share(w_up.T), mixed_order, axis=0, tiled=True)  56 us
    all_gather x1, waiting for transfers between devices, per_device(): matrix_down = lax.all_gather(share(w_down), mixed_order, axis=0, tiled=True)  52.1 us
    all_gather x4, blocking collectives, reduce_plain(): return lax.all_gather(value[0], 'batch', axis=0, tiled=True).astype(F32)  36.7 us
    dot_general x6, matrix products, dot_nt(): lax.dot_general(a, b, (((1,), (1,)), ((), ())), preferred_element_type=F32)  36.4 us
  transfers between devices with their start and end apart: 30, of which 10 were waited for; matrix products, arithmetic and copies ran while one was open for 31% of the time, Pallas kernels for 5%

profile of v1, /device:TPU:0, one launch (start us, length us, event | category | flops | bytes accessed | tf_op | source)
XLA Modules:
  0.0 891.5 jit_solution(13706383833602635090)
XLA Ops:
  37.7 69.1 %all-gather.6 = bf16[4,1,1152]{2,1,0:T(2,128)(2,1)S(1)} all-gather(bf16[1,1,1152]{2,1,0:T(2,128)(2,1)S(1)} %reshape.205), channel_id=3, replica_groups=mesh['batch'=8,'tensor'=4] {'tensor'}, dimensions={0}, use_global_device_ids=true | all-gather | bytes 11520 | tf_op jit(solution)/shard_map/all_gather | solution.py:303
  138.2 21.9 %attend.1 = (bf16[960,768]{1,0:T(8,128)(2,1)}, f32[6,2,960]{2,1,0:T(2,128)}) custom-call(s32[1]{0:T(128)} %bitcast.5.live_ref, bf16[960,768]{1,0:T(8,128)(2,1)} %add_convert_fusion.2.q_ref, bf16[960,768]{1,0:T(8,128)(2,1)} %convolution_convert_fusion.3.k_ref, bf16[960,768]{1,0:T(8,128)(2,1)} %add_convert_fusion.1.v_ref), custom_call_target="tpu_custom_call" | custom-call | flops 2831155200 | bytes 5898240 | tf_op jit(solution)/shard_map/attend/pallas_call | solution.py:147
  168.0 56.0 %all-gather.16.cloned.1.call-done = bf16[3072,768]{1,0:T(8,128)(2,1)} async-done(((bf16[96,768]{1,0:T(8,128)(2,1)}), bf16[3072,768]{1,0:T(8,128)(2,1)}) %all-gather.16.cloned.1.call-update) | async-done | bytes 4718608 | tf_op jit(solution)/shard_map/all_gather | solution.py:300
  224.0 12.5 %fusion.22 = f32[960,3072]{1,0:T(8,128)} fusion(bf16[3072,768]{1,0:T(8,128)(2,1)} %all-gather.16.cloned.1.call-done, f32[960,768]{1,0:T(8,128)} %get-tuple-element.147, f32[768]{0:T(1024)S(1)} %convert_element_type.150, f32[768]{0:T(1024)S(1)} %convert_element_type.149, f32[960]{0:T(1024)S(1)} %add_rsqrt_fusion, f32[960]{0:T(1024)S(1)} %broadcast_multiply_fusion.4), kind=kOutput, calls=%fused_computation.132 | convolution fusion | flops 4533534720 | bytes 19478016 | tf_op jit(solution)/shard_map/dot_general | solution.py:27
  236.6 52.1 %all-gather.18.cloned.1.call-done = bf16[3072,768]{1,0:T(8,128)(2,1)} async-done(((bf16[96,768]{1,0:T(8,128)(2,1)}), bf16[3072,768]{1,0:T(8,128)(2,1)}) %all-gather.18.cloned.1.call-update) | async-done | bytes 4718608 | tf_op jit(solution)/shard_map/all_gather | solution.py:301
  288.6 14.0 %convert_reduce_fusion = (f32[3072]{0:T(1024)S(1)}, bf16[960,3072]{1,0:T(8,128)(2,1)S(1)}) fusion(f32[960,3072]{1,0:T(8,128)} %fusion.22, f32[3072]{0:T(1024)S(1)} %reshape.192, bf16[3072,768]{1,0:T(8,128)(2,1)} %all-gather.18.cloned.1.call-done, bf16[960,768]{1,0:T(8,128)(2,1)S(1)} %constant_dynamic-update-slice_fusion, pred[960]{0:T(1024)(128)(4,1)S(1)} %iota_compare_fusion), kind=kOutput, calls=%fused_computation.9 | convolution fusion | flops 4595463168 | bytes 23913408 | tf_op jit(solution)/shard_map/dot_general | solution.py:27
  314.8 12.3 %convolution_convert_fusion = bf16[3072,768]{1,0:T(8,128)(2,1)} fusion(bf16[960,768]{1,0:T(8,128)(2,1)S(1)} %constant_dynamic-update-slice_fusion, pred[960]{0:T(1024)(128)(4,1)S(1)} %iota_compare_fusion, f32[960,3072]{1,0:T(8,128)} %fusion.22, f32[3072]{0:T(1024)S(1)} %reshape.192), kind=kOutput, calls=%fused_computation.11 | convolution fusion | flops 4562436096 | bytes 18002880 | tf_op jit(solution)/shard_map/dot_general | solution.py:35
  327.2 10.5 %multiply_reduce_fusion = (f32[768]{0:T(1024)S(1)}, f32[960]{0:T(1024)S(1)}, f32[960]{0:T(1024)S(1)}, f32[768]{0:T(1024)S(1)}, f32[960,768]{1,0:T(8,128)S(1)}) fusion(f32[960,768]{1,0:T(8,128)} %get-tuple-element.147, f32[960]{0:T(1024)S(1)} %add_rsqrt_fusion, f32[960]{0:T(1024)S(1)} %broadcast_multiply_fusion.4, f32[768]{0:T(1024)S(1)} %convert_element_type.149, ...), kind=kOutput, calls=%fused_computation.22 | convolution fusion | flops 4536479744 | bytes 16539648 | tf_op jit(solution)/shard_map/dot_general | solution.py:31
  344.0 23.4 %attend_back.1 = (bf16[960,768]{1,0:T(8,128)(2,1)}, bf16[960,768]{1,0:T(8,128)(2,1)}, bf16[960,768]{1,0:T(8,128)(2,1)}) custom-call(s32[1]{0:T(128)} %bitcast.5.live_ref, bf16[960,768]{1,0:T(8,128)(2,1)} %add_convert_fusion.2.q_ref, bf16[960,768]{1,0:T(8,128)(2,1)} %convolution_convert_fusion.3.k_ref, bf16[960,768]{1,0:T(8,128)(2,1)} %add_convert_fusion.1.v_ref, ...), custom_call_target="tpu_custom_call" | custom-call | flops 7077888000 | bytes 11796480 | tf_op jit(solution)/shard_map/attend_back/pallas_call | solution.py:174
  390.3 33.8 %reduce-scatter.33.cloned.1.call-done = bf16[384,768]{1,0:T(8,128)(2,1)} async-done(((bf16[3072,768]{1,0:T(8,128)(2,1)}), bf16[384,768]{1,0:T(8,128)(2,1)}) %reduce-scatter.33.cloned.1.call-update) | async-done | bytes 589840 | tf_op jit(solution)/shard_map/reduce_scatter | solution.py:359
  424.2 40.4 %reduce-scatter.41.cloned.1.call-done = bf16[24,3072]{1,0:T(8,128)(2,1)} async-done(((bf16[192,3072]{1,0:T(8,128)(2,1)}), bf16[24,3072]{1,0:T(8,128)(2,1)}) %reduce-scatter.41.cloned.1.call-update) | async-done | bytes 147472
  466.4 38.8 %reduce-scatter.39.cloned.1.call-done = bf16[24,3072]{1,0:T(8,128)(2,1)} async-done(((bf16[192,3072]{1,0:T(8,128)(2,1)}), bf16[24,3072]{1,0:T(8,128)(2,1)}) %reduce-scatter.39.cloned.1.call-update) | async-done | bytes 147472
  506.9 38.8 %reduce-scatter.37.cloned.1.call-done = bf16[24,3072]{1,0:T(8,128)(2,1)} async-done(((bf16[192,3072]{1,0:T(8,128)(2,1)}), bf16[24,3072]{1,0:T(8,128)(2,1)}) %reduce-scatter.37.cloned.1.call-update) | async-done | bytes 147472
  547.4 38.6 %reduce-scatter.43.cloned.1.call-done = bf16[24,3072]{1,0:T(8,128)(2,1)} async-done(((bf16[192,3072]{1,0:T(8,128)(2,1)}), bf16[24,3072]{1,0:T(8,128)(2,1)}) %reduce-scatter.43.cloned.1.call-update) | async-done | bytes 147472
  587.9 22.6 %reduce-scatter.31.cloned.1.call-done = bf16[96,768]{1,0:T(8,128)(2,1)} async-done(((bf16[384,768]{1,0:T(8,128)(2,1)}), bf16[96,768]{1,0:T(8,128)(2,1)}) %reduce-scatter.31.cloned.1.call-update) | async-done | bytes 147472 | tf_op jit(solution)/shard_map/reduce_scatter | solution.py:360
  610.6 12.1 %select_convert_fusion = bf16[960,768]{1,0:T(8,128)(2,1)S(1)} fusion(f32[960,768]{1,0:T(8,128)} %get-tuple-element.147, bf16[3072,768]{1,0:T(8,128)(2,1)} %all-gather.18.cloned.1.call-done, f32[768]{0:T(1024)S(1)} %convert_element_type.157, pred[960]{0:T(1024)(128)(4,1)S(1)} %iota_compare_fusion, f32[960,3072]{1,0:T(8,128)} %fusion.22, f32[3072]{0:T(1024)S(1)} %reshape.192), kind=kOutput, calls=%fused_computation.28 | convolution fusion | flops 4562288640 | bytes 20955072 | tf_op jit(solution)/shard_map/dot_general | solution.py:31
  659.4 57.7 %psum.7 = f32[17,768]{1,0:T(8,128)S(1)} all-reduce(f32[17,768]{1,0:T(8,128)S(1)} %concatenate.11), channel_id=1, replica_groups=mesh['batch'=8,'tensor'=4] {'batch','tensor'}, use_global_device_ids=true, to_apply=%region_28.29 | all-reduce | flops 13056 | bytes 104448 | tf_op jit(solution)/shard_map/psum | solution.py:397
  720.3 13.6 %dynamic_update_slice.52 = bf16[4,240,768]{2,0,1:T(4,128)(2,1)} dynamic-update-slice(bf16[4,240,768]{2,0,1:T(4,128)(2,1)} %broadcast.216.clone, bf16[1,240,768]{2,0,1:T(2,128)(2,1)S(1)} %copy.83, s32[]{:T(128)S(6)} %select_n.226, s32[]{:T(128)} %constant.164.clone.1, s32[]{:T(128)} %constant.164.clone.1) | dynamic-update-slice | bytes 737284 | tf_op jit(solution)/shard_map/dynamic_update_slice | solution.py:223
  757.3 13.7 %dynamic_update_slice.53 = bf16[4,240,768]{2,0,1:T(4,128)(2,1)} dynamic-update-slice(bf16[4,240,768]{2,0,1:T(4,128)(2,1)} %dynamic_update_slice.52, bf16[1,240,768]{2,0,1:T(2,128)(2,1)S(1)} %copy.84, s32[]{:T(128)S(6)} %select_n.251, s32[]{:T(128)} %constant.164.clone.1, s32[]{:T(128)} %constant.164.clone.1) | dynamic-update-slice | bytes 737284 | tf_op jit(solution)/shard_map/dynamic_update_slice | solution.py:223
  771.0 13.8 %dynamic_update_slice.61 = bf16[4,240,768]{2,0,1:T(4,128)(2,1)} dynamic-update-slice(bf16[4,240,768]{2,0,1:T(4,128)(2,1)} %copy-done.15, bf16[1,240,768]{2,0,1:T(2,128)(2,1)} %copy.92, s32[]{:T(128)S(6)} %select_n.251, s32[]{:T(128)} %constant.164.clone.1, s32[]{:T(128)} %constant.164.clone.1) | dynamic-update-slice | bytes 737284 | tf_op jit(solution)/shard_map/dynamic_update_slice | solution.py:223
  784.7 13.6 %dynamic_update_slice.54 = bf16[4,240,768]{2,0,1:T(4,128)(2,1)} dynamic-update-slice(bf16[4,240,768]{2,0,1:T(4,128)(2,1)} %dynamic_update_slice.53, bf16[1,240,768]{2,0,1:T(2,128)(2,1)S(1)} %copy.85, s32[]{:T(128)S(6)} %select_n.253, s32[]{:T(128)} %constant.164.clone.1, s32[]{:T(128)} %constant.164.clone.1) | dynamic-update-slice | bytes 737284 | tf_op jit(solution)/shard_map/dynamic_update_slice | solution.py:223
  798.4 13.6 %dynamic_update_slice.62 = bf16[4,240,768]{2,0,1:T(4,128)(2,1)} dynamic-update-slice(bf16[4,240,768]{2,0,1:T(4,128)(2,1)} %dynamic_update_slice.61, bf16[1,240,768]{2,0,1:T(2,128)(2,1)S(1)} %copy-done.11, s32[]{:T(128)S(6)} %select_n.253, s32[]{:T(128)} %constant.164.clone.1, s32[]{:T(128)} %constant.164.clone.1) | dynamic-update-slice | bytes 737284 | tf_op jit(solution)/shard_map/dynamic_update_slice | solution.py:223
  812.0 13.6 %dynamic_update_slice.55 = bf16[4,240,768]{2,0,1:T(4,128)(2,1)} dynamic-update-slice(bf16[4,240,768]{2,0,1:T(4,128)(2,1)} %dynamic_update_slice.54, bf16[1,240,768]{2,0,1:T(2,128)(2,1)S(1)} %copy.86, s32[]{:T(128)S(6)} %select_n.255, s32[]{:T(128)} %constant.164.clone.1, s32[]{:T(128)} %constant.164.clone.1) | dynamic-update-slice | bytes 737284 | tf_op jit(solution)/shard_map/dynamic_update_slice | solution.py:223
  825.7 13.6 %dynamic_update_slice.63 = bf16[4,240,768]{2,0,1:T(4,128)(2,1)} dynamic-update-slice(bf16[4,240,768]{2,0,1:T(4,128)(2,1)} %dynamic_update_slice.62, bf16[1,240,768]{2,0,1:T(2,128)(2,1)S(1)} %copy.94, s32[]{:T(128)S(6)} %select_n.255, s32[]{:T(128)} %constant.164.clone.1, s32[]{:T(128)} %constant.164.clone.1) | dynamic-update-slice | bytes 737284 | tf_op jit(solution)/shard_map/dynamic_update_slice | solution.py:223
  (285 shorter events, 223.6 us)
Async XLA Ops:
  7.2 121.2 %all-gather.24.cloned.1.call-start = ((), (), s32[]{:S(2)}) async-start(), calls=%async_computation.25 | async-start | bytes 3649536 | tf_op jit(solution)/shard_map/all_gather | solution.py:292
  9.3 150.9 %all-gather.14.cloned.1.call-start = ((), (), s32[]{:S(2)}) async-start(), calls=%async_computation.12 | async-start | bytes 1216512 | tf_op jit(solution)/shard_map/all_gather | solution.py:298
  10.8 213.2 %all-gather.16.cloned.1.call-start = ((), (), s32[]{:S(2)}) async-start(), calls=%async_computation.13 | async-start | bytes 4866048 | tf_op jit(solution)/shard_map/all_gather | solution.py:300
  11.8 276.8 %all-gather.18.cloned.1.call-start = ((), (), s32[]{:S(2)}) async-start(), calls=%async_computation.14 | async-start | bytes 4866048 | tf_op jit(solution)/shard_map/all_gather | solution.py:301
  13.5 376.1 %reduce-scatter.29.cloned.1.call-start = ((), (), s32[]{:S(2)}) async-start(), calls=%async_computation.19 | async-start | bytes 5308416 | tf_op jit(solution)/shard_map/reduce_scatter | solution.py:359
  28.3 87.3 %collective-permute-start.1 = (bf16[240,768]{1,0:T(8,128)(2,1)}, bf16[240,768]{1,0:T(8,128)(2,1)}, u32[]{:S(2)}, u32[]{:S(2)}) collective-permute-start(bf16[240,768]{1,0:T(8,128)(2,1)} %bitcast.112), channel_id=1, source_target_pairs={{0,2},{1,3},{2,0},{3,1},{4,6},{5,7},{6,4},{7,5},{8,10},{9,11},{10,... | collective-permute-start | bytes 1105928 | tf_op jit(solution)/shard_map/ppermute | solution.py:208
  314.7 109.4 %reduce-scatter.33.cloned.1.call-start = ((), (), s32[]{:S(2)}) async-start(), calls=%async_computation.22 | async-start | bytes 5308416 | tf_op jit(solution)/shard_map/reduce_scatter | solution.py:359
  327.1 137.5 %reduce-scatter.41.cloned.1.call-start = ((), (), s32[]{:S(2)}) async-start(), calls=%async_computation.28 | async-start | bytes 1327104
  372.8 132.3 %reduce-scatter.39.cloned.1.call-start = ((), (), s32[]{:S(2)}) async-start(), calls=%async_computation.27 | async-start | bytes 1327104
  378.2 167.4 %reduce-scatter.37.cloned.1.call-start = ((), (), s32[]{:S(2)}) async-start(), calls=%async_computation.26 | async-start | bytes 1327104
  384.5 201.6 %reduce-scatter.43.cloned.1.call-start = ((), (), s32[]{:S(2)}) async-start(), calls=%async_computation.29 | async-start | bytes 1327104
  389.5 221.0 %reduce-scatter.31.cloned.1.call-start = ((), (), s32[]{:S(2)}) async-start(), calls=%async_computation.20 | async-start | bytes 737280 | tf_op jit(solution)/shard_map/reduce_scatter | solution.py:360
  390.3 250.7 %reduce-scatter.35.cloned.1.call-start = ((), (), s32[]{:S(2)}) async-start(), calls=%async_computation.23 | async-start | bytes 737280 | tf_op jit(solution)/shard_map/reduce_scatter | solution.py:360
  424.1 415.2 %reduce-scatter.25.cloned.1.call-start = ((), (), s32[]{:S(2)}) async-start(), calls=%async_computation.17 | async-start | bytes 184320 | tf_op jit(solution)/shard_map/reduce_scatter | solution.py:366
  466.3 383.2 %reduce-scatter.23.cloned.1.call-start = ((), (), s32[]{:S(2)}) async-start(), calls=%async_computation.16 | async-start | bytes 184320 | tf_op jit(solution)/shard_map/reduce_scatter | solution.py:366
  506.8 351.3 %reduce-scatter.21.cloned.1.call-start = ((), (), s32[]{:S(2)}) async-start(), calls=%async_computation.15 | async-start | bytes 184320 | tf_op jit(solution)/shard_map/reduce_scatter | solution.py:366
  547.4 320.0 %reduce-scatter.27.cloned.1.call-start = ((), (), s32[]{:S(2)}) async-start(), calls=%async_computation.18 | async-start | bytes 184320 | tf_op jit(solution)/shard_map/reduce_scatter | solution.py:366
  587.7 290.5 %all-gather.20.cloned.1.call-start = ((), (), s32[]{:S(2)}) async-start(), calls=%async_computation.21 | async-start | bytes 1327104 | tf_op jit(solution)/shard_map/all_gather | solution.py:361
  610.5 271.1 %all-gather.22.cloned.1.call-start = ((), (), s32[]{:S(2)}) async-start(), calls=%async_computation.24 | async-start | bytes 1327104 | tf_op jit(solution)/shard_map/all_gather | solution.py:361
  623.7 124.0 %collective-permute-start.4 = (bf16[240,768]{1,0:T(8,128)(2,1)}, bf16[240,768]{1,0:T(8,128)(2,1)}, u32[]{:S(2)}, u32[]{:S(2)}) collective-permute-start(bf16[240,768]{1,0:T(8,128)(2,1)} %get-tuple-element.132), channel_id=1, source_target_pairs={{0,2},{1,3},{2,0},{3,1},{4,6},{5,7},{6,4},{7,5},{8,10},{9,11},{10,... | collective-permute-start | bytes 1105928 | tf_op jit(solution)/shard_map/ppermute | solution.py:222
  624.9 124.4 %collective-permute-start.5 = (bf16[240,768]{1,0:T(8,128)(2,1)}, bf16[240,768]{1,0:T(8,128)(2,1)}, u32[]{:S(2)}, u32[]{:S(2)}) collective-permute-start(bf16[240,768]{1,0:T(8,128)(2,1)} %get-tuple-element.131), channel_id=1, source_target_pairs={{0,3},{1,0},{2,1},{3,2},{4,7},{5,4},{6,5},{7,6},{8,11},{9,8},{10,9... | collective-permute-start | bytes 1105928 | tf_op jit(solution)/shard_map/ppermute | solution.py:222
  647.1 103.8 %collective-permute-start.9 = (bf16[240,768]{1,0:T(8,128)(2,1)}, bf16[240,768]{1,0:T(8,128)(2,1)}, u32[]{:S(2)}, u32[]{:S(2)}) collective-permute-start(bf16[240,768]{1,0:T(8,128)(2,1)} %get-tuple-element.125), channel_id=1, source_target_pairs={{0,1},{1,2},{2,3},{3,0},{4,5},{5,6},{6,7},{7,4},{8,9},{9,10},{10,1... | collective-permute-start | bytes 1105928 | tf_op jit(solution)/shard_map/ppermute | solution.py:222
  655.9 97.5 %collective-permute-start.10 = (bf16[240,768]{1,0:T(8,128)(2,1)S(1)}, bf16[240,768]{1,0:T(8,128)(2,1)}, u32[]{:S(2)}, u32[]{:S(2)}) collective-permute-start(bf16[240,768]{1,0:T(8,128)(2,1)S(1)} %get-tuple-element.124), channel_id=1, source_target_pairs={{0,2},{1,3},{2,0},{3,1},{4,6},{5,7},{6,4},{7,5},{8,10},{9,11},{10,... | collective-permute-start | bytes 1105928 | tf_op jit(solution)/shard_map/ppermute | solution.py:222
  656.3 99.5 %collective-permute-start.11 = (bf16[240,768]{1,0:T(8,128)(2,1)S(1)}, bf16[240,768]{1,0:T(8,128)(2,1)}, u32[]{:S(2)}, u32[]{:S(2)}) collective-permute-start(bf16[240,768]{1,0:T(8,128)(2,1)S(1)} %get-tuple-element.123), channel_id=1, source_target_pairs={{0,3},{1,0},{2,1},{3,2},{4,7},{5,4},{6,5},{7,6},{8,11},{9,8},{10,9... | collective-permute-start | bytes 1105928 | tf_op jit(solution)/shard_map/ppermute | solution.py:222
  (44 other events, 1401.2 us)
Sparse Core Ops, SparseCore 0:
  10.9 89.1 all-gather.23
  103.0 55.8 all-gather.13
  161.7 62.2 all-gather.15
  226.7 61.8 all-gather.17
  314.8 52.1 reduce-scatter.28
  370.3 53.7 reduce-scatter.32
  427.9 36.6 reduce-scatter.40
  468.4 36.6 reduce-scatter.38
  508.9 36.6 reduce-scatter.36
  549.3 36.6 reduce-scatter.42
  588.3 22.1 reduce-scatter.30
  612.6 28.2 reduce-scatter.34
  643.8 31.3 reduce-scatter.24
  677.2 28.4 reduce-scatter.22
  707.8 17.9 reduce-scatter.20
  727.9 17.7 reduce-scatter.26
  747.4 22.0 all-gather.19
  771.2 23.9 all-gather.21

commit v2 on v1

--- a/solution.py
+++ b/solution.py
@@ -200,7 +200,7 @@
     size = lax.axis_size("tensor")
     me = lax.axis_index("tensor")
     rows, seqs, width = block.shape
-    block = block.transpose(1, 0, 2)
+    block = lax.optimization_barrier(block.transpose(1, 0, 2))
     out = jnp.zeros((size * rows, width), block.dtype)
     for shift in range(size):
         piece = lax.dynamic_index_in_dim(block, (me + shift) % size, 0, keepdims=False)
@@ -215,13 +215,31 @@
     me = lax.axis_index("tensor")
     slots, width = values.shape
     rows = slots // size
-    out = jnp.zeros((size, rows, width), values.dtype)
+    out = jnp.zeros((slots, width), values.dtype)
     for shift in range(size):
         piece = lax.dynamic_slice(values, (((me + shift) % size) * rows, 0), (rows, width))
         if shift:
             piece = lax.ppermute(piece, "tensor", ring_pairs(size, shift))
-        out = lax.dynamic_update_slice(out, piece[None], ((me - shift) % size, 0, 0))
-    return out.transpose(1, 0, 2)
+        out = lax.dynamic_update_slice(out, piece, (((me - shift) % size) * rows, 0))
+    return lax.optimization_barrier(out).reshape(size, rows, width).transpose(1, 0, 2)
+
+
+def gather_pieces(shard):
+    size = lax.axis_size("tensor")
+    me = lax.axis_index("tensor")
+    core = lax.axis_index("batch") % 2
+    rows, width = shard.shape
+    half = rows // 2
+    partners = [(place, place ^ 1) for place in range(lax.axis_size("batch"))]
+    mine = lax.dynamic_slice(shard, (core * half, 0), (half, width))
+    out = lax.dynamic_update_slice(jnp.zeros((size * rows, width), shard.dtype), shard, (me * rows, 0))
+    for shift in range(1, size):
+        piece = lax.ppermute(mine, "tensor", ring_pairs(size, shift))
+        other = lax.ppermute(piece, "batch", partners)
+        first = ((me - shift) % size) * rows
+        out = lax.dynamic_update_slice(out, piece, (first + core * half, 0))
+        out = lax.dynamic_update_slice(out, other, (first + (1 - core) * half, 0))
+    return out.reshape(size, rows, width)
 
 
 def share(rows):
@@ -253,6 +271,132 @@
         1.0 + 3.0 * 0.044715 * values * values
     )
     return act, slope
+
+
+def rows_in(slots):
+    return [(r0, min(r0 + 240, slots)) for r0 in range(0, slots, 240)]
+
+
+def mlp_kernel(
+    live_ref, hid_ref, mix_ref, wo_ref, cot_ref, vec_ref, bup_ref, up_ref, down_ref,
+    y_ref, ga_ref, gmix_ref, gblock_ref, gwo_ref, sums_ref, gbup_ref,
+    n2_s, xhat_s, inv_s, y_s, d_s, gm_s,
+):
+    slots = hid_ref.shape[0]
+    step = pl.program_id(0)
+    live = live_ref[0]
+
+    def live_rows(r0, r1):
+        return lax.broadcasted_iota(jnp.int32, (r1 - r0, 1), 0) + r0 < live
+
+    @pl.when(step == 0)
+    def _():
+        for r0, r1 in rows_in(slots):
+            after = hid_ref[r0:r1, :] + dot_nn(mix_ref[r0:r1, :], wo_ref[...]) + vec_ref[0:1, :]
+            xhat, inverse = norm_parts(after)
+            xhat_s[r0:r1, :] = xhat
+            inv_s[r0:r1, :] = inverse
+            n2_s[r0:r1, :] = (xhat * vec_ref[1:2, :] + vec_ref[2:3, :]).astype(BF16)
+            y_s[r0:r1, :] = after + vec_ref[3:4, :]
+            cot = cot_ref[r0:r1, :]
+            gm_s[r0:r1, :] = jnp.where(live_rows(r0, r1), cot, jnp.zeros_like(cot))
+            d_s[r0:r1, :] = jnp.zeros((r1 - r0, d_s.shape[1]), F32)
+
+    count, units, width = up_ref.shape
+    up = up_ref[...].reshape(count * units, width)
+    down = down_ref[...].reshape(count * units, width)
+    n2 = n2_s[...]
+    grad_m = gm_s[...]
+    act, slope = gelu_parts(dot_nt(n2, up) + bup_ref[...])
+    act = act.astype(BF16)
+    grad_u = (dot_nt(grad_m, down) * slope).astype(BF16)
+    y_s[...] += dot_nn(act, down)
+    d_s[...] += dot_nn(grad_u, up)
+    gblock_ref[:, 0, 0:units, :] = dot_tn(grad_u, n2).reshape(count, units, width).astype(BF16)
+    gblock_ref[:, 0, units : 2 * units, :] = dot_tn(act, grad_m).reshape(count, units, width).astype(BF16)
+    gbup_ref[...] = jnp.sum(grad_u.astype(F32), axis=0, keepdims=True)
+
+    @pl.when(step == pl.num_programs(0) - 1)
+    def _():
+        sums = [jnp.zeros((1, width), F32)] * 4
+        for r0, r1 in rows_in(slots):
+            y_ref[r0:r1, :] = jnp.where(live_rows(r0, r1), y_s[r0:r1, :], 0.0).astype(BF16)
+            grad_n2 = d_s[r0:r1, :]
+            xhat = xhat_s[r0:r1, :]
+            grad_y = gm_s[r0:r1, :].astype(F32)
+            grad_a = grad_y + norm_back(grad_n2, xhat, inv_s[r0:r1, :], vec_ref[1:2, :])
+            ga_ref[r0:r1, :] = grad_a
+            grad_att = grad_a.astype(BF16)
+            n2_s[r0:r1, :] = grad_att
+            gmix_ref[r0:r1, :] = dot_nt(grad_att, wo_ref[...]).astype(BF16)
+            for place, value in enumerate((grad_n2 * xhat, grad_n2, grad_a, grad_y)):
+                sums[place] = sums[place] + jnp.sum(value, axis=0, keepdims=True)
+        gwo_ref[...] = dot_tn(mix_ref[...], n2_s[...]).astype(BF16)
+        for place in range(4):
+            sums_ref[place : place + 1, :] = sums[place]
+        sums_ref[4:8, :] = jnp.zeros((4, width), F32)
+
+
+def mlp(live, hidden, mixed, w_out, cot, vectors, bias_up, blocks, blocks_first, spread, groups, units):
+    slots, width = hidden.shape
+    take = 4
+    chunk = take * units
+    steps = groups * spread // take
+    per_group = spread // take
+    one = pl.Buffered(1)
+
+    def whole(shape):
+        return pl.BlockSpec(shape, lambda c, live: (0,) * len(shape), pipeline_mode=one)
+
+    full = whole((slots, width))
+    flops = 2 * slots * width * (6 * units * groups * spread + 3 * width)
+    return pl.pallas_call(
+        mlp_kernel,
+        out_shape=(
+            jax.ShapeDtypeStruct((slots, width), BF16),
+            jax.ShapeDtypeStruct((slots, width), F32),
+            jax.ShapeDtypeStruct((slots, width), BF16),
+            jax.ShapeDtypeStruct((spread, groups, 2 * units, width), BF16),
+            jax.ShapeDtypeStruct((width, width), BF16),
+            jax.ShapeDtypeStruct((8, width), F32),
+            jax.ShapeDtypeStruct((1, steps * chunk), F32),
+        ),
+        grid_spec=pltpu.PrefetchScalarGridSpec(
+            num_scalar_prefetch=1,
+            grid=(steps,),
+            in_specs=[
+                full,
+                full,
+                whole((width, width)),
+                full,
+                whole((8, width)),
+                pl.BlockSpec((1, chunk), lambda c, live: (0, c)),
+                pl.BlockSpec((take, units, width), lambda c, live: (c, blocks_first, 0)),
+                pl.BlockSpec((take, units, width), lambda c, live: (c, blocks_first + 1, 0)),
+            ],
+            out_specs=(
+                full,
+                full,
+                full,
+                pl.BlockSpec((take, 1, 2 * units, width), lambda c, live: (c % per_group, c // per_group, 0, 0)),
+                whole((width, width)),
+                whole((8, width)),
+                pl.BlockSpec((1, chunk), lambda c, live: (0, c)),
+            ),
+            scratch_shapes=[
+                pltpu.VMEM((slots, width), BF16),
+                pltpu.VMEM((slots, width), F32),
+                pltpu.VMEM((slots, 1), F32),
+                pltpu.VMEM((slots, width), F32),
+                pltpu.VMEM((slots, width), F32),
+                pltpu.VMEM((slots, width), BF16),
+            ],
+        ),
+        cost_estimate=pl.CostEstimate(
+            flops=flops, transcendentals=slots * steps * chunk, bytes_accessed=20 * slots * width + 8 * steps * chunk * width
+        ),
+        name="mlp",
+    )(live, hidden, mixed, w_out, cot, vectors, bias_up, blocks, blocks)
 
 
 def per_device(
@@ -287,28 +431,29 @@
     gain_two, shift_two = ln2_gain.astype(F32), ln2_bias.astype(F32)
     table = pass_table.astype(F32)
 
-    qkv_rows = w_qkv.transpose(1, 2, 0)
-    every = ("tensor", "batch")
-    gathered_qkv = lax.all_gather(
-        jnp.concatenate([share(qkv_rows[part]) for part in range(3)], axis=0)[None], every, axis=0, tiled=True
-    )
     each = width // (groups * spread)
-    gathered_qkv = gathered_qkv.reshape(groups * spread, 3, each, width)
-    matrix_q, matrix_k, matrix_v = (gathered_qkv[:, part].reshape(width, width) for part in range(3))
-    matrix_out = lax.all_gather(share(w_out), every, axis=0, tiled=True)
-    mixed_order = ("batch", "tensor")
-    matrix_up = lax.all_gather(share(w_up.T), mixed_order, axis=0, tiled=True)
-    matrix_down = lax.all_gather(share(w_down), mixed_order, axis=0, tiled=True)
-    bias_row = jnp.concatenate([q_bias, v_bias, up_bias]).astype(BF16)
-    bias_rows = lax.all_gather(bias_row, "tensor", axis=0)
+    units = hidden_here // spread
     here = q_bias.shape[0]
-    bias_query = bias_rows[:, :here].reshape(1, width).astype(F32)
-    bias_value = bias_rows[:, here : 2 * here].reshape(1, width).astype(F32)
-    bias_up = bias_rows[:, 2 * here :].reshape(groups, spread, hidden_here // spread)
-    bias_up = bias_up.transpose(1, 0, 2).reshape(1, hidden_units).astype(F32)
-
     states = to_sequence(slot_states).astype(F32)
-    cot = to_sequence(cotangent)
+    biases = jnp.concatenate([q_bias, v_bias, jnp.zeros((width - 2 * here,), BF16)]).reshape(1, width)
+    shard = jnp.concatenate(
+        [w_qkv.transpose(1, 2, 0).reshape(3 * here, width), jnp.pad(biases, ((0, 15), (0, 0)))], axis=0
+    )
+    shards = gather_pieces(shard)
+    matrix_q, matrix_k, matrix_v = (
+        shards[:, part * here : (part + 1) * here].reshape(width, width) for part in range(3)
+    )
+    bias_rows = shards[:, 3 * here].astype(F32)
+    bias_query = bias_rows[:, :here].reshape(1, width)
+    bias_value = bias_rows[:, here : 2 * here].reshape(1, width)
+
+    bias_row = jnp.pad(up_bias.reshape(1, width), ((0, 15), (0, 0)))
+    block = jnp.concatenate([share(w_up.T), share(w_down), share(w_out), bias_row], axis=0)
+    blocks = lax.all_gather(block, ("tensor", "batch"), axis=0, tiled=False)
+    matrix_out = blocks[:, 2 * units : 2 * units + each].reshape(width, width)
+    bias_up = blocks.reshape(groups, spread, block.shape[0], width)[:, 0, 2 * units + each]
+    bias_up = bias_up.reshape(1, hidden_units).astype(F32)
+
     count = lax.dynamic_index_in_dim(pass_counts, me, 0, keepdims=False)
     index = jnp.arange(slots, dtype=jnp.int32)
     passes = (index % count)[:, None]
@@ -325,29 +470,31 @@
     query = (dot_nt(n1, matrix_q) + bias_query).astype(BF16)
     keys = dot_nt(n1, matrix_k).astype(BF16)
     values = (dot_nt(n1, matrix_v) + bias_value).astype(BF16)
+    query, cotangent = lax.optimization_barrier((query, cotangent))
+    cot = to_sequence(cotangent)
     mixed, lse = attend(live_arg, query, keys, values)
-    after = hidden + dot_nn(mixed, matrix_out) + out_bias.astype(F32)
-    xhat_two, inverse_two = norm_parts(after)
-    n2 = (xhat_two * gain_two + shift_two).astype(BF16)
-    pre_act = dot_nt(n2, matrix_up) + bias_up
-    act, slope = gelu_parts(pre_act)
-    act = act.astype(BF16)
-    result = after + dot_nn(act, matrix_down) + down_bias.astype(F32)
-    layer_out = jnp.where(live, result, 0.0).astype(BF16)
+    vectors = jnp.stack([out_bias.astype(F32), gain_two, shift_two, down_bias.astype(F32)])
+    vectors = jnp.pad(vectors, ((0, 4), (0, 0)))
+    regroup = units % 32 != 0
+    fold, fold_units = (8, hidden_here // 8) if regroup else (spread, units)
+    if regroup:
+        blocks = jnp.concatenate(
+            [
+                blocks[:, part * units : (part + 1) * units].reshape(groups * fold, fold_units, width)
+                for part in range(2)
+            ],
+            axis=1,
+        )
+    layer_out, grad_a, grad_mixed, mlp_block, grad_out, sums, grad_bias_up = mlp(
+        live_arg, hidden, mixed, matrix_out, cot, vectors, bias_up, blocks, 0, fold, groups, fold_units
+    )
+    if regroup:
+        mlp_block = mlp_block.reshape(fold, groups, 2, fold_units, width).transpose(1, 2, 0, 3, 4)
+        mlp_block = mlp_block.reshape(groups, 2, spread, units, width).transpose(2, 0, 1, 3, 4)
+        mlp_block = mlp_block.reshape(spread, groups, 2 * units, width)
     layer_part = to_slots(layer_out)
-
-    grad_m = jnp.where(live, cot, jnp.zeros_like(cot))
-    grad_y = grad_m.astype(F32)
-    grad_down = dot_tn(act, grad_m).astype(BF16)
-    grad_act = dot_nt(grad_m, matrix_down)
-    grad_u = (grad_act * slope).astype(BF16)
-    grad_up = dot_tn(grad_u, n2).astype(BF16)
-    grad_n2 = dot_nn(grad_u, matrix_up)
-    grad_a = grad_y + norm_back(grad_n2, xhat_two, inverse_two, gain_two)
-    grad_att = grad_a.astype(BF16)
-    grad_out = dot_tn(mixed, grad_att).astype(BF16)
-    grad_mixed = dot_nt(grad_att, matrix_out).astype(BF16)
     grad_q, grad_k, grad_v = attend_back(live_arg, query, keys, values, mixed, grad_mixed, lse)
+    grad_q, layer_part = lax.optimization_barrier((grad_q, layer_part))
     grad_wq = dot_tn(grad_q, n1).astype(BF16)
     grad_wk = dot_tn(grad_k, n1).astype(BF16)
     grad_wv = dot_tn(grad_v, n1).astype(BF16)
@@ -355,58 +502,70 @@
     grad_h = grad_a + norm_back(grad_n1, xhat_one, inverse_one, gain_one)
     grad_part = to_slots(grad_h.astype(BF16))
 
-    def reduce_mixed(value):
-        value = lax.psum_scatter(value, "batch", scatter_dimension=0, tiled=True)
-        value = lax.psum_scatter(value, "tensor", scatter_dimension=0, tiled=True)
-        return lax.all_gather(value, "batch", axis=0, tiled=True).astype(F32)
-
-    def reduce_plain(value):
-        value = value.reshape(groups, -1, width)
-        value = lax.psum_scatter(value, "batch", scatter_dimension=1, tiled=True)
-        value = lax.psum_scatter(value, "tensor", scatter_dimension=0, tiled=True)
-        return lax.all_gather(value[0], "batch", axis=0, tiled=True).astype(F32)
-
-    out_down = reduce_mixed(grad_down)
-    out_up = reduce_mixed(grad_up).T
-    out_out = reduce_plain(grad_out)
-    out_qkv = jnp.stack([reduce_plain(value) for value in (grad_wq, grad_wk, grad_wv)], axis=0).transpose(2, 0, 1)
-
     def total(value):
         return jnp.sum(value.astype(F32), axis=0, keepdims=True)
 
-    grad_pass = jnp.concatenate(
-        [total(jnp.where(passes == number, grad_h, 0.0)) for number in range(PASSES)], axis=0
-    )
-    grad_bias_up = total(grad_u).reshape(spread, groups, hidden_here // spread)
-    grad_bias_up = grad_bias_up.transpose(1, 0, 2).reshape(groups, width)
-    small = jnp.concatenate(
+    grad_bias_up = grad_bias_up.reshape(groups, 1, hidden_here)
+    common = jnp.concatenate(
         [
             total(grad_n1 * xhat_one),
             total(grad_n1),
-            total(grad_n2 * xhat_two),
-            total(grad_n2),
-            total(grad_a),
-            total(grad_y),
-            grad_pass,
-            total(grad_q),
-            total(grad_v),
-            grad_bias_up,
+            sums[0:4],
+        ]
+        + [total(jnp.where(passes == number, grad_h, 0.0)) for number in range(PASSES)],
+        axis=0,
+    )
+    lead = common.shape[0]
+    own = jnp.concatenate(
+        [
+            total(grad_q).reshape(groups, 1, here),
+            total(grad_v).reshape(groups, 1, here),
+            jnp.zeros((groups, 1, width - 2 * here), F32),
         ],
-        axis=0,
-    )
-    small = lax.psum(small, ("batch", "tensor"))
-    lead = 6 + PASSES
-    mine = lax.dynamic_slice_in_dim(small[lead : lead + 2], me * here, here, axis=1)
+        axis=2,
+    )
+    small = jnp.concatenate(
+        [jnp.broadcast_to(common[None], (groups, lead, width)), own, grad_bias_up], axis=1
+    )
+    extra = 16
+    small = jnp.pad(small, ((0, 0), (0, spread * extra - lead - 2), (0, 0)))
+    small = small.reshape(groups, spread, extra, width).transpose(1, 0, 2, 3).astype(BF16)
+
+    def spread_rows(value):
+        return value.reshape(groups, spread, each, width).transpose(1, 0, 2, 3)
+
+    attn_block = jnp.concatenate(
+        [spread_rows(value) for value in (grad_wq, grad_wk, grad_wv, grad_out)] + [small], axis=2
+    )
+    def over_tensor(value):
+        kept = lax.dynamic_index_in_dim(value, me, 0, keepdims=False).astype(F32)
+        for shift in range(1, groups):
+            piece = lax.dynamic_index_in_dim(value, (me + shift) % groups, 0, keepdims=False)
+            kept = kept + lax.ppermute(piece, "tensor", ring_pairs(groups, shift)).astype(F32)
+        return kept.astype(BF16)
+
+    mlp_block = lax.psum_scatter(mlp_block, "batch", scatter_dimension=0, tiled=True)[0]
+    attn_block, mlp_block = lax.optimization_barrier((attn_block, mlp_block))
+    attn_block = lax.psum_scatter(attn_block, "batch", scatter_dimension=0, tiled=True)[0]
+    mlp_piece = over_tensor(mlp_block)
+    attn_piece = over_tensor(attn_block)
+    whole = lax.all_gather(jnp.concatenate([attn_piece, mlp_piece], axis=0), "batch", axis=0, tiled=False)
+    parts = [whole[:, part * each : (part + 1) * each].reshape(here, width).astype(F32) for part in range(4)]
+    small = whole[:, 4 * each : 4 * each + extra].reshape(spread * extra, width).astype(F32)
+    base = 4 * each + extra
+    out_up = whole[:, base : base + units].reshape(hidden_here, width).astype(F32).T
+    out_down = whole[:, base + units :].reshape(hidden_here, width).astype(F32)
+    out_qkv = jnp.stack(parts[:3], axis=0).transpose(2, 0, 1)
     return (
         layer_part,
         grad_part,
         out_qkv,
-        mine[0],
-        mine[1],
-        out_out,
+        small[lead, :here],
+        small[lead, here : 2 * here],
+        parts[3],
         small[4],
         out_up,
-        lax.dynamic_index_in_dim(small[lead + 2 :], me, 0, keepdims=False),
+        small[lead + 1],
         out_down,
         small[5],
         small[0],

time: 904 us -> 468 us (0.52)
  blocking collectives: 163 us -> 0 us
  waiting for transfers between devices: 330 us -> 182 us
  local copies, waits for them, and re-layouts: 176 us -> 59.5 us
  matrix products: 105 us -> 25.3 us
  Pallas kernels: 45.3 us -> 108 us
  starting transfers between devices: 26.7 us -> 52.8 us
    unnamed x22 -> x4, waiting for transfers between devices: 157 us -> 0.07 us
    all_gather x5 -> x0, blocking collectives: 106 us -> none  [the longest x1 69.1 us: per_device(): bias_rows = lax.all_gather(bias_row, 'tensor', axis=0)]
    all_gather x6 -> x2, waiting for transfers between devices: 108 us -> 5.81 us  [the longest x1 5.79 us: per_device(): lax.all_gather(jnp.concatenate([attn_piece, mlp_piece], axis=0), 'batch',...]
    dynamic_update_slice x8 -> x12, local copies, waits for them, and re-layouts: 105 us -> 9.06 us  [the longest x3 3.42 us: gather_pieces(): out = lax.dynamic_update_slice(out, piece, (first + core * half, 0))]
    ppermute x6, waiting for transfers between devices: 1.41 us -> 61.3 us  [to_sequence(): piece = lax.ppermute(piece, 'tensor', ring_pairs(size, shift))]
    psum x1 -> x0, blocking collectives: 57.7 us -> none  [per_device(): small = lax.psum(small, ('batch', 'tensor'))]
    pallas_call x0 -> x1, Pallas kernels: none -> 51.2 us  [mlp(): pl.pallas_call(mlp_kernel, out_shape=(jax.ShapeDtypeStruct((slots, width)...]
    ppermute x0 -> x12, waiting for transfers between devices: none -> 38.9 us  [the longest x3 30.5 us: gather_pieces(): piece = lax.ppermute(mine, 'tensor', ring_pairs(size, shift))]
  transfers between devices with their start and end apart: 30 -> 28, of which waited for: 10 -> 9; matrix products, arithmetic and copies ran while one was open for 31% -> 16% of each run, Pallas kernels for 5% -> 12%
where the time goes in v2:
time: 468 us; the launch traced here: 464 us
  waiting for transfers between devices  182 us (39%)
  Pallas kernels  108 us (23%)
  local copies, waits for them, and re-layouts  59.5 us (13%)
  starting transfers between devices  52.8 us (11%)
  matrix products  25.3 us (5%)
  other arithmetic  19.2 us (4%)
  between operations  17 us (4%)
    ppermute x6, waiting for transfers between devices, to_sequence(): piece = lax.ppermute(piece, 'tensor', ring_pairs(size, shift))  61.3 us
    reduce_scatter x1, waiting for transfers between devices, per_device(): lax.psum_scatter(attn_block, 'batch', scatter_dimension=0, tiled=True)[0]  54.3 us
    pallas_call x1, Pallas kernels, mlp(): pl.pallas_call(mlp_kernel, out_shape=(jax.ShapeDtypeStruct((slots, width)...  51.2 us
    pallas_call x1, Pallas kernels, attend_back(): pl.pallas_call(attend_back_kernel, out_shape=(shape, shape, shape), grid_...  34.7 us
    ppermute x3, waiting for transfers between devices, gather_pieces(): piece = lax.ppermute(mine, 'tensor', ring_pairs(size, shift))  30.5 us
    ppermute x6, waiting for transfers between devices, to_slots(): piece = lax.ppermute(piece, 'tensor', ring_pairs(size, shift))  22 us
    pallas_call x1, Pallas kernels, attend(): pl.pallas_call(attend_kernel, out_shape=(jax.ShapeDtypeStruct((slots, wid...  21.9 us
    ppermute x6, starting transfers between devices, to_slots(): piece = lax.ppermute(piece, 'tensor', ring_pairs(size, shift))  18 us
  transfers between devices with their start and end apart: 28, of which 9 were waited for; matrix products, arithmetic and copies ran while one was open for 16% of the time, Pallas kernels for 12%

profile of v2, /device:TPU:0, one launch (start us, length us, event | category | flops | bytes accessed | tf_op | source)
XLA Modules:
  0.0 463.9 jit_solution(4475253356610100225)
XLA Ops:
  16.1 3.1 collective-permute-start.3
  19.2 2.5 collective-permute-start.5
  30.1 28.0 %collective-permute-done = bf16[240,768]{1,0:T(8,128)(2,1)} collective-permute-done((bf16[240,768]{1,0:T(8,128)(2,1)S(1)}, bf16[240,768]{1,0:T(8,128)(2,1)}, u32[]{:S(2)}, u32[]{:S(2)}) %collective-permute-start) | collective-permute-done | bytes 368672 | tf_op jit(solution)/shard_map/ppermute | solution.py:208
  59.1 33.3 %collective-permute-done.1 = bf16[240,768]{1,0:T(8,128)(2,1)} collective-permute-done((bf16[240,768]{1,0:T(8,128)(2,1)S(1)}, bf16[240,768]{1,0:T(8,128)(2,1)}, u32[]{:S(2)}, u32[]{:S(2)}) %collective-permute-start.1) | collective-permute-done | bytes 368672 | tf_op jit(solution)/shard_map/ppermute | solution.py:208
  97.9 30.5 %collective-permute-done.7 = bf16[296,768]{1,0:T(8,128)(2,1)S(1)} collective-permute-done((bf16[296,768]{1,0:T(8,128)(2,1)}, bf16[296,768]{1,0:T(8,128)(2,1)S(1)}, u32[]{:S(2)}, u32[]{:S(2)}) %collective-permute-start.7) | collective-permute-done | bytes 454688 | tf_op jit(solution)/shard_map/ppermute | solution.py:237
  135.3 3.4 fusion.30
  142.4 4.1 collective-permute-start.9
  149.1 4.3 convolution_convert_fusion.k_ref
  155.9 21.9 %attend.1 = (bf16[960,768]{1,0:T(8,128)(2,1)}, f32[6,2,960]{2,1,0:T(2,128)}) custom-call(s32[1]{0:T(128)} %bitcast.1.live_ref, bf16[960,768]{1,0:T(8,128)(2,1)} %add_convert_fusion.1.q_ref, bf16[960,768]{1,0:T(8,128)(2,1)} %convolution_convert_fusion.k_ref, bf16[960,768]{1,0:T(8,128)(2,1)} %add_convert_fusion.v_ref), custom_call_target="tpu_custom_call" | custom-call | flops 2831155200 | bytes 5898240 | tf_op jit(solution)/shard_map/attend/pallas_call | solution.py:147
  181.1 2.9 slice.135
  185.4 51.2 %mlp.1 = (bf16[960,768]{1,0:T(8,128)(2,1)}, f32[960,768]{1,0:T(8,128)}, bf16[960,768]{1,0:T(8,128)(2,1)}, bf16[8,4,192,768]{3,2,1,0:T(8,128)(2,1)}, bf16[768,768...) custom-call(s32[1]{0:T(128)} %bitcast.1.live_ref, f32[960,768]{1,0:T(8,128)} %copy-done.2, ...), custom_call_target="tpu_custom_call" | custom-call | flops 30576476160 | bytes 33619968 | tf_op jit(solution)/shard_map/mlp/pallas_call | solution.py:353
  240.6 9.7 %collective-permute-start.13 = (bf16[240,768]{1,0:T(8,128)(2,1)}, bf16[240,768]{1,0:T(8,128)(2,1)}, u32[]{:S(2)}, u32[]{:S(2)}) collective-permute-start(bf16[240,768]{1,0:T(8,128)(2,1)} %get-tuple-element.106), channel_id=1, source_target_pairs={{0,2},{1,3},{2,0},{3,1},{4,6},{5,7},{6,4},{7,5},{8,10},{9,11},{10,... | collective-permute-start | bytes 1105928 | tf_op jit(solution)/shard_map/ppermute | solution.py:222
  250.3 34.7 %attend_back.1 = (bf16[960,768]{1,0:T(8,128)(2,1)}, bf16[960,768]{1,0:T(8,128)(2,1)}, bf16[960,768]{1,0:T(8,128)(2,1)}) custom-call(s32[1]{0:T(128)} %bitcast.1.live_ref, bf16[960,768]{1,0:T(8,128)(2,1)} %add_convert_fusion.1.q_ref, bf16[960,768]{1,0:T(8,128)(2,1)} %convolution_convert_fusion.k_ref, bf16[960,768]{1,0:T(8,128)(2,1)} %add_convert_fusion.v_ref, ...), custom_call_target="tpu_custom_call" | custom-call | flops 7077888000 | bytes 11796480 | tf_op jit(solution)/shard_map/attend_back/pallas_call | solution.py:174
  285.0 4.4 convolution_convert_fusion.2
  291.9 2.9 fusion.34
  306.7 2.8 select_reduce_fusion
  311.6 2.9 convolution_convert_fusion.3
  324.3 10.7 %collective-permute-start.22 = (bf16[192,768]{1,0:T(8,128)(2,1)S(1)}, bf16[192,768]{1,0:T(8,128)(2,1)}, u32[]{:S(2)}, u32[]{:S(2)}) collective-permute-start(bf16[192,768]{1,0:T(8,128)(2,1)S(1)} %get-tuple-element.117), channel_id=1, source_target_pairs={{0,2},{1,3},{2,0},{3,1},{4,6},{5,7},{6,4},{7,5},{8,10},{9,11},{10,... | collective-permute-start | bytes 884744 | tf_op jit(solution)/shard_map/ppermute | solution.py:544
  335.0 54.3 %reduce-scatter.5.cloned.1.call-done = bf16[1,4,112,768]{3,2,1,0:T(8,128)(2,1)} async-done(((bf16[8,4,112,768]{3,2,1,0:T(8,128)(2,1)}), bf16[1,4,112,768]{3,2,1,0:T(8,128)(2,1)}) %reduce-scatter.5.cloned.1.call-update) | async-done | bytes 688144 | tf_op jit(solution)/shard_map/reduce_scatter | solution.py:549
  399.6 6.1 %collective-permute-done.19 = bf16[112,768]{1,0:T(8,128)(2,1)S(1)} collective-permute-done((bf16[112,768]{1,0:T(8,128)(2,1)S(1)}, bf16[112,768]{1,0:T(8,128)(2,1)S(1)}, u32[]{:S(2)}, u32[]{:S(2)}) %collective-permute-start.19) | collective-permute-done | bytes 172064 | tf_op jit(solution)/shard_map/ppermute | solution.py:544
  407.8 4.2 collective-permute-start.15
  414.4 8.1 %collective-permute-done.15 = bf16[240,768]{1,0:T(8,128)(2,1)S(1)} collective-permute-done((bf16[240,768]{1,0:T(8,128)(2,1)S(1)}, bf16[240,768]{1,0:T(8,128)(2,1)S(1)}, u32[]{:S(2)}, u32[]{:S(2)}) %collective-permute-start.15) | collective-permute-done | bytes 368672 | tf_op jit(solution)/shard_map/ppermute | solution.py:222
  422.5 13.9 %collective-permute-done.16 = bf16[240,768]{1,0:T(8,128)(2,1)S(1)} collective-permute-done((bf16[240,768]{1,0:T(8,128)(2,1)S(1)}, bf16[240,768]{1,0:T(8,128)(2,1)S(1)}, u32[]{:S(2)}, u32[]{:S(2)}) %collective-permute-start.16) | collective-permute-done | bytes 368672 | tf_op jit(solution)/shard_map/ppermute | solution.py:222
  438.4 5.8 %all-gather.7.cloned.1.call-done = bf16[2432,768]{1,0:T(8,128)(2,1)} async-done(((bf16[304,768]{1,0:T(8,128)(2,1)}), bf16[2432,768]{1,0:T(8,128)(2,1)}) %all-gather.7.cloned.1.call-update) | async-done | bytes 3735568 | tf_op jit(solution)/shard_map/all_gather | solution.py:552
  (248 shorter events, 101.3 us)
Async XLA Ops:
  7.2 173.9 %all-gather.5.cloned.1.call-start = ((), (), s32[]{:S(2)}) async-start(), calls=%async_computation.4 | async-start | bytes 11759616 | tf_op jit(solution)/shard_map/all_gather | solution.py:452
  11.9 309.4 %reduce-scatter.3.cloned.1.call-start = ((), (), s32[]{:S(2)}) async-start(), calls=%async_computation.2 | async-start | bytes 10616832 | tf_op jit(solution)/shard_map/reduce_scatter | solution.py:547
  16.1 79.1 %collective-permute-start.3 = (bf16[296,768]{1,0:T(8,128)(2,1)}, bf16[296,768]{1,0:T(8,128)(2,1)}, u32[]{:S(2)}, u32[]{:S(2)}) collective-permute-start(bf16[296,768]{1,0:T(8,128)(2,1)} %constant_dynamic-slice_fusion.9), channel_id=1, source_target_pairs={{0,1},{1,2},{2,3},{3,0},{4,5},{5,6},{6,7},{7,4},{8,9},{9,10},{10,1... | collective-permute-start | bytes 1363976 | tf_op jit(solution)/shard_map/ppermute | solution.py:237
  19.2 76.1 %collective-permute-start.5 = (bf16[296,768]{1,0:T(8,128)(2,1)}, bf16[296,768]{1,0:T(8,128)(2,1)S(1)}, u32[]{:S(2)}, u32[]{:S(2)}) collective-permute-start(bf16[296,768]{1,0:T(8,128)(2,1)} %constant_dynamic-slice_fusion.9), channel_id=1, source_target_pairs={{0,2},{1,3},{2,0},{3,1},{4,6},{5,7},{6,4},{7,5},{8,10},{9,11},{10,... | collective-permute-start | bytes 1363976 | tf_op jit(solution)/shard_map/ppermute | solution.py:237
  22.1 36.0 %collective-permute-start = (bf16[240,768]{1,0:T(8,128)(2,1)S(1)}, bf16[240,768]{1,0:T(8,128)(2,1)}, u32[]{:S(2)}, u32[]{:S(2)}) collective-permute-start(bf16[240,768]{1,0:T(8,128)(2,1)S(1)} %get-tuple-element.114), channel_id=1, source_target_pairs={{0,1},{1,2},{2,3},{3,0},{4,5},{5,6},{6,7},{7,4},{8,9},{9,10},{10,1... | collective-permute-start | bytes 1105928 | tf_op jit(solution)/shard_map/ppermute | solution.py:208
  22.2 70.2 %collective-permute-start.1 = (bf16[240,768]{1,0:T(8,128)(2,1)S(1)}, bf16[240,768]{1,0:T(8,128)(2,1)}, u32[]{:S(2)}, u32[]{:S(2)}) collective-permute-start(bf16[240,768]{1,0:T(8,128)(2,1)S(1)} %get-tuple-element.113), channel_id=1, source_target_pairs={{0,2},{1,3},{2,0},{3,1},{4,6},{5,7},{6,4},{7,5},{8,10},{9,11},{10,... | collective-permute-start | bytes 1105928 | tf_op jit(solution)/shard_map/ppermute | solution.py:208
  24.1 69.3 %collective-permute-start.2 = (bf16[240,768]{1,0:T(8,128)(2,1)S(1)}, bf16[240,768]{1,0:T(8,128)(2,1)S(1)}, u32[]{:S(2)}, u32[]{:S(2)}) collective-permute-start(bf16[240,768]{1,0:T(8,128)(2,1)S(1)} %get-tuple-element.112), channel_id=1, source_target_pairs={{0,3},{1,0},{2,1},{3,2},{4,7},{5,4},{6,5},{7,6},{8,11},{9,8},{10,9... | collective-permute-start | bytes 1105928 | tf_op jit(solution)/shard_map/ppermute | solution.py:208
  58.1 70.3 %collective-permute-start.7 = (bf16[296,768]{1,0:T(8,128)(2,1)}, bf16[296,768]{1,0:T(8,128)(2,1)S(1)}, u32[]{:S(2)}, u32[]{:S(2)}) collective-permute-start(bf16[296,768]{1,0:T(8,128)(2,1)} %constant_dynamic-slice_fusion.9), channel_id=1, source_target_pairs={{0,3},{1,0},{2,1},{3,2},{4,7},{5,4},{6,5},{7,6},{8,11},{9,8},{10,9... | collective-permute-start | bytes 1363976 | tf_op jit(solution)/shard_map/ppermute | solution.py:237
  95.2 35.0 %collective-permute-start.4 = (bf16[296,768]{1,0:T(8,128)(2,1)}, bf16[296,768]{1,0:T(8,128)(2,1)S(1)}, u32[]{:S(2)}, u32[]{:S(2)}) collective-permute-start(bf16[296,768]{1,0:T(8,128)(2,1)} %collective-permute-done.3), channel_id=1, source_target_pairs={{0,4},{4,0},{8,12},{12,8},{16,20},{20,16},{24,28},{28,24},{1,5},{5... | collective-permute-start | bytes 1363976 | tf_op jit(solution)/shard_map/ppermute | solution.py:238
  95.3 36.5 %collective-permute-start.6 = (bf16[296,768]{1,0:T(8,128)(2,1)S(1)}, bf16[296,768]{1,0:T(8,128)(2,1)S(1)}, u32[]{:S(2)}, u32[]{:S(2)}) collective-permute-start(bf16[296,768]{1,0:T(8,128)(2,1)S(1)} %collective-permute-done.5), channel_id=1, source_target_pairs={{0,4},{4,0},{8,12},{12,8},{16,20},{20,16},{24,28},{28,24},{1,5},{5... | collective-permute-start | bytes 1363976 | tf_op jit(solution)/shard_map/ppermute | solution.py:238
  142.4 35.6 %collective-permute-start.9 = (bf16[240,768]{1,0:T(8,128)(2,1)}, bf16[240,768]{1,0:T(8,128)(2,1)}, u32[]{:S(2)}, u32[]{:S(2)}) collective-permute-start(bf16[240,768]{1,0:T(8,128)(2,1)} %get-tuple-element.111), channel_id=1, source_target_pairs={{0,1},{1,2},{2,3},{3,0},{4,5},{5,6},{6,7},{7,4},{8,9},{9,10},{10,1... | collective-permute-start | bytes 1105928 | tf_op jit(solution)/shard_map/ppermute | solution.py:208
  146.5 32.5 %collective-permute-start.10 = (bf16[240,768]{1,0:T(8,128)(2,1)}, bf16[240,768]{1,0:T(8,128)(2,1)}, u32[]{:S(2)}, u32[]{:S(2)}) collective-permute-start(bf16[240,768]{1,0:T(8,128)(2,1)} %get-tuple-element.110), channel_id=1, source_target_pairs={{0,2},{1,3},{2,0},{3,1},{4,6},{5,7},{6,4},{7,5},{8,10},{9,11},{10,... | collective-permute-start | bytes 1105928 | tf_op jit(solution)/shard_map/ppermute | solution.py:208
  147.2 32.8 %collective-permute-start.11 = (bf16[240,768]{1,0:T(8,128)(2,1)S(1)}, bf16[240,768]{1,0:T(8,128)(2,1)}, u32[]{:S(2)}, u32[]{:S(2)}) collective-permute-start(bf16[240,768]{1,0:T(8,128)(2,1)S(1)} %get-tuple-element.109), channel_id=1, source_target_pairs={{0,3},{1,0},{2,1},{3,2},{4,7},{5,4},{6,5},{7,6},{8,11},{9,8},{10,9... | collective-permute-start | bytes 1105928 | tf_op jit(solution)/shard_map/ppermute | solution.py:208
  236.6 152.7 %reduce-scatter.5.cloned.1.call-start = ((), (), s32[]{:S(2)}) async-start(), calls=%async_computation.3 | async-start | bytes 6193152 | tf_op jit(solution)/shard_map/reduce_scatter | solution.py:549
  239.0 57.0 %collective-permute-start.12 = (bf16[240,768]{1,0:T(8,128)(2,1)}, bf16[240,768]{1,0:T(8,128)(2,1)}, u32[]{:S(2)}, u32[]{:S(2)}) collective-permute-start(bf16[240,768]{1,0:T(8,128)(2,1)} %get-tuple-element.107), channel_id=1, source_target_pairs={{0,1},{1,2},{2,3},{3,0},{4,5},{5,6},{6,7},{7,4},{8,9},{9,10},{10,1... | collective-permute-start | bytes 1105928 | tf_op jit(solution)/shard_map/ppermute | solution.py:222
  240.6 56.4 %collective-permute-start.13 = (bf16[240,768]{1,0:T(8,128)(2,1)}, bf16[240,768]{1,0:T(8,128)(2,1)}, u32[]{:S(2)}, u32[]{:S(2)}) collective-permute-start(bf16[240,768]{1,0:T(8,128)(2,1)} %get-tuple-element.106), channel_id=1, source_target_pairs={{0,2},{1,3},{2,0},{3,1},{4,6},{5,7},{6,4},{7,5},{8,10},{9,11},{10,... | collective-permute-start | bytes 1105928 | tf_op jit(solution)/shard_map/ppermute | solution.py:222
  250.3 47.8 %collective-permute-start.14 = (bf16[240,768]{1,0:T(8,128)(2,1)S(1)}, bf16[240,768]{1,0:T(8,128)(2,1)}, u32[]{:S(2)}, u32[]{:S(2)}) collective-permute-start(bf16[240,768]{1,0:T(8,128)(2,1)S(1)} %get-tuple-element.105), channel_id=1, source_target_pairs={{0,3},{1,0},{2,1},{3,2},{4,7},{5,4},{6,5},{7,6},{8,11},{9,8},{10,9... | collective-permute-start | bytes 1105928 | tf_op jit(solution)/shard_map/ppermute | solution.py:222
  321.3 122.8 %all-gather.7.cloned.1.call-start = ((), (), s32[]{:S(2)}) async-start(), calls=%async_computation.5 | async-start | bytes 4202496 | tf_op jit(solution)/shard_map/all_gather | solution.py:552
  322.6 71.7 %collective-permute-start.21 = (bf16[192,768]{1,0:T(8,128)(2,1)S(1)}, bf16[192,768]{1,0:T(8,128)(2,1)}, u32[]{:S(2)}, u32[]{:S(2)}) collective-permute-start(bf16[192,768]{1,0:T(8,128)(2,1)S(1)} %get-tuple-element.115), channel_id=1, source_target_pairs={{0,1},{1,2},{2,3},{3,0},{4,5},{5,6},{6,7},{7,4},{8,9},{9,10},{10,1... | collective-permute-start | bytes 884744 | tf_op jit(solution)/shard_map/ppermute | solution.py:544
  324.3 71.7 %collective-permute-start.22 = (bf16[192,768]{1,0:T(8,128)(2,1)S(1)}, bf16[192,768]{1,0:T(8,128)(2,1)}, u32[]{:S(2)}, u32[]{:S(2)}) collective-permute-start(bf16[192,768]{1,0:T(8,128)(2,1)S(1)} %get-tuple-element.117), channel_id=1, source_target_pairs={{0,2},{1,3},{2,0},{3,1},{4,6},{5,7},{6,4},{7,5},{8,10},{9,11},{10,... | collective-permute-start | bytes 884744 | tf_op jit(solution)/shard_map/ppermute | solution.py:544
  335.0 61.0 %collective-permute-start.23 = (bf16[192,768]{1,0:T(8,128)(2,1)S(1)}, bf16[192,768]{1,0:T(8,128)(2,1)}, u32[]{:S(2)}, u32[]{:S(2)}) collective-permute-start(bf16[192,768]{1,0:T(8,128)(2,1)S(1)} %get-tuple-element.116), channel_id=1, source_target_pairs={{0,3},{1,0},{2,1},{3,2},{4,7},{5,4},{6,5},{7,6},{8,11},{9,8},{10,9... | collective-permute-start | bytes 884744 | tf_op jit(solution)/shard_map/ppermute | solution.py:544
  407.8 14.7 %collective-permute-start.15 = (bf16[240,768]{1,0:T(8,128)(2,1)S(1)}, bf16[240,768]{1,0:T(8,128)(2,1)S(1)}, u32[]{:S(2)}, u32[]{:S(2)}) collective-permute-start(bf16[240,768]{1,0:T(8,128)(2,1)S(1)} %get-tuple-element.103), channel_id=1, source_target_pairs={{0,1},{1,2},{2,3},{3,0},{4,5},{5,6},{6,7},{7,4},{8,9},{9,10},{10,1... | collective-permute-start | bytes 1105928 | tf_op jit(solution)/shard_map/ppermute | solution.py:222
  412.0 24.4 %collective-permute-start.16 = (bf16[240,768]{1,0:T(8,128)(2,1)S(1)}, bf16[240,768]{1,0:T(8,128)(2,1)S(1)}, u32[]{:S(2)}, u32[]{:S(2)}) collective-permute-start(bf16[240,768]{1,0:T(8,128)(2,1)S(1)} %get-tuple-element.102), channel_id=1, source_target_pairs={{0,2},{1,3},{2,0},{3,1},{4,6},{5,7},{6,4},{7,5},{8,10},{9,11},{10,... | collective-permute-start | bytes 1105928 | tf_op jit(solution)/shard_map/ppermute | solution.py:222
  413.5 23.0 %collective-permute-start.17 = (bf16[240,768]{1,0:T(8,128)(2,1)S(1)}, bf16[240,768]{1,0:T(8,128)(2,1)S(1)}, u32[]{:S(2)}, u32[]{:S(2)}) collective-permute-start(bf16[240,768]{1,0:T(8,128)(2,1)S(1)} %get-tuple-element.101), channel_id=1, source_target_pairs={{0,3},{1,0},{2,1},{3,2},{4,7},{5,4},{6,5},{7,6},{8,11},{9,8},{10,9... | collective-permute-start | bytes 1105928 | tf_op jit(solution)/shard_map/ppermute | solution.py:222
  (46 other events, 193.8 us)
Sparse Core Ops, SparseCore 0:
  12.0 138.0 all-gather.4
  236.7 84.5 reduce-scatter.2
  324.8 64.4 reduce-scatter.4
  407.7 36.4 all-gather.6

commit v3 on v2

v3 whole, which is shorter than its diff:
```python
import functools
import math

import jax
import jax.numpy as jnp
from jax import lax
from jax.experimental import pallas as pl
from jax.experimental.pallas import tpu as pltpu
from jax.sharding import PartitionSpec as P


HEAD_DIM = 64
PASSES = 5
LEN = 192
EPSILON = 1e-05
MASKED = -1e30
QUERY_TILE = 256
LANES = 128
F32 = jnp.float32
BF16 = jnp.bfloat16


def tiles_of(slots):
    return [(q0, min(q0 + QUERY_TILE, slots)) for q0 in range(0, slots, QUERY_TILE)]


def rows_in(slots):
    return [(r0, min(r0 + 240, slots)) for r0 in range(0, slots, 240)]


def dot_nt(a, b):
    return lax.dot_general(a, b, (((1,), (1,)), ((), ())), preferred_element_type=F32)


def dot_nn(a, b):
    return lax.dot_general(a, b, (((1,), (0,)), ((), ())), preferred_element_type=F32)


def dot_tn(a, b):
    return lax.dot_general(a, b, (((0,), (0,)), ((), ())), preferred_element_type=F32)


def half_lanes(values, half):
    lane = lax.broadcasted_iota(jnp.int32, (1, LANES), 1)
    return jnp.where((lane // HEAD_DIM) == half, values, jnp.zeros_like(values))


def diagonal_mask(q0, rows, live):
    key = lax.broadcasted_iota(jnp.int32, (rows, rows), 0)
    query = lax.broadcasted_iota(jnp.int32, (rows, rows), 1)
    return (key <= query) & (key + q0 < live)


def place_rows(block_ref, part, each, place):
    spread, groups = block_ref.shape[:2]
    for group in range(groups):
        for member in range(spread):
            rows = block_ref[member, group, part * each : (part + 1) * each, :]
            place((group * spread + member) * each, rows)


def attend_kernel(
    each, live_ref, n1_ref, w_ref, bias_ref, q_ref, k_ref, v_ref, o_ref, lse_ref, matrix_ref, vt_ref
):
    slots = n1_ref.shape[0]
    live = live_ref[0]
    pair = pl.program_id(0)

    @pl.when(pair == 0)
    def _():
        for part in range(3):

            def place(first, rows, part=part):
                done = 0
                while done < rows.shape[0]:
                    at = (first + done) % LANES
                    size = min(rows.shape[0] - done, LANES - at)
                    start = part * LANES + at
                    matrix_ref[(first + done) // LANES, start : start + size, :] = rows[done : done + size, :]
                    done += size

            place_rows(w_ref, part, each, place)

    projected = dot_nt(n1_ref[...], matrix_ref[pair])
    q_ref[...] = (projected[:, :LANES] + bias_ref[0, 0:1, :]).astype(BF16)
    k_ref[...] = projected[:, LANES : 2 * LANES].astype(BF16)
    values = projected[:, 2 * LANES :] + bias_ref[0, 1:2, :]
    v_ref[...] = values.astype(BF16)
    vt_ref[...] = values.T.astype(BF16)
    for q0, q1 in tiles_of(slots):
        rows = q1 - q0

        @pl.when(q0 >= live)
        def _():
            o_ref[q0:q1, :] = jnp.zeros((rows, LANES), BF16)
            lse_ref[0, :, q0:q1] = jnp.zeros((2, rows), F32)

        @pl.when(q0 < live)
        def _():
            query = q_ref[q0:q1, :] * jnp.asarray(1.0 / math.sqrt(HEAD_DIM), BF16)
            allowed = diagonal_mask(q0, rows, live)
            outs = []
            for half in range(2):
                one = half_lanes(query, half)
                last = dot_nt(k_ref[q0:q1, :], one)
                last = jnp.where(allowed, last, MASKED)
                peak = jnp.max(last, axis=0, keepdims=True)
                if q0:
                    early = dot_nt(k_ref[0:q0, :], one)
                    peak = jnp.maximum(peak, jnp.max(early, axis=0, keepdims=True))
                last = jnp.exp(last - peak)
                total = jnp.sum(last, axis=0, keepdims=True)
                lanes = slice(half * HEAD_DIM, (half + 1) * HEAD_DIM)
                if q0:
                    early = jnp.exp(early - peak)
                    total = total + jnp.sum(early, axis=0, keepdims=True)
                inverse = 1.0 / total
                out = dot_nn(vt_ref[lanes, q0:q1], (last * inverse).astype(BF16))
                if q0:
                    out = out + dot_nn(vt_ref[lanes, 0:q0], (early * inverse).astype(BF16))
                outs.append(out)
                lse_ref[0, half : half + 1, q0:q1] = peak + jnp.log(total)
            o_ref[q0:q1, :] = jnp.concatenate(outs, axis=0).T.astype(BF16)


def attend_back_kernel(
    each, live_ref, q_ref, k_ref, v_ref, o_ref, lse_ref, matrix_ref, mixed_ref, n1_ref, hid_ref, pass_ref,
    d_ref, xhat_ref, inv_ref, cot_ref, vec_ref, wo_ref,
    gblock_ref, gh_ref, sums_ref, gbias_ref,
    kt_ref, dk_sum, dv_sum, ga_s, gmix_s, gn1_s, dw_s, gproj_s,
):
    slots = q_ref.shape[0]
    width = n1_ref.shape[1]
    pairs = gmix_s.shape[0]
    spread, groups = gblock_ref.shape[:2]
    live = live_ref[0]
    pair = pl.program_id(0)
    scale = 1.0 / math.sqrt(HEAD_DIM)

    def add_rows(place, value):
        sums_ref[place : place + 1, :] += jnp.sum(value, axis=0, keepdims=True)

    @pl.when(pair == 0)
    def _():
        sums_ref[...] = jnp.zeros_like(sums_ref)
        for r0, r1 in rows_in(slots):
            grad_n2 = d_ref[r0:r1, :]
            xhat = xhat_ref[r0:r1, :]
            alive = lax.broadcasted_iota(jnp.int32, (r1 - r0, 1), 0) + r0 < live
            grad_y = jnp.where(alive, cot_ref[r0:r1, :].astype(F32), 0.0)
            grad_a = grad_y + norm_back(grad_n2, xhat, inv_ref[r0:r1, :], vec_ref[1:2, :])
            ga_s[r0:r1, :] = grad_a
            grad_att = grad_a.astype(BF16)
            gh_ref[r0:r1, :] = grad_att
            grad_mixed = dot_nt(grad_att, wo_ref[...]).astype(BF16)
            for number in range(pairs):
                gmix_s[number, r0:r1, :] = grad_mixed[:, number * LANES : (number + 1) * LANES]
            for place, value in enumerate((grad_n2 * xhat, grad_n2, grad_a, grad_y)):
                add_rows(2 + place, value)
        grad_out = dot_tn(mixed_ref[...], gh_ref[...]).astype(BF16)
        for group in range(groups):
            for member in range(spread):
                first = (group * spread + member) * each
                gblock_ref[member, group, 3 * each : 4 * each, :] = grad_out[first : first + each, :]
                gblock_ref[member, group, 4 * each :, :] = jnp.zeros(
                    (gblock_ref.shape[2] - 4 * each, width), BF16
                )
        gn1_s[...] = jnp.zeros_like(gn1_s)

    kt_ref[...] = k_ref[...].T
    dk_sum[...] = jnp.zeros_like(dk_sum)
    dv_sum[...] = jnp.zeros_like(dv_sum)
    for q0, q1 in tiles_of(slots):
        rows = q1 - q0

        @pl.when(q0 >= live)
        def _():
            gproj_s[q0:q1, :LANES] = jnp.zeros((rows, LANES), BF16)

        @pl.when(q0 < live)
        def _():
            query = q_ref[q0:q1, :] * jnp.asarray(scale, BF16)
            grad = gmix_s[pair, q0:q1, :]
            allowed = diagonal_mask(q0, rows, live)
            both = (grad.astype(F32) * o_ref[q0:q1, :].astype(F32)).T
            parts = []
            for half in range(2):
                lanes = slice(half * HEAD_DIM, (half + 1) * HEAD_DIM)
                one = half_lanes(query, half)
                grad_one = half_lanes(grad, half)
                lse = lse_ref[0, half : half + 1, q0:q1]
                inner = jnp.sum(both[lanes, :], axis=0, keepdims=True)
                turned = None
                for start, stop in ([(0, q0)] if q0 else []) + [(q0, q1)]:
                    scores = dot_nt(k_ref[start:stop, :], one)
                    probs = jnp.exp(scores - lse)
                    if start == q0:
                        probs = jnp.where(allowed, probs, 0.0)
                    grad_weights = dot_nt(v_ref[start:stop, :], grad_one)
                    grad_scores = (probs * (grad_weights - inner)).astype(BF16)
                    dk_sum[start:stop, :] += dot_nn(grad_scores, one)
                    dv_sum[start:stop, :] += dot_nn(probs.astype(BF16), grad_one)
                    piece = dot_nn(kt_ref[lanes, start:stop], grad_scores)
                    turned = piece if turned is None else turned + piece
                parts.append(turned)
            gproj_s[q0:q1, :LANES] = (jnp.concatenate(parts, axis=0).T * scale).astype(BF16)

    gproj_s[:, LANES : 2 * LANES] = dk_sum[...].astype(BF16)
    gproj_s[:, 2 * LANES :] = dv_sum[...].astype(BF16)
    grad_proj = gproj_s[...]
    dw_s[pair] = dot_tn(grad_proj, n1_ref[...]).astype(BF16)
    gn1_s[...] += dot_nn(grad_proj, matrix_ref[0])
    gbias_ref[0] = jnp.sum(grad_proj.astype(F32), axis=0, keepdims=True)

    @pl.when(pair == pairs - 1)
    def _():
        for r0, r1 in rows_in(slots):
            xhat, inverse = norm_parts(hid_ref[r0:r1, :])
            grad_n1 = gn1_s[r0:r1, :]
            grad_h = ga_s[r0:r1, :] + norm_back(grad_n1, xhat, inverse, vec_ref[4:5, :])
            gh_ref[r0:r1, :] = grad_h.astype(BF16)
            add_rows(0, grad_n1 * xhat)
            add_rows(1, grad_n1)
            passes = pass_ref[r0:r1, :]
            for number in range(PASSES):
                add_rows(6 + number, jnp.where(passes == number, grad_h, 0.0))
        for part in range(3):
            for group in range(groups):
                for member in range(spread):
                    first = (group * spread + member) * each
                    done = 0
                    while done < each:
                        at = (first + done) % LANES
                        size = min(each - done, LANES - at)
                        start = part * LANES + at
                        gblock_ref[member, group, part * each + done : part * each + done + size, :] = dw_s[
                            (first + done) // LANES, start : start + size, :
                        ]
                        done += size


def pair_spec(slots):
    return pl.BlockSpec((slots, LANES), lambda p, live: (0, p))


def attend(live, n1, blocks, biases, each):
    slots, width = n1.shape
    pairs = width // LANES
    spec = pair_spec(slots)
    lse_spec = pl.BlockSpec((1, 2, slots), lambda p, live: (p, 0, 0))
    flops = 2 * 2 * slots * slots * width + 2 * slots * width * 3 * width
    shape = jax.ShapeDtypeStruct((slots, width), BF16)
    return pl.pallas_call(
        functools.partial(attend_kernel, each),
        out_shape=(
            shape,
            shape,
            shape,
            shape,
            jax.ShapeDtypeStruct((pairs, 2, slots), F32),
            jax.ShapeDtypeStruct((pairs, 3 * LANES, width), BF16),
        ),
        grid_spec=pltpu.PrefetchScalarGridSpec(
            num_scalar_prefetch=1,
            grid=(pairs,),
            in_specs=[
                pl.BlockSpec((slots, width), lambda p, live: (0, 0), pipeline_mode=pl.Buffered(1)),
                pl.BlockSpec(blocks.shape, lambda p, live: (0, 0, 0, 0), pipeline_mode=pl.Buffered(1)),
                pl.BlockSpec((1, 2, LANES), lambda p, live: (p, 0, 0)),
            ],
            out_specs=(
                spec,
                spec,
                spec,
                spec,
                lse_spec,
                pl.BlockSpec((pairs, 3 * LANES, width), lambda p, live: (0, 0, 0), pipeline_mode=pl.Buffered(1)),
            ),
            scratch_shapes=[pltpu.VMEM((LANES, slots), BF16)],
        ),
        cost_estimate=pl.CostEstimate(
            flops=flops, transcendentals=slots * slots * width // HEAD_DIM, bytes_accessed=16 * slots * width
        ),
        name="attend",
    )(live, n1, blocks, biases)


def attend_back(
    live, query, keys, values, mixed, lse, matrix, n1, hidden, passes, grad_n2, xhat, inverse, cot, vectors, w_out,
    spread, groups, extra,
):
    slots, width = query.shape
    pairs = width // LANES
    each = width // (spread * groups)
    one = pl.Buffered(1)
    spec = pair_spec(slots)

    def whole(shape):
        return pl.BlockSpec(shape, lambda p, live: (0,) * len(shape), pipeline_mode=one)

    full = whole((slots, width))
    column = whole((slots, 1))
    flops = 5 * 2 * slots * slots * width + 2 * slots * width * 8 * width
    return pl.pallas_call(
        functools.partial(attend_back_kernel, each),
        out_shape=(
            jax.ShapeDtypeStruct((spread, groups, 4 * each + extra, width), BF16),
            jax.ShapeDtypeStruct((slots, width), BF16),
            jax.ShapeDtypeStruct((16, width), F32),
            jax.ShapeDtypeStruct((pairs, 1, 3 * LANES), F32),
        ),
        grid_spec=pltpu.PrefetchScalarGridSpec(
            num_scalar_prefetch=1,
            grid=(pairs,),
            in_specs=[
                spec,
                spec,
                spec,
                spec,
                pl.BlockSpec((1, 2, slots), lambda p, live: (p, 0, 0)),
                pl.BlockSpec((1, 3 * LANES, width), lambda p, live: (p, 0, 0)),
                full,
                full,
                full,
                column,
                full,
                full,
                column,
                full,
                whole((8, width)),
                whole((width, width)),
            ],
            out_specs=(
                whole((spread, groups, 4 * each + extra, width)),
                full,
                whole((16, width)),
                pl.BlockSpec((1, 1, 3 * LANES), lambda p, live: (p, 0, 0)),
            ),
            scratch_shapes=[
                pltpu.VMEM((LANES, slots), BF16),
                pltpu.VMEM((slots, LANES), F32),
                pltpu.VMEM((slots, LANES), F32),
                pltpu.VMEM((slots, width), F32),
                pltpu.VMEM((pairs, slots, LANES), BF16),
                pltpu.VMEM((slots, width), F32),
                pltpu.VMEM((pairs, 3 * LANES, width), BF16),
                pltpu.VMEM((slots, 3 * LANES), BF16),
            ],
        ),
        cost_estimate=pl.CostEstimate(
            flops=flops, transcendentals=slots * slots * width // HEAD_DIM, bytes_accessed=40 * slots * width
        ),
        name="attend_back",
    )(
        live, query, keys, values, mixed, lse, matrix, mixed, n1, hidden, passes, grad_n2, xhat, inverse, cot,
        vectors, w_out,
    )


def ring_pairs(size, shift):
    return [(source, (source + shift) % size) for source in range(size)]


def to_sequence(block, hold=None):
    size = lax.axis_size("tensor")
    me = lax.axis_index("tensor")
    rows, _, width = block.shape
    block = lax.optimization_barrier(block.transpose(1, 0, 2))
    pieces = []
    for shift in range(size):
        piece = lax.dynamic_index_in_dim(block, (me + shift) % size, 0, keepdims=False)
        pieces.append(lax.ppermute(piece, "tensor", ring_pairs(size, shift)) if shift else piece)
    if hold is not None:
        pieces, hold = lax.optimization_barrier((pieces, hold))
    out = jnp.zeros((size * rows, width), block.dtype)
    for shift, piece in enumerate(pieces):
        out = lax.dynamic_update_slice(out, piece, (((me - shift) % size) * rows, 0))
    return (out, hold) if hold is not None else out


def to_slots(values):
    size = lax.axis_size("tensor")
    me = lax.axis_index("tensor")
    slots, width = values.shape
    rows = slots // size
    out = jnp.zeros((slots, width), values.dtype)
    for shift in range(size):
        piece = lax.dynamic_slice(values, (((me + shift) % size) * rows, 0), (rows, width))
        if shift:
            piece = lax.ppermute(piece, "tensor", ring_pairs(size, shift))
        out = lax.dynamic_update_slice(out, piece, (((me - shift) % size) * rows, 0))
    return lax.optimization_barrier(out).reshape(size, rows, width).transpose(1, 0, 2)


def gather_tensor(piece):
    size = lax.axis_size("tensor")
    me = lax.axis_index("tensor")
    rows, width = piece.shape
    out = jnp.zeros((size * rows, width), piece.dtype)
    for shift in range(size):
        other = lax.ppermute(piece, "tensor", ring_pairs(size, shift)) if shift else piece
        out = lax.dynamic_update_slice(out, other, (((me - shift) % size) * rows, 0))
    return out.reshape(size, rows, width)


def gather_batch(piece):
    size = lax.axis_size("batch")
    if size != 8:
        return lax.all_gather(piece, "batch", axis=0, tiled=False)
    me = lax.axis_index("batch")
    rows, width = piece.shape
    out = jnp.zeros((size * rows, width), piece.dtype)
    for turn in range(size):
        other = lax.ppermute(piece, "batch", [(place, place ^ turn) for place in range(size)]) if turn else piece
        out = lax.dynamic_update_slice(out, other, ((me ^ turn) * rows, 0))
    return out.reshape(size, rows, width)


def share(rows):
    size = lax.axis_size("batch")
    each = rows.shape[0] // size
    return lax.dynamic_slice(rows, (lax.axis_index("batch") * each, 0), (each, rows.shape[1]))


def norm_parts(values):
    mean = jnp.mean(values, axis=-1, keepdims=True)
    center = values - mean
    spread = jnp.mean(center * center, axis=-1, keepdims=True)
    inverse = lax.rsqrt(spread + EPSILON)
    return center * inverse, inverse


def norm_back(grad, xhat, inverse, gain):
    scaled = grad * gain
    first = jnp.mean(scaled, axis=-1, keepdims=True)
    second = jnp.mean(scaled * xhat, axis=-1, keepdims=True)
    return inverse * (scaled - first - xhat * second)


def gelu_parts(values):
    outer = math.sqrt(2.0 / math.pi)
    inside = jnp.tanh(outer * (values + 0.044715 * values * values * values))
    act = 0.5 * values * (1.0 + inside)
    slope = 0.5 * (1.0 + inside) + 0.5 * values * (1.0 - inside * inside) * outer * (
        1.0 + 3.0 * 0.044715 * values * values
    )
    return act, slope


def mlp_kernel(
    live_ref, hid_ref, mix_ref, out_ref, cot_ref, vec_ref, bup_ref, up_ref, down_ref,
    y_ref, d_s, xhat_s, inv_s, wo_s, gblock_ref, gbup_ref,
    n2_s, y_s, gm_s,
):
    slots = hid_ref.shape[0]
    step = pl.program_id(0)
    live = live_ref[0]

    def live_rows(r0, r1):
        return lax.broadcasted_iota(jnp.int32, (r1 - r0, 1), 0) + r0 < live

    @pl.when(step == 0)
    def _():
        def place(first, rows):
            wo_s[first : first + rows.shape[0], :] = rows

        place_rows(out_ref, 0, out_ref.shape[2], place)
        for r0, r1 in rows_in(slots):
            after = hid_ref[r0:r1, :] + dot_nn(mix_ref[r0:r1, :], wo_s[...]) + vec_ref[0:1, :]
            xhat, inverse = norm_parts(after)
            xhat_s[r0:r1, :] = xhat
            inv_s[r0:r1, :] = inverse
            n2_s[r0:r1, :] = (xhat * vec_ref[1:2, :] + vec_ref[2:3, :]).astype(BF16)
            y_s[r0:r1, :] = after + vec_ref[3:4, :]
            cot = cot_ref[r0:r1, :]
            gm_s[r0:r1, :] = jnp.where(live_rows(r0, r1), cot, jnp.zeros_like(cot))
            d_s[r0:r1, :] = jnp.zeros((r1 - r0, d_s.shape[1]), F32)

    _, count, units, width = up_ref.shape
    up = up_ref[...].reshape(count * units, width)
    down = down_ref[...].reshape(count * units, width)
    n2 = n2_s[...]
    grad_m = gm_s[...]
    act, slope = gelu_parts(dot_nt(n2, up) + bup_ref[...])
    act = act.astype(BF16)
    grad_u = (dot_nt(grad_m, down) * slope).astype(BF16)
    y_s[...] += dot_nn(act, down)
    d_s[...] += dot_nn(grad_u, up)
    gblock_ref[0, :, 0:units, :] = dot_tn(grad_u, n2).reshape(count, units, width).astype(BF16)
    gblock_ref[0, :, units : 2 * units, :] = dot_tn(act, grad_m).reshape(count, units, width).astype(BF16)
    gbup_ref[...] = jnp.sum(grad_u.astype(F32), axis=0, keepdims=True)

    @pl.when(step == pl.num_programs(0) - 1)
    def _():
        for r0, r1 in rows_in(slots):
            y_ref[r0:r1, :] = jnp.where(live_rows(r0, r1), y_s[r0:r1, :], 0.0).astype(BF16)


def mlp(live, hidden, mixed, cot, vectors, bias_up, blocks, each):
    slots, width = hidden.shape
    steps, groups = blocks.shape[:2]
    units = 4 * each
    chunk = groups * units
    one = pl.Buffered(1)

    def whole(shape):
        return pl.BlockSpec(shape, lambda c, live: (0,) * len(shape), pipeline_mode=one)

    full = whole((slots, width))
    flops = 2 * slots * width * (6 * chunk * steps + 3 * width)
    return pl.pallas_call(
        mlp_kernel,
        out_shape=(
            jax.ShapeDtypeStruct((slots, width), BF16),
            jax.ShapeDtypeStruct((slots, width), F32),
            jax.ShapeDtypeStruct((slots, width), F32),
            jax.ShapeDtypeStruct((slots, 1), F32),
            jax.ShapeDtypeStruct((width, width), BF16),
            jax.ShapeDtypeStruct((steps, groups, 2 * units, width), BF16),
            jax.ShapeDtypeStruct((1, steps * chunk), F32),
        ),
        grid_spec=pltpu.PrefetchScalarGridSpec(
            num_scalar_prefetch=1,
            grid=(steps,),
            in_specs=[
                full,
                full,
                pl.BlockSpec((steps, groups, each, width), lambda c, live: (0, 0, 8, 0), pipeline_mode=one),
                full,
                whole((8, width)),
                pl.BlockSpec((1, chunk), lambda c, live: (0, c)),
                pl.BlockSpec((1, groups, units, width), lambda c, live: (c, 0, 0, 0)),
                pl.BlockSpec((1, groups, units, width), lambda c, live: (c, 0, 1, 0)),
            ],
            out_specs=(
                full,
                full,
                full,
                whole((slots, 1)),
                whole((width, width)),
                pl.BlockSpec((1, groups, 2 * units, width), lambda c, live: (c, 0, 0, 0)),
                pl.BlockSpec((1, chunk), lambda c, live: (0, c)),
            ),
            scratch_shapes=[
                pltpu.VMEM((slots, width), BF16),
                pltpu.VMEM((slots, width), F32),
                pltpu.VMEM((slots, width), BF16),
            ],
        ),
        cost_estimate=pl.CostEstimate(
            flops=flops, transcendentals=slots * steps * chunk, bytes_accessed=20 * slots * width + 8 * steps * chunk * width
        ),
        name="mlp",
    )(live, hidden, mixed, blocks, cot, vectors, bias_up, blocks, blocks)


def layer(
    slot_states,
    pass_counts,
    w_qkv,
    q_bias,
    v_bias,
    w_out,
    out_bias,
    w_up,
    up_bias,
    w_down,
    down_bias,
    ln1_gain,
    ln1_bias,
    ln2_gain,
    ln2_bias,
    pass_table,
    cotangent,
):
    groups = lax.axis_size("tensor")
    spread = lax.axis_size("batch")
    me = lax.axis_index("tensor")
    rows, seqs, width = slot_states.shape
    slots = rows * groups
    hidden_here = w_up.shape[1]
    hidden_units = hidden_here * groups
    assert seqs == groups

    gain_one, shift_one = ln1_gain.astype(F32), ln1_bias.astype(F32)
    gain_two, shift_two = ln2_gain.astype(F32), ln2_bias.astype(F32)
    table = pass_table.astype(F32)

    each = width // (groups * spread)
    units = hidden_here // spread
    here = q_bias.shape[0]
    biases = jnp.concatenate([q_bias, v_bias, jnp.zeros((width - 2 * here,), BF16)]).reshape(1, width)
    qkv_rows = w_qkv.transpose(1, 2, 0)
    qkv_piece = jnp.concatenate(
        [share(qkv_rows[part]) for part in range(3)] + [jnp.pad(biases, ((0, 7), (0, 0)))], axis=0
    )
    qkv_blocks = lax.all_gather(gather_tensor(qkv_piece), "batch", axis=0, tiled=False)
    bias_row = jnp.pad(up_bias.reshape(1, width), ((0, 7), (0, 0)))
    mlp_piece = jnp.concatenate([share(w_up.T), share(w_down), share(w_out), bias_row], axis=0)
    mlp_blocks = lax.all_gather(gather_tensor(mlp_piece), "batch", axis=0, tiled=False)
    states = to_sequence(slot_states).astype(F32)

    bias_rows = qkv_blocks[0, :, 3 * each].astype(F32)
    bias_pairs = jnp.stack(
        [bias_rows[:, part * here : (part + 1) * here].reshape(width // LANES, LANES) for part in range(2)], axis=1
    )
    bias_up = mlp_blocks[0, :, 2 * units + each].reshape(groups, spread, units)

    fold = spread if units % 32 == 0 else 8
    if fold != spread:

        def regrouped(values, first, rows):
            rows_of = values[:, :, first : first + rows].transpose(1, 0, 2, 3)
            return rows_of.reshape(groups, fold, -1, width).transpose(1, 0, 2, 3)

        qkv_blocks = jnp.concatenate([regrouped(qkv_blocks, part * each, each) for part in range(3)], axis=2)
        mlp_blocks = jnp.concatenate(
            [
                regrouped(mlp_blocks, 0, units),
                regrouped(mlp_blocks, units, units),
                regrouped(mlp_blocks, 2 * units, each),
            ],
            axis=2,
        )
        bias_up = bias_up.reshape(groups, fold, -1)
    bias_up = bias_up.transpose(1, 0, 2).reshape(1, hidden_units).astype(F32)

    count = lax.dynamic_index_in_dim(pass_counts, me, 0, keepdims=False)
    index = jnp.arange(slots, dtype=jnp.int32)
    passes = (index % count)[:, None]
    live_count = count * LEN
    live_arg = live_count.reshape(1).astype(jnp.int32)
    added = jnp.zeros((slots, width), F32)
    for number in range(PASSES):
        added = jnp.where(passes == number, table[number][None, :], added)
    hidden = states + added

    xhat_one, _ = norm_parts(hidden)
    n1 = (xhat_one * gain_one + shift_one).astype(BF16)
    n1, hidden, passes, cotangent = lax.optimization_barrier((n1, hidden, passes, cotangent))
    fold_each = width // (groups * fold)
    query, keys, values, mixed, lse, matrix = attend(live_arg, n1, qkv_blocks, bias_pairs, fold_each)
    cot, mixed = to_sequence(cotangent, mixed)
    vectors = jnp.stack([out_bias.astype(F32), gain_two, shift_two, down_bias.astype(F32), gain_one])
    vectors = jnp.pad(vectors, ((0, 3), (0, 0)))
    layer_out, grad_n2, xhat_two, inverse_two, matrix_out, mlp_block, grad_bias_up = mlp(
        live_arg, hidden, mixed, cot, vectors, bias_up, mlp_blocks, fold_each
    )
    if fold != spread:
        mlp_block = mlp_block.reshape(fold, groups, 2, -1, width).transpose(1, 2, 0, 3, 4)
        mlp_block = mlp_block.reshape(groups, 2, spread, units, width).transpose(2, 0, 1, 3, 4)
        mlp_block = mlp_block.reshape(spread, groups, 2 * units, width)
    layer_part = to_slots(layer_out)
    extra = 16
    attn_block, grad_h, sums, grad_bias = attend_back(
        live_arg, query, keys, values, mixed, lse, matrix, n1, hidden, passes, grad_n2, xhat_two, inverse_two, cot,
        vectors, matrix_out, fold, groups, extra,
    )
    grad_part = to_slots(grad_h)

    grad_bias_up = grad_bias_up.reshape(fold, groups, -1).transpose(1, 0, 2).reshape(groups, 1, hidden_here)
    lead = 6 + PASSES
    own = jnp.concatenate(
        [
            grad_bias[:, 0, :LANES].reshape(groups, 1, here),
            grad_bias[:, 0, 2 * LANES :].reshape(groups, 1, here),
            jnp.zeros((groups, 1, width - 2 * here), F32),
        ],
        axis=2,
    )
    small = jnp.concatenate(
        [jnp.broadcast_to(sums[None, :lead], (groups, lead, width)), own, grad_bias_up], axis=1
    )
    small = jnp.pad(small, ((0, 0), (0, spread * extra - lead - 2), (0, 0)))
    small = small.reshape(groups, spread, extra, width).transpose(1, 0, 2, 3).astype(BF16)
    if fold != spread:
        attn_block = attn_block[:, :, : 4 * fold_each].reshape(fold, groups, 4, fold_each, width)
        attn_block = attn_block.transpose(1, 2, 0, 3, 4).reshape(groups, 4, spread, each, width)
        attn_block = attn_block.transpose(2, 0, 1, 3, 4).reshape(spread, groups, 4 * each, width)
        attn_block = jnp.pad(attn_block, ((0, 0), (0, 0), (0, extra), (0, 0)))
    attn_block = lax.dynamic_update_slice(attn_block, small, (0, 0, 4 * each, 0))

    def over_tensor(value):
        kept = lax.dynamic_index_in_dim(value, me, 0, keepdims=False).astype(F32)
        for shift in range(1, groups):
            piece = lax.dynamic_index_in_dim(value, (me + shift) % groups, 0, keepdims=False)
            kept = kept + lax.ppermute(piece, "tensor", ring_pairs(groups, shift)).astype(F32)
        return kept.astype(BF16)

    mlp_block = lax.psum_scatter(mlp_block, "batch", scatter_dimension=0, tiled=True)[0]
    attn_block, mlp_block = lax.optimization_barrier((attn_block, mlp_block))
    attn_block = lax.psum_scatter(attn_block, "batch", scatter_dimension=0, tiled=True)[0]
    mlp_piece = over_tensor(mlp_block)
    attn_piece = over_tensor(attn_block)
    mlp_whole = lax.all_gather(mlp_piece, "batch", axis=0, tiled=False)
    attn_whole = gather_batch(attn_piece)
    parts = [attn_whole[:, part * each : (part + 1) * each].reshape(here, width).astype(F32) for part in range(4)]
    small = attn_whole[:, 4 * each :].reshape(spread * extra, width).astype(F32)
    out_up = mlp_whole[:, :units].reshape(hidden_here, width).astype(F32).T
    out_down = mlp_whole[:, units:].reshape(hidden_here, width).astype(F32)
    out_qkv = jnp.stack(parts[:3], axis=0).transpose(2, 0, 1)
    return (
        layer_part,
        grad_part,
        out_qkv,
        small[lead, :here],
        small[lead, here : 2 * here],
        parts[3],
        small[4],
        out_up,
        small[lead + 1],
        out_down,
        small[5],
        small[0],
        small[1],
        small[2],
        small[3],
        small[6:lead],
    )


def solution(mesh):
    in_specs = (
        P("tensor", "batch", None),
        P("batch"),
        P(None, None, "tensor"),
        P("tensor"),
        P("tensor"),
        P("tensor", None),
        P(),
        P(None, "tensor"),
        P("tensor"),
        P("tensor", None),
        P(),
        P(),
        P(),
        P(),
        P(),
        P(),
        P("tensor", "batch", None),
    )
    out_specs = (
        P("tensor", "batch", None),
        P("tensor", "batch", None),
        P(None, None, "tensor"),
        P("tensor"),
        P("tensor"),
        P("tensor", None),
        P(),
        P(None, "tensor"),
        P("tensor"),
        P("tensor", None),
        P(),
        P(),
        P(),
        P(),
        P(),
        P(),
    )
    return jax.shard_map(layer, mesh=mesh, in_specs=in_specs, out_specs=out_specs, check_vma=False)
```

time: 468 us -> 463 us (0.989)
  the two profiles are of different devices: /device:TPU:0 before, /device:TPU:9 now
where the time goes in v3:
time: 463 us; the launch traced here: 454 us
  waiting for transfers between devices  223 us (48%)
  Pallas kernels  110 us (24%)
  local copies, waits for them, and re-layouts  49.5 us (11%)
  starting transfers between devices  31.7 us (7%)
  other arithmetic  22.7 us (5%)
  between operations  16.8 us (4%)
    ppermute x6, waiting for transfers between devices, to_slots(): piece = lax.ppermute(piece, 'tensor', ring_pairs(size, shift))  52 us
    pallas_call x1, Pallas kernels, mlp(): pl.pallas_call(mlp_kernel, out_shape=(jax.ShapeDtypeStruct((slots, width)...  47.4 us
    reduce_scatter x1, waiting for transfers between devices, layer(): lax.psum_scatter(mlp_block, 'batch', scatter_dimension=0, tiled=True)[0]  44.4 us
    pallas_call x1, Pallas kernels, attend_back(): pl.pallas_call(functools.partial(attend_back_kernel, each), out_shape=(ja...  40.3 us
    ppermute x6, waiting for transfers between devices, gather_tensor(): lax.ppermute(piece, 'tensor', ring_pairs(size, shift))  38.7 us
    ppermute x6, waiting for transfers between devices, over_tensor(): lax.ppermute(piece, 'tensor', ring_pairs(groups, shift)).astype(F32)  38.4 us
    ppermute x6, waiting for transfers between devices, to_sequence(): lax.ppermute(piece, 'tensor', ring_pairs(size, shift))  24.1 us
    pallas_call x1, Pallas kernels, attend(): pl.pallas_call(functools.partial(attend_kernel, each), out_shape=(shape,...  22.7 us
  transfers between devices with their start and end apart: 36, of which 25 were waited for; matrix products, arithmetic and copies ran while one was open for 11% of the time, Pallas kernels for 14%

profile of v3, /device:TPU:9, one launch (start us, length us, event | category | flops | bytes accessed | tf_op | source)
XLA Modules:
  0.0 454.3 jit_solution(3044077730564623508)
XLA Ops:
  13.1 7.0 %collective-permute-done.7 = bf16[80,768]{1,0:T(8,128)(2,1)S(1)} collective-permute-done((bf16[80,768]{1,0:T(8,128)(2,1)S(1)}, bf16[80,768]{1,0:T(8,128)(2,1)S(1)}, u32[]{:S(2)}, u32[]{:S(2)}) %collective-permute-start.7) | collective-permute-done | bytes 122912 | tf_op jit(solution)/shard_map/ppermute | solution.py:401
  27.8 7.4 %collective-permute-done.9 = bf16[224,768]{1,0:T(8,128)(2,1)S(1)} collective-permute-done((bf16[224,768]{1,0:T(8,128)(2,1)S(1)}, bf16[224,768]{1,0:T(8,128)(2,1)S(1)}, u32[]{:S(2)}, u32[]{:S(2)}) %collective-permute-start.9) | collective-permute-done | bytes 344096 | tf_op jit(solution)/shard_map/ppermute | solution.py:401
  35.2 20.1 %collective-permute-done.10 = bf16[224,768]{1,0:T(8,128)(2,1)} collective-permute-done((bf16[224,768]{1,0:T(8,128)(2,1)S(1)}, bf16[224,768]{1,0:T(8,128)(2,1)}, u32[]{:S(2)}, u32[]{:S(2)}) %collective-permute-start.10) | collective-permute-done | bytes 344096 | tf_op jit(solution)/shard_map/ppermute | solution.py:401
  69.5 5.4 %add_select_fusion.pass_ref = s32[960,1]{1,0:T(8,128)} fusion(s32[]{:T(128)S(6)} %select_n.300, pred[]{:T(512)S(6)} %lt.284), kind=kLoop, calls=%fused_computation.11 | loop fusion | flops 6720 | bytes 3845 | tf_op jit(solution)/shard_map/jit(remainder)/select_n | solution.py:630
  76.6 14.9 %collective-permute-done.1 = bf16[240,768]{1,0:T(8,128)(2,1)S(1)} collective-permute-done((bf16[240,768]{1,0:T(8,128)(2,1)S(1)}, bf16[240,768]{1,0:T(8,128)(2,1)S(1)}, u32[]{:S(2)}, u32[]{:S(2)}) %collective-permute-start.1) | collective-permute-done | bytes 368672 | tf_op jit(solution)/shard_map/ppermute | solution.py:372
  106.4 22.7 %attend.1 = (bf16[960,768]{1,0:T(8,128)(2,1)}, bf16[960,768]{1,0:T(8,128)(2,1)}, bf16[960,768]{1,0:T(8,128)(2,1)}, bf16[960,768]{1,0:T(8,128)(2,1)}, f32[6,2,960]{2,1,0:T(2,128)}, /*index=5*/bf16[6,384,768]{2,1,0:T(8,128)(2,1)}) custom-call(s32[1]{0:T(128)} %bitcast.1.live_ref, bf16[960,768]{1,0:T(8,128)(2,1)} %add_convert_fusion.n1_ref, ...), custom_call_target="tpu_custom_call" | custom-call | flops 6228541440 | bytes 11796480 | tf_op jit(solution)/shard_map/attend/pallas_call | solution.py:253
  129.1 4.3 collective-permute-done.4
  137.6 47.4 %mlp.1 = (bf16[960,768]{1,0:T(8,128)(2,1)}, f32[960,768]{1,0:T(8,128)}, f32[960,768]{1,0:T(8,128)}, f32[960,1]{1,0:T(8,128)}, bf16[768,768]{1,0:T(8,128)(2,1)}, ...) custom-call(s32[1]{0:T(128)} %bitcast.1.live_ref, f32[960,768]{1,0:T(8,128)} %copy-done.2, ...), custom_call_target="tpu_custom_call" | custom-call | flops 30576476160 | bytes 33619968 | tf_op jit(solution)/shard_map/mlp/pallas_call | solution.py:511
  185.1 40.3 %attend_back.1 = (bf16[8,4,112,768]{3,2,1,0:T(8,128)(2,1)}, bf16[960,768]{1,0:T(8,128)(2,1)}, f32[16,768]{1,0:T(8,128)}, f32[6,1,384]{2,1,0:T(1,128)}) custom-call(s32[1]{0:T(128)} %bitcast.1.live_ref, bf16[960,768]{1,0:T(8,128)(2,1)} %get-tuple-element.54.q_ref, bf16[960,768]{1,0:T(8,128)(2,1)} %get-tuple-element.55.k_ref, ...), custom_call_target="tpu_custom_call" | custom-call | flops 16137584640 | bytes 29491200 | tf_op jit(solution)/shard_map/attend_back/pallas_call | solution.py:304
  228.5 44.4 %reduce-scatter.3.cloned.1.call-done = bf16[1,4,192,768]{3,2,1,0:T(8,128)(2,1)} async-done(((bf16[8,4,192,768]{3,2,1,0:T(8,128)(2,1)}), bf16[1,4,192,768]{3,2,1,0:T(8,128)(2,1)}) %reduce-scatter.3.cloned.1.call-update) | async-done | bytes 1179664 | tf_op jit(solution)/shard_map/reduce_scatter | solution.py:690
  277.7 4.1 collective-permute-done.28
  281.9 18.0 %collective-permute-done.29 = bf16[192,768]{1,0:T(8,128)(2,1)S(1)} collective-permute-done((bf16[192,768]{1,0:T(8,128)(2,1)S(1)}, bf16[192,768]{1,0:T(8,128)(2,1)S(1)}, u32[]{:S(2)}, u32[]{:S(2)}) %collective-permute-start.29) | collective-permute-done | bytes 294944 | tf_op jit(solution)/shard_map/ppermute | solution.py:687
  299.8 3.1 collective-permute-done.30
  311.5 3.0 collective-permute-start.13
  314.5 3.2 collective-permute-done.15
  318.8 20.8 %collective-permute-done.16 = bf16[240,768]{1,0:T(8,128)(2,1)} collective-permute-done((bf16[240,768]{1,0:T(8,128)(2,1)}, bf16[240,768]{1,0:T(8,128)(2,1)}, u32[]{:S(2)}, u32[]{:S(2)}) %collective-permute-start.16) | collective-permute-done | bytes 368672 | tf_op jit(solution)/shard_map/ppermute | solution.py:390
  340.5 16.2 %collective-permute-done.17 = bf16[240,768]{1,0:T(8,128)(2,1)} collective-permute-done((bf16[240,768]{1,0:T(8,128)(2,1)}, bf16[240,768]{1,0:T(8,128)(2,1)}, u32[]{:S(2)}, u32[]{:S(2)}) %collective-permute-start.17) | collective-permute-done | bytes 368672 | tf_op jit(solution)/shard_map/ppermute | solution.py:390
  359.6 3.6 collective-permute-done.12
  364.2 6.9 %collective-permute-done.13 = bf16[240,768]{1,0:T(8,128)(2,1)S(1)} collective-permute-done((bf16[240,768]{1,0:T(8,128)(2,1)}, bf16[240,768]{1,0:T(8,128)(2,1)S(1)}, u32[]{:S(2)}, u32[]{:S(2)}) %collective-permute-start.13) | collective-permute-done | bytes 368672 | tf_op jit(solution)/shard_map/ppermute | solution.py:390
  374.4 2.8 fusion.26
  377.2 16.5 %reduce-scatter.5.cloned.1.call-done = bf16[1,4,112,768]{3,2,1,0:T(8,128)(2,1)} async-done(((bf16[8,4,112,768]{3,2,1,0:T(8,128)(2,1)}), bf16[1,4,112,768]{3,2,1,0:T(8,128)(2,1)}) %reduce-scatter.5.cloned.1.call-update) | async-done | bytes 688144 | tf_op jit(solution)/shard_map/reduce_scatter | solution.py:692
  399.9 10.1 %collective-permute-done.19 = bf16[112,768]{1,0:T(8,128)(2,1)S(1)} collective-permute-done((bf16[112,768]{1,0:T(8,128)(2,1)S(1)}, bf16[112,768]{1,0:T(8,128)(2,1)S(1)}, u32[]{:S(2)}, u32[]{:S(2)}) %collective-permute-start.19) | collective-permute-done | bytes 172064 | tf_op jit(solution)/shard_map/ppermute | solution.py:687
  410.0 3.1 collective-permute-done.20
  430.7 8.4 %collective-permute-done.25 = bf16[112,768]{1,0:T(8,128)(2,1)S(1)} collective-permute-done((bf16[112,768]{1,0:T(8,128)(2,1)}, bf16[112,768]{1,0:T(8,128)(2,1)S(1)}, u32[]{:S(2)}, u32[]{:S(2)}) %collective-permute-start.25) | collective-permute-done | bytes 172064 | tf_op jit(solution)/shard_map/ppermute | solution.py:414
  (217 shorter events, 103.9 us)
Async XLA Ops:
  7.2 97.5 %all-gather.5.cloned.1.call-start = ((), (), s32[]{:S(2)}) async-start(), calls=%async_computation.2 | async-start | bytes 4423680 | tf_op jit(solution)/shard_map/all_gather | solution.py:597
  23.7 112.2 %all-gather.7.cloned.1.call-start = ((), (), s32[]{:S(2)}) async-start(), calls=%async_computation.3 | async-start | bytes 12386304 | tf_op jit(solution)/shard_map/all_gather | solution.py:600
  26.0 29.3 %collective-permute-start.10 = (bf16[224,768]{1,0:T(8,128)(2,1)S(1)}, bf16[224,768]{1,0:T(8,128)(2,1)}, u32[]{:S(2)}, u32[]{:S(2)}) collective-permute-start(bf16[224,768]{1,0:T(8,128)(2,1)S(1)} %get-tuple-element.154), channel_id=1, source_target_pairs={{0,2},{1,3},{2,0},{3,1},{4,6},{5,7},{6,4},{7,5},{8,10},{9,11},{10,... | collective-permute-start | bytes 1032200 | tf_op jit(solution)/shard_map/ppermute | solution.py:401
  26.6 30.8 %collective-permute-start.11 = (bf16[224,768]{1,0:T(8,128)(2,1)S(1)}, bf16[224,768]{1,0:T(8,128)(2,1)}, u32[]{:S(2)}, u32[]{:S(2)}) collective-permute-start(bf16[224,768]{1,0:T(8,128)(2,1)S(1)} %get-tuple-element.154), channel_id=1, source_target_pairs={{0,3},{1,0},{2,1},{3,2},{4,7},{5,4},{6,5},{7,6},{8,11},{9,8},{10,9... | collective-permute-start | bytes 1032200 | tf_op jit(solution)/shard_map/ppermute | solution.py:401
  59.5 213.4 %reduce-scatter.3.cloned.1.call-start = ((), (), s32[]{:S(2)}) async-start(), calls=%async_computation.4 | async-start | bytes 10616832 | tf_op jit(solution)/shard_map/reduce_scatter | solution.py:690
  60.0 14.9 %collective-permute-start = (bf16[240,768]{1,0:T(8,128)(2,1)S(1)}, bf16[240,768]{1,0:T(8,128)(2,1)}, u32[]{:S(2)}, u32[]{:S(2)}) collective-permute-start(bf16[240,768]{1,0:T(8,128)(2,1)S(1)} %get-tuple-element.138), channel_id=1, source_target_pairs={{0,1},{1,2},{2,3},{3,0},{4,5},{5,6},{6,7},{7,4},{8,9},{9,10},{10,1... | collective-permute-start | bytes 1105928 | tf_op jit(solution)/shard_map/ppermute | solution.py:372
  60.1 31.4 %collective-permute-start.1 = (bf16[240,768]{1,0:T(8,128)(2,1)S(1)}, bf16[240,768]{1,0:T(8,128)(2,1)S(1)}, u32[]{:S(2)}, u32[]{:S(2)}) collective-permute-start(bf16[240,768]{1,0:T(8,128)(2,1)S(1)} %get-tuple-element.137), channel_id=1, source_target_pairs={{0,2},{1,3},{2,0},{3,1},{4,6},{5,7},{6,4},{7,5},{8,10},{9,11},{10,... | collective-permute-start | bytes 1105928 | tf_op jit(solution)/shard_map/ppermute | solution.py:372
  62.3 32.7 %collective-permute-start.2 = (bf16[240,768]{1,0:T(8,128)(2,1)S(1)}, bf16[240,768]{1,0:T(8,128)(2,1)S(1)}, u32[]{:S(2)}, u32[]{:S(2)}) collective-permute-start(bf16[240,768]{1,0:T(8,128)(2,1)S(1)} %get-tuple-element.136), channel_id=1, source_target_pairs={{0,3},{1,0},{2,1},{3,2},{4,7},{5,4},{6,5},{7,6},{8,11},{9,8},{10,9... | collective-permute-start | bytes 1105928 | tf_op jit(solution)/shard_map/ppermute | solution.py:372
  101.9 27.2 %collective-permute-start.3 = (bf16[240,768]{1,0:T(8,128)(2,1)S(1)}, bf16[240,768]{1,0:T(8,128)(2,1)S(1)}, u32[]{:S(2)}, u32[]{:S(2)}) collective-permute-start(bf16[240,768]{1,0:T(8,128)(2,1)S(1)} %get-tuple-element.134), channel_id=1, source_target_pairs={{0,1},{1,2},{2,3},{3,0},{4,5},{5,6},{6,7},{7,4},{8,9},{9,10},{10,1... | collective-permute-start | bytes 1105928 | tf_op jit(solution)/shard_map/ppermute | solution.py:372
  102.0 31.4 %collective-permute-start.4 = (bf16[240,768]{1,0:T(8,128)(2,1)S(1)}, bf16[240,768]{1,0:T(8,128)(2,1)S(1)}, u32[]{:S(2)}, u32[]{:S(2)}) collective-permute-start(bf16[240,768]{1,0:T(8,128)(2,1)S(1)} %get-tuple-element.133), channel_id=1, source_target_pairs={{0,2},{1,3},{2,0},{3,1},{4,6},{5,7},{6,4},{7,5},{8,10},{9,11},{10,... | collective-permute-start | bytes 1105928 | tf_op jit(solution)/shard_map/ppermute | solution.py:372
  102.9 32.7 %collective-permute-start.5 = (bf16[240,768]{1,0:T(8,128)(2,1)S(1)}, bf16[240,768]{1,0:T(8,128)(2,1)S(1)}, u32[]{:S(2)}, u32[]{:S(2)}) collective-permute-start(bf16[240,768]{1,0:T(8,128)(2,1)S(1)} %get-tuple-element.132), channel_id=1, source_target_pairs={{0,3},{1,0},{2,1},{3,2},{4,7},{5,4},{6,5},{7,6},{8,11},{9,8},{10,9... | collective-permute-start | bytes 1105928 | tf_op jit(solution)/shard_map/ppermute | solution.py:372
  185.0 189.4 %all-gather.9.cloned.1.call-start = ((), (), s32[]{:S(2)}) async-start(), calls=%async_computation.6 | async-start | bytes 2654208 | tf_op jit(solution)/shard_map/all_gather | solution.py:695
  275.4 24.5 %collective-permute-start.29 = (bf16[192,768]{1,0:T(8,128)(2,1)S(1)}, bf16[192,768]{1,0:T(8,128)(2,1)S(1)}, u32[]{:S(2)}, u32[]{:S(2)}) collective-permute-start(bf16[192,768]{1,0:T(8,128)(2,1)S(1)} %get-tuple-element.145), channel_id=1, source_target_pairs={{0,2},{1,3},{2,0},{3,1},{4,6},{5,7},{6,4},{7,5},{8,10},{9,11},{10,... | collective-permute-start | bytes 884744 | tf_op jit(solution)/shard_map/ppermute | solution.py:687
  276.5 26.5 %collective-permute-start.30 = (bf16[192,768]{1,0:T(8,128)(2,1)S(1)}, bf16[192,768]{1,0:T(8,128)(2,1)S(1)}, u32[]{:S(2)}, u32[]{:S(2)}) collective-permute-start(bf16[192,768]{1,0:T(8,128)(2,1)S(1)} %get-tuple-element.144), channel_id=1, source_target_pairs={{0,3},{1,0},{2,1},{3,2},{4,7},{5,4},{6,5},{7,6},{8,11},{9,8},{10,9... | collective-permute-start | bytes 884744 | tf_op jit(solution)/shard_map/ppermute | solution.py:687
  304.8 88.9 %reduce-scatter.5.cloned.1.call-start = ((), (), s32[]{:S(2)}) async-start(), calls=%async_computation.5 | async-start | bytes 6193152 | tf_op jit(solution)/shard_map/reduce_scatter | solution.py:692
  307.8 31.7 %collective-permute-start.16 = (bf16[240,768]{1,0:T(8,128)(2,1)}, bf16[240,768]{1,0:T(8,128)(2,1)}, u32[]{:S(2)}, u32[]{:S(2)}) collective-permute-start(bf16[240,768]{1,0:T(8,128)(2,1)} %get-tuple-element.125), channel_id=1, source_target_pairs={{0,2},{1,3},{2,0},{3,1},{4,6},{5,7},{6,4},{7,5},{8,10},{9,11},{10,... | collective-permute-start | bytes 1105928 | tf_op jit(solution)/shard_map/ppermute | solution.py:390
  307.8 48.9 %collective-permute-start.17 = (bf16[240,768]{1,0:T(8,128)(2,1)}, bf16[240,768]{1,0:T(8,128)(2,1)}, u32[]{:S(2)}, u32[]{:S(2)}) collective-permute-start(bf16[240,768]{1,0:T(8,128)(2,1)} %get-tuple-element.124), channel_id=1, source_target_pairs={{0,3},{1,0},{2,1},{3,2},{4,7},{5,4},{6,5},{7,6},{8,11},{9,8},{10,9... | collective-permute-start | bytes 1105928 | tf_op jit(solution)/shard_map/ppermute | solution.py:390
  310.3 52.9 %collective-permute-start.12 = (bf16[240,768]{1,0:T(8,128)(2,1)}, bf16[240,768]{1,0:T(8,128)(2,1)}, u32[]{:S(2)}, u32[]{:S(2)}) collective-permute-start(bf16[240,768]{1,0:T(8,128)(2,1)} %get-tuple-element.130), channel_id=1, source_target_pairs={{0,1},{1,2},{2,3},{3,0},{4,5},{5,6},{6,7},{7,4},{8,9},{9,10},{10,1... | collective-permute-start | bytes 1105928 | tf_op jit(solution)/shard_map/ppermute | solution.py:390
  311.5 59.6 %collective-permute-start.13 = (bf16[240,768]{1,0:T(8,128)(2,1)}, bf16[240,768]{1,0:T(8,128)(2,1)S(1)}, u32[]{:S(2)}, u32[]{:S(2)}) collective-permute-start(bf16[240,768]{1,0:T(8,128)(2,1)} %get-tuple-element.129), channel_id=1, source_target_pairs={{0,2},{1,3},{2,0},{3,1},{4,6},{5,7},{6,4},{7,5},{8,10},{9,11},{10,... | collective-permute-start | bytes 1105928 | tf_op jit(solution)/shard_map/ppermute | solution.py:390
  317.7 54.8 %collective-permute-start.14 = (bf16[240,768]{1,0:T(8,128)(2,1)S(1)}, bf16[240,768]{1,0:T(8,128)(2,1)S(1)}, u32[]{:S(2)}, u32[]{:S(2)}) collective-permute-start(bf16[240,768]{1,0:T(8,128)(2,1)S(1)} %get-tuple-element.128), channel_id=1, source_target_pairs={{0,3},{1,0},{2,1},{3,2},{4,7},{5,4},{6,5},{7,6},{8,11},{9,8},{10,9... | collective-permute-start | bytes 1105928 | tf_op jit(solution)/shard_map/ppermute | solution.py:390
  397.2 15.9 %collective-permute-start.20 = (bf16[112,768]{1,0:T(8,128)(2,1)S(1)}, bf16[112,768]{1,0:T(8,128)(2,1)S(1)}, u32[]{:S(2)}, u32[]{:S(2)}) collective-permute-start(bf16[112,768]{1,0:T(8,128)(2,1)S(1)} %get-tuple-element.150), channel_id=1, source_target_pairs={{0,3},{1,0},{2,1},{3,2},{4,7},{5,4},{6,5},{7,6},{8,11},{9,8},{10,9... | collective-permute-start | bytes 516104 | tf_op jit(solution)/shard_map/ppermute | solution.py:687
  422.9 16.2 %collective-permute-start.25 = (bf16[112,768]{1,0:T(8,128)(2,1)}, bf16[112,768]{1,0:T(8,128)(2,1)S(1)}, u32[]{:S(2)}, u32[]{:S(2)}) collective-permute-start(bf16[112,768]{1,0:T(8,128)(2,1)} %get-tuple-element.119), channel_id=1, source_target_pairs={{0,20},{4,16},{8,28},{12,24},{16,4},{20,0},{24,12},{28,8},{1,21},{... | collective-permute-start | bytes 516104 | tf_op jit(solution)/shard_map/ppermute | solution.py:414
  423.6 16.2 %collective-permute-start.26 = (bf16[112,768]{1,0:T(8,128)(2,1)}, bf16[112,768]{1,0:T(8,128)(2,1)S(1)}, u32[]{:S(2)}, u32[]{:S(2)}) collective-permute-start(bf16[112,768]{1,0:T(8,128)(2,1)} %get-tuple-element.119), channel_id=1, source_target_pairs={{0,24},{4,28},{8,16},{12,20},{16,8},{20,12},{24,0},{28,4},{1,25},{... | collective-permute-start | bytes 516104 | tf_op jit(solution)/shard_map/ppermute | solution.py:414
  426.4 14.1 %collective-permute-start.27 = (bf16[112,768]{1,0:T(8,128)(2,1)}, bf16[112,768]{1,0:T(8,128)(2,1)S(1)}, u32[]{:S(2)}, u32[]{:S(2)}) collective-permute-start(bf16[112,768]{1,0:T(8,128)(2,1)} %get-tuple-element.119), channel_id=1, source_target_pairs={{0,28},{4,24},{8,20},{12,16},{16,12},{20,8},{24,4},{28,0},{1,29},{... | collective-permute-start | bytes 516104 | tf_op jit(solution)/shard_map/ppermute | solution.py:414
  (34 other events, 281.1 us)
Sparse Core Ops, SparseCore 0:
  23.8 35.9 all-gather.4
  61.6 65.4 all-gather.6
  185.2 87.6 reduce-scatter.2
  304.9 28.1 all-gather.8
  336.4 57.1 reduce-scatter.4

commit v4 on v3

--- a/solution.py
+++ b/solution.py
@@ -14,7 +14,8 @@
 LEN = 192
 EPSILON = 1e-05
 MASKED = -1e30
-QUERY_TILE = 256
+QUERY_TILE = 480
+TAKE = 2
 LANES = 128
 F32 = jnp.float32
 BF16 = jnp.bfloat16
@@ -114,11 +115,10 @@
                 if q0:
                     early = jnp.exp(early - peak)
                     total = total + jnp.sum(early, axis=0, keepdims=True)
-                inverse = 1.0 / total
-                out = dot_nn(vt_ref[lanes, q0:q1], (last * inverse).astype(BF16))
+                out = dot_nn(vt_ref[lanes, q0:q1], last.astype(BF16))
                 if q0:
-                    out = out + dot_nn(vt_ref[lanes, 0:q0], (early * inverse).astype(BF16))
-                outs.append(out)
+                    out = out + dot_nn(vt_ref[lanes, 0:q0], early.astype(BF16))
+                outs.append(out / total)
                 lse_ref[0, half : half + 1, q0:q1] = peak + jnp.log(total)
             o_ref[q0:q1, :] = jnp.concatenate(outs, axis=0).T.astype(BF16)
 
@@ -476,9 +476,9 @@
             gm_s[r0:r1, :] = jnp.where(live_rows(r0, r1), cot, jnp.zeros_like(cot))
             d_s[r0:r1, :] = jnp.zeros((r1 - r0, d_s.shape[1]), F32)
 
-    _, count, units, width = up_ref.shape
-    up = up_ref[...].reshape(count * units, width)
-    down = down_ref[...].reshape(count * units, width)
+    take, count, units, width = up_ref.shape
+    up = up_ref[...].reshape(take * count * units, width)
+    down = down_ref[...].reshape(take * count * units, width)
     n2 = n2_s[...]
     grad_m = gm_s[...]
     act, slope = gelu_parts(dot_nt(n2, up) + bup_ref[...])
@@ -486,8 +486,8 @@
     grad_u = (dot_nt(grad_m, down) * slope).astype(BF16)
     y_s[...] += dot_nn(act, down)
     d_s[...] += dot_nn(grad_u, up)
-    gblock_ref[0, :, 0:units, :] = dot_tn(grad_u, n2).reshape(count, units, width).astype(BF16)
-    gblock_ref[0, :, units : 2 * units, :] = dot_tn(act, grad_m).reshape(count, units, width).astype(BF16)
+    gblock_ref[:, :, 0:units, :] = dot_tn(grad_u, n2).astype(BF16).reshape(take, count, units, width)
+    gblock_ref[:, :, units : 2 * units, :] = dot_tn(act, grad_m).astype(BF16).reshape(take, count, units, width)
     gbup_ref[...] = jnp.sum(grad_u.astype(F32), axis=0, keepdims=True)
 
     @pl.when(step == pl.num_programs(0) - 1)
@@ -498,9 +498,11 @@
 
 def mlp(live, hidden, mixed, cot, vectors, bias_up, blocks, each):
     slots, width = hidden.shape
-    steps, groups = blocks.shape[:2]
+    spread, groups = blocks.shape[:2]
     units = 4 * each
-    chunk = groups * units
+    take = TAKE
+    steps = spread // take
+    chunk = take * groups * units
     one = pl.Buffered(1)
 
     def whole(shape):
@@ -516,7 +518,7 @@
             jax.ShapeDtypeStruct((slots, width), F32),
             jax.ShapeDtypeStruct((slots, 1), F32),
             jax.ShapeDtypeStruct((width, width), BF16),
-            jax.ShapeDtypeStruct((steps, groups, 2 * units, width), BF16),
+            jax.ShapeDtypeStruct((spread, groups, 2 * units, width), BF16),
             jax.ShapeDtypeStruct((1, steps * chunk), F32),
         ),
         grid_spec=pltpu.PrefetchScalarGridSpec(
@@ -525,12 +527,12 @@
             in_specs=[
                 full,
                 full,
-                pl.BlockSpec((steps, groups, each, width), lambda c, live: (0, 0, 8, 0), pipeline_mode=one),
+                pl.BlockSpec((spread, groups, each, width), lambda c, live: (0, 0, 8, 0), pipeline_mode=one),
                 full,
                 whole((8, width)),
                 pl.BlockSpec((1, chunk), lambda c, live: (0, c)),
-                pl.BlockSpec((1, groups, units, width), lambda c, live: (c, 0, 0, 0)),
-                pl.BlockSpec((1, groups, units, width), lambda c, live: (c, 0, 1, 0)),
+                pl.BlockSpec((take, groups, units, width), lambda c, live: (c, 0, 0, 0)),
+                pl.BlockSpec((take, groups, units, width), lambda c, live: (c, 0, 1, 0)),
             ],
             out_specs=(
                 full,
@@ -538,7 +540,7 @@
                 full,
                 whole((slots, 1)),
                 whole((width, width)),
-                pl.BlockSpec((1, groups, 2 * units, width), lambda c, live: (c, 0, 0, 0)),
+                pl.BlockSpec((take, groups, 2 * units, width), lambda c, live: (c, 0, 0, 0)),
                 pl.BlockSpec((1, chunk), lambda c, live: (0, c)),
             ),
             scratch_shapes=[
@@ -651,7 +653,7 @@
         mlp_block = mlp_block.reshape(groups, 2, spread, units, width).transpose(2, 0, 1, 3, 4)
         mlp_block = mlp_block.reshape(spread, groups, 2 * units, width)
     layer_part = to_slots(layer_out)
-    extra = 16
+    extra = 8 if spread * 8 >= 8 + PASSES else 16
     attn_block, grad_h, sums, grad_bias = attend_back(
         live_arg, query, keys, values, mixed, lse, matrix, n1, hidden, passes, grad_n2, xhat_two, inverse_two, cot,
         vectors, matrix_out, fold, groups, extra,
@@ -692,7 +694,7 @@
     attn_block = lax.psum_scatter(attn_block, "batch", scatter_dimension=0, tiled=True)[0]
     mlp_piece = over_tensor(mlp_block)
     attn_piece = over_tensor(attn_block)
-    mlp_whole = lax.all_gather(mlp_piece, "batch", axis=0, tiled=False)
+    mlp_whole = gather_batch(mlp_piece)
     attn_whole = gather_batch(attn_piece)
     parts = [attn_whole[:, part * each : (part + 1) * each].reshape(here, width).astype(F32) for part in range(4)]
     small = attn_whole[:, 4 * each :].reshape(spread * extra, width).astype(F32)

time: 463 us -> 453 us (0.978)
  Pallas kernels: 110 us -> 97.8 us
  starting transfers between devices: 31.7 us -> 40.3 us
  local copies, waits for them, and re-layouts: 49.5 us -> 44.4 us
    ppermute x7 -> x14, waiting for transfers between devices: 8.42 us -> 30.4 us  [gather_batch(): lax.ppermute(piece, 'batch', [(place, place ^ turn) for place in range(si...]
    reduce_scatter x1, waiting for transfers between devices: 16.5 us -> 0.01 us  [layer(): lax.psum_scatter(attn_block, 'batch', scatter_dimension=0, tiled=True)[0]]
    ppermute x7 -> x14, starting transfers between devices: 6.53 us -> 15.8 us  [gather_batch(): lax.ppermute(piece, 'batch', [(place, place ^ turn) for place in range(si...]
    reduce_scatter x1, waiting for transfers between devices: 44.4 us -> 36.2 us  [layer(): lax.psum_scatter(mlp_block, 'batch', scatter_dimension=0, tiled=True)[0]]
    ppermute x6, waiting for transfers between devices: 52 us -> 46.7 us  [to_slots(): piece = lax.ppermute(piece, 'tensor', ring_pairs(size, shift))]
    pallas_call x1, Pallas kernels: 47.4 us -> 42.2 us  [mlp(): pl.pallas_call(mlp_kernel, out_shape=(jax.ShapeDtypeStruct((slots, width)...]
    ppermute x6, waiting for transfers between devices: 24.1 us -> 29.1 us  [to_sequence(): lax.ppermute(piece, 'tensor', ring_pairs(size, shift))]
    pallas_call x1, Pallas kernels: 22.7 us -> 17.9 us  [attend(): pl.pallas_call(functools.partial(attend_kernel, each), out_shape=(shape,...]
  transfers between devices with their start and end apart: 36 -> 42, of which waited for: 25 -> 26; matrix products, arithmetic and copies ran while one was open for 11% -> 11% of each run, Pallas kernels for 14% -> 13%
where the time goes in v4:
time: 453 us; the launch traced here: 444 us
  waiting for transfers between devices  223 us (49%)
  Pallas kernels  97.8 us (22%)
  local copies, waits for them, and re-layouts  44.4 us (10%)
  starting transfers between devices  40.3 us (9%)
  other arithmetic  22 us (5%)
  between operations  17.1 us (4%)
    ppermute x6, waiting for transfers between devices, to_slots(): piece = lax.ppermute(piece, 'tensor', ring_pairs(size, shift))  46.7 us
    pallas_call x1, Pallas kernels, mlp(): pl.pallas_call(mlp_kernel, out_shape=(jax.ShapeDtypeStruct((slots, width)...  42.2 us
    ppermute x6, waiting for transfers between devices, over_tensor(): lax.ppermute(piece, 'tensor', ring_pairs(groups, shift)).astype(F32)  40.4 us
    ppermute x6, waiting for transfers between devices, gather_tensor(): lax.ppermute(piece, 'tensor', ring_pairs(size, shift))  39.8 us
    pallas_call x1, Pallas kernels, attend_back(): pl.pallas_call(functools.partial(attend_back_kernel, each), out_shape=(ja...  37.7 us
    reduce_scatter x1, waiting for transfers between devices, layer(): lax.psum_scatter(mlp_block, 'batch', scatter_dimension=0, tiled=True)[0]  36.2 us
    ppermute x14, waiting for transfers between devices, gather_batch(): lax.ppermute(piece, 'batch', [(place, place ^ turn) for place in range(si...  30.4 us
    ppermute x6, waiting for transfers between devices, to_sequence(): lax.ppermute(piece, 'tensor', ring_pairs(size, shift))  29.1 us
  transfers between devices with their start and end apart: 42, of which 26 were waited for; matrix products, arithmetic and copies ran while one was open for 11% of the time, Pallas kernels for 13%

profile of v4, /device:TPU:9, one launch (start us, length us, event | category | flops | bytes accessed | tf_op | source)
XLA Modules:
  0.0 444.2 jit_solution(21541614123002104)
XLA Ops:
  13.1 7.0 %collective-permute-done.7 = bf16[80,768]{1,0:T(8,128)(2,1)S(1)} collective-permute-done((bf16[80,768]{1,0:T(8,128)(2,1)S(1)}, bf16[80,768]{1,0:T(8,128)(2,1)S(1)}, u32[]{:S(2)}, u32[]{:S(2)}) %collective-permute-start.7) | collective-permute-done | bytes 122912 | tf_op jit(solution)/shard_map/ppermute | solution.py:401
  27.8 7.4 %collective-permute-done.9 = bf16[224,768]{1,0:T(8,128)(2,1)S(1)} collective-permute-done((bf16[224,768]{1,0:T(8,128)(2,1)S(1)}, bf16[224,768]{1,0:T(8,128)(2,1)S(1)}, u32[]{:S(2)}, u32[]{:S(2)}) %collective-permute-start.9) | collective-permute-done | bytes 344096 | tf_op jit(solution)/shard_map/ppermute | solution.py:401
  35.2 20.1 %collective-permute-done.10 = bf16[224,768]{1,0:T(8,128)(2,1)S(1)} collective-permute-done((bf16[224,768]{1,0:T(8,128)(2,1)S(1)}, bf16[224,768]{1,0:T(8,128)(2,1)S(1)}, u32[]{:S(2)}, u32[]{:S(2)}) %collective-permute-start.10) | collective-permute-done | bytes 344096 | tf_op jit(solution)/shard_map/ppermute | solution.py:401
  68.8 5.5 %add_select_fusion.pass_ref = s32[960,1]{1,0:T(8,128)} fusion(s32[]{:T(128)S(6)} %select_n.324, pred[]{:T(512)S(6)} %lt.308), kind=kLoop, calls=%fused_computation.10 | loop fusion | flops 6720 | bytes 3845 | tf_op jit(solution)/shard_map/jit(remainder)/select_n | solution.py:632
  76.0 16.0 %collective-permute-done.1 = bf16[240,768]{1,0:T(8,128)(2,1)S(1)} collective-permute-done((bf16[240,768]{1,0:T(8,128)(2,1)S(1)}, bf16[240,768]{1,0:T(8,128)(2,1)S(1)}, u32[]{:S(2)}, u32[]{:S(2)}) %collective-permute-start.1) | collective-permute-done | bytes 368672 | tf_op jit(solution)/shard_map/ppermute | solution.py:372
  106.6 17.9 %attend.1 = (bf16[960,768]{1,0:T(8,128)(2,1)}, bf16[960,768]{1,0:T(8,128)(2,1)}, bf16[960,768]{1,0:T(8,128)(2,1)}, bf16[960,768]{1,0:T(8,128)(2,1)}, f32[6,2,960]{2,1,0:T(2,128)}, /*index=5*/bf16[6,384,768]{2,1,0:T(8,128)(2,1)}) custom-call(s32[1]{0:T(128)} %bitcast.1.live_ref, bf16[960,768]{1,0:T(8,128)(2,1)} %add_convert_fusion.n1_ref, ...), custom_call_target="tpu_custom_call" | custom-call | flops 6228541440 | bytes 11796480 | tf_op jit(solution)/shard_map/attend/pallas_call | solution.py:253
  124.5 8.3 %collective-permute-done.4 = bf16[240,768]{1,0:T(8,128)(2,1)S(1)} collective-permute-done((bf16[240,768]{1,0:T(8,128)(2,1)S(1)}, bf16[240,768]{1,0:T(8,128)(2,1)S(1)}, u32[]{:S(2)}, u32[]{:S(2)}) %collective-permute-start.4) | collective-permute-done | bytes 368672 | tf_op jit(solution)/shard_map/ppermute | solution.py:372
  132.8 3.3 collective-permute-done.5
  139.7 42.2 %mlp.1 = (bf16[960,768]{1,0:T(8,128)(2,1)}, f32[960,768]{1,0:T(8,128)}, f32[960,768]{1,0:T(8,128)}, f32[960,1]{1,0:T(8,128)}, bf16[768,768]{1,0:T(8,128)(2,1)}, ...) custom-call(s32[1]{0:T(128)} %bitcast.1.live_ref, f32[960,768]{1,0:T(8,128)} %copy-done.2, ...), custom_call_target="tpu_custom_call" | custom-call | flops 30576476160 | bytes 33619968 | tf_op jit(solution)/shard_map/mlp/pallas_call | solution.py:513
  182.0 37.7 %attend_back.1 = (bf16[8,4,104,768]{3,2,1,0:T(8,128)(2,1)}, bf16[960,768]{1,0:T(8,128)(2,1)}, f32[16,768]{1,0:T(8,128)}, f32[6,1,384]{2,1,0:T(1,128)}) custom-call(s32[1]{0:T(128)} %bitcast.1.live_ref, bf16[960,768]{1,0:T(8,128)(2,1)} %get-tuple-element.54.q_ref, bf16[960,768]{1,0:T(8,128)(2,1)} %get-tuple-element.55.k_ref, ...), custom_call_target="tpu_custom_call" | custom-call | flops 16137584640 | bytes 29491200 | tf_op jit(solution)/shard_map/attend_back/pallas_call | solution.py:304
  222.5 36.2 %reduce-scatter.3.cloned.1.call-done = bf16[1,4,192,768]{3,2,1,0:T(8,128)(2,1)} async-done(((bf16[8,4,192,768]{3,2,1,0:T(8,128)(2,1)}), bf16[1,4,192,768]{3,2,1,0:T(8,128)(2,1)}) %reduce-scatter.3.cloned.1.call-update) | async-done | bytes 1179664 | tf_op jit(solution)/shard_map/reduce_scatter | solution.py:692
  266.7 3.0 collective-permute-start.29
  273.8 20.5 %collective-permute-done.16 = bf16[240,768]{1,0:T(8,128)(2,1)S(1)} collective-permute-done((bf16[240,768]{1,0:T(8,128)(2,1)S(1)}, bf16[240,768]{1,0:T(8,128)(2,1)S(1)}, u32[]{:S(2)}, u32[]{:S(2)}) %collective-permute-start.16) | collective-permute-done | bytes 368672 | tf_op jit(solution)/shard_map/ppermute | solution.py:390
  294.3 14.7 %collective-permute-done.17 = bf16[240,768]{1,0:T(8,128)(2,1)S(1)} collective-permute-done((bf16[240,768]{1,0:T(8,128)(2,1)S(1)}, bf16[240,768]{1,0:T(8,128)(2,1)S(1)}, u32[]{:S(2)}, u32[]{:S(2)}) %collective-permute-start.17) | collective-permute-done | bytes 368672 | tf_op jit(solution)/shard_map/ppermute | solution.py:390
  309.0 6.3 %collective-permute-done.28 = bf16[192,768]{1,0:T(8,128)(2,1)S(1)} collective-permute-done((bf16[192,768]{1,0:T(8,128)(2,1)S(1)}, bf16[192,768]{1,0:T(8,128)(2,1)S(1)}, u32[]{:S(2)}, u32[]{:S(2)}) %collective-permute-start.28) | collective-permute-done | bytes 294944 | tf_op jit(solution)/shard_map/ppermute | solution.py:689
  315.3 18.9 %collective-permute-done.29 = bf16[192,768]{1,0:T(8,128)(2,1)S(1)} collective-permute-done((bf16[192,768]{1,0:T(8,128)(2,1)S(1)}, bf16[192,768]{1,0:T(8,128)(2,1)S(1)}, u32[]{:S(2)}, u32[]{:S(2)}) %collective-permute-start.29) | collective-permute-done | bytes 294944 | tf_op jit(solution)/shard_map/ppermute | solution.py:689
  334.3 3.2 collective-permute-done.30
  338.5 3.7 collective-permute-done.12
  343.5 6.6 %collective-permute-done.13 = bf16[240,768]{1,0:T(8,128)(2,1)S(1)} collective-permute-done((bf16[240,768]{1,0:T(8,128)(2,1)S(1)}, bf16[240,768]{1,0:T(8,128)(2,1)S(1)}, u32[]{:S(2)}, u32[]{:S(2)}) %collective-permute-start.13) | collective-permute-done | bytes 368672 | tf_op jit(solution)/shard_map/ppermute | solution.py:390
  350.1 2.8 collective-permute-start.33
  361.7 16.1 %collective-permute-done.34 = bf16[192,768]{1,0:T(8,128)(2,1)S(1)} collective-permute-done((bf16[192,768]{1,0:T(8,128)(2,1)S(1)}, bf16[192,768]{1,0:T(8,128)(2,1)S(1)}, u32[]{:S(2)}, u32[]{:S(2)}) %collective-permute-start.34) | collective-permute-done | bytes 294944 | tf_op jit(solution)/shard_map/ppermute | solution.py:414
  377.8 7.0 %collective-permute-done.35 = bf16[192,768]{1,0:T(8,128)(2,1)S(1)} collective-permute-done((bf16[192,768]{1,0:T(8,128)(2,1)S(1)}, bf16[192,768]{1,0:T(8,128)(2,1)S(1)}, u32[]{:S(2)}, u32[]{:S(2)}) %collective-permute-start.35) | collective-permute-done | bytes 294944 | tf_op jit(solution)/shard_map/ppermute | solution.py:414
  393.1 8.2 %collective-permute-done.19 = bf16[104,768]{1,0:T(8,128)(2,1)S(1)} collective-permute-done((bf16[104,768]{1,0:T(8,128)(2,1)S(1)}, bf16[104,768]{1,0:T(8,128)(2,1)S(1)}, u32[]{:S(2)}, u32[]{:S(2)}) %collective-permute-start.19) | collective-permute-done | bytes 159776 | tf_op jit(solution)/shard_map/ppermute | solution.py:689
  421.5 7.4 %collective-permute-done.25 = bf16[104,768]{1,0:T(8,128)(2,1)S(1)} collective-permute-done((bf16[104,768]{1,0:T(8,128)(2,1)}, bf16[104,768]{1,0:T(8,128)(2,1)S(1)}, u32[]{:S(2)}, u32[]{:S(2)}) %collective-permute-start.25) | collective-permute-done | bytes 159776 | tf_op jit(solution)/shard_map/ppermute | solution.py:414
  (234 shorter events, 107.4 us)
Async XLA Ops:
  7.2 97.7 %all-gather.3.cloned.1.call-start = ((), (), s32[]{:S(2)}) async-start(), calls=%async_computation.2 | async-start | bytes 4423680 | tf_op jit(solution)/shard_map/all_gather | solution.py:599
  23.7 114.3 %all-gather.5.cloned.1.call-start = ((), (), s32[]{:S(2)}) async-start(), calls=%async_computation.3 | async-start | bytes 12386304 | tf_op jit(solution)/shard_map/all_gather | solution.py:602
  26.0 29.3 %collective-permute-start.10 = (bf16[224,768]{1,0:T(8,128)(2,1)S(1)}, bf16[224,768]{1,0:T(8,128)(2,1)S(1)}, u32[]{:S(2)}, u32[]{:S(2)}) collective-permute-start(bf16[224,768]{1,0:T(8,128)(2,1)S(1)} %get-tuple-element.154), channel_id=1, source_target_pairs={{0,2},{1,3},{2,0},{3,1},{4,6},{5,7},{6,4},{7,5},{8,10},{9,11},{10,... | collective-permute-start | bytes 1032200 | tf_op jit(solution)/shard_map/ppermute | solution.py:401
  26.6 30.8 %collective-permute-start.11 = (bf16[224,768]{1,0:T(8,128)(2,1)S(1)}, bf16[224,768]{1,0:T(8,128)(2,1)S(1)}, u32[]{:S(2)}, u32[]{:S(2)}) collective-permute-start(bf16[224,768]{1,0:T(8,128)(2,1)S(1)} %get-tuple-element.154), channel_id=1, source_target_pairs={{0,3},{1,0},{2,1},{3,2},{4,7},{5,4},{6,5},{7,6},{8,11},{9,8},{10,9... | collective-permute-start | bytes 1032200 | tf_op jit(solution)/shard_map/ppermute | solution.py:401
  58.5 200.1 %reduce-scatter.3.cloned.1.call-start = ((), (), s32[]{:S(2)}) async-start(), calls=%async_computation.4 | async-start | bytes 10616832 | tf_op jit(solution)/shard_map/reduce_scatter | solution.py:692
  60.5 31.5 %collective-permute-start.1 = (bf16[240,768]{1,0:T(8,128)(2,1)S(1)}, bf16[240,768]{1,0:T(8,128)(2,1)S(1)}, u32[]{:S(2)}, u32[]{:S(2)}) collective-permute-start(bf16[240,768]{1,0:T(8,128)(2,1)S(1)} %get-tuple-element.139), channel_id=1, source_target_pairs={{0,2},{1,3},{2,0},{3,1},{4,6},{5,7},{6,4},{7,5},{8,10},{9,11},{10,... | collective-permute-start | bytes 1105928 | tf_op jit(solution)/shard_map/ppermute | solution.py:372
  61.6 32.7 %collective-permute-start.2 = (bf16[240,768]{1,0:T(8,128)(2,1)S(1)}, bf16[240,768]{1,0:T(8,128)(2,1)S(1)}, u32[]{:S(2)}, u32[]{:S(2)}) collective-permute-start(bf16[240,768]{1,0:T(8,128)(2,1)S(1)} %get-tuple-element.138), channel_id=1, source_target_pairs={{0,3},{1,0},{2,1},{3,2},{4,7},{5,4},{6,5},{7,6},{8,11},{9,8},{10,9... | collective-permute-start | bytes 1105928 | tf_op jit(solution)/shard_map/ppermute | solution.py:372
  101.3 23.2 %collective-permute-start.3 = (bf16[240,768]{1,0:T(8,128)(2,1)S(1)}, bf16[240,768]{1,0:T(8,128)(2,1)S(1)}, u32[]{:S(2)}, u32[]{:S(2)}) collective-permute-start(bf16[240,768]{1,0:T(8,128)(2,1)S(1)} %get-tuple-element.136), channel_id=1, source_target_pairs={{0,1},{1,2},{2,3},{3,0},{4,5},{5,6},{6,7},{7,4},{8,9},{9,10},{10,1... | collective-permute-start | bytes 1105928 | tf_op jit(solution)/shard_map/ppermute | solution.py:372
  101.4 31.4 %collective-permute-start.4 = (bf16[240,768]{1,0:T(8,128)(2,1)S(1)}, bf16[240,768]{1,0:T(8,128)(2,1)S(1)}, u32[]{:S(2)}, u32[]{:S(2)}) collective-permute-start(bf16[240,768]{1,0:T(8,128)(2,1)S(1)} %get-tuple-element.135), channel_id=1, source_target_pairs={{0,2},{1,3},{2,0},{3,1},{4,6},{5,7},{6,4},{7,5},{8,10},{9,11},{10,... | collective-permute-start | bytes 1105928 | tf_op jit(solution)/shard_map/ppermute | solution.py:372
  103.4 32.7 %collective-permute-start.5 = (bf16[240,768]{1,0:T(8,128)(2,1)S(1)}, bf16[240,768]{1,0:T(8,128)(2,1)S(1)}, u32[]{:S(2)}, u32[]{:S(2)}) collective-permute-start(bf16[240,768]{1,0:T(8,128)(2,1)S(1)} %get-tuple-element.134), channel_id=1, source_target_pairs={{0,3},{1,0},{2,1},{3,2},{4,7},{5,4},{6,5},{7,6},{8,11},{9,8},{10,9... | collective-permute-start | bytes 1105928 | tf_op jit(solution)/shard_map/ppermute | solution.py:372
  181.9 204.2 %reduce-scatter.5.cloned.1.call-start = ((), (), s32[]{:S(2)}) async-start(), calls=%async_computation.5 | async-start | bytes 5750784 | tf_op jit(solution)/shard_map/reduce_scatter | solution.py:694
  262.2 32.1 %collective-permute-start.16 = (bf16[240,768]{1,0:T(8,128)(2,1)S(1)}, bf16[240,768]{1,0:T(8,128)(2,1)S(1)}, u32[]{:S(2)}, u32[]{:S(2)}) collective-permute-start(bf16[240,768]{1,0:T(8,128)(2,1)S(1)} %get-tuple-element.127), channel_id=1, source_target_pairs={{0,2},{1,3},{2,0},{3,1},{4,6},{5,7},{6,4},{7,5},{8,10},{9,11},{10,... | collective-permute-start | bytes 1105928 | tf_op jit(solution)/shard_map/ppermute | solution.py:390
  263.3 45.7 %collective-permute-start.17 = (bf16[240,768]{1,0:T(8,128)(2,1)S(1)}, bf16[240,768]{1,0:T(8,128)(2,1)S(1)}, u32[]{:S(2)}, u32[]{:S(2)}) collective-permute-start(bf16[240,768]{1,0:T(8,128)(2,1)S(1)} %get-tuple-element.126), channel_id=1, source_target_pairs={{0,3},{1,0},{2,1},{3,2},{4,7},{5,4},{6,5},{7,6},{8,11},{9,8},{10,9... | collective-permute-start | bytes 1105928 | tf_op jit(solution)/shard_map/ppermute | solution.py:390
  266.5 48.9 %collective-permute-start.28 = (bf16[192,768]{1,0:T(8,128)(2,1)S(1)}, bf16[192,768]{1,0:T(8,128)(2,1)S(1)}, u32[]{:S(2)}, u32[]{:S(2)}) collective-permute-start(bf16[192,768]{1,0:T(8,128)(2,1)S(1)} %get-tuple-element.145), channel_id=1, source_target_pairs={{0,1},{1,2},{2,3},{3,0},{4,5},{5,6},{6,7},{7,4},{8,9},{9,10},{10,1... | collective-permute-start | bytes 884744 | tf_op jit(solution)/shard_map/ppermute | solution.py:689
  266.7 67.5 %collective-permute-start.29 = (bf16[192,768]{1,0:T(8,128)(2,1)S(1)}, bf16[192,768]{1,0:T(8,128)(2,1)S(1)}, u32[]{:S(2)}, u32[]{:S(2)}) collective-permute-start(bf16[192,768]{1,0:T(8,128)(2,1)S(1)} %get-tuple-element.147), channel_id=1, source_target_pairs={{0,2},{1,3},{2,0},{3,1},{4,6},{5,7},{6,4},{7,5},{8,10},{9,11},{10,... | collective-permute-start | bytes 884744 | tf_op jit(solution)/shard_map/ppermute | solution.py:689
  270.6 66.9 %collective-permute-start.30 = (bf16[192,768]{1,0:T(8,128)(2,1)S(1)}, bf16[192,768]{1,0:T(8,128)(2,1)S(1)}, u32[]{:S(2)}, u32[]{:S(2)}) collective-permute-start(bf16[192,768]{1,0:T(8,128)(2,1)S(1)} %get-tuple-element.146), channel_id=1, source_target_pairs={{0,3},{1,0},{2,1},{3,2},{4,7},{5,4},{6,5},{7,6},{8,11},{9,8},{10,9... | collective-permute-start | bytes 884744 | tf_op jit(solution)/shard_map/ppermute | solution.py:689
  294.2 47.9 %collective-permute-start.12 = (bf16[240,768]{1,0:T(8,128)(2,1)S(1)}, bf16[240,768]{1,0:T(8,128)(2,1)S(1)}, u32[]{:S(2)}, u32[]{:S(2)}) collective-permute-start(bf16[240,768]{1,0:T(8,128)(2,1)S(1)} %get-tuple-element.132), channel_id=1, source_target_pairs={{0,1},{1,2},{2,3},{3,0},{4,5},{5,6},{6,7},{7,4},{8,9},{9,10},{10,1... | collective-permute-start | bytes 1105928 | tf_op jit(solution)/shard_map/ppermute | solution.py:390
  309.0 41.1 %collective-permute-start.13 = (bf16[240,768]{1,0:T(8,128)(2,1)S(1)}, bf16[240,768]{1,0:T(8,128)(2,1)S(1)}, u32[]{:S(2)}, u32[]{:S(2)}) collective-permute-start(bf16[240,768]{1,0:T(8,128)(2,1)S(1)} %get-tuple-element.131), channel_id=1, source_target_pairs={{0,2},{1,3},{2,0},{3,1},{4,6},{5,7},{6,4},{7,5},{8,10},{9,11},{10,... | collective-permute-start | bytes 1105928 | tf_op jit(solution)/shard_map/ppermute | solution.py:390
  315.3 37.9 %collective-permute-start.14 = (bf16[240,768]{1,0:T(8,128)(2,1)S(1)}, bf16[240,768]{1,0:T(8,128)(2,1)S(1)}, u32[]{:S(2)}, u32[]{:S(2)}) collective-permute-start(bf16[240,768]{1,0:T(8,128)(2,1)S(1)} %get-tuple-element.130), channel_id=1, source_target_pairs={{0,3},{1,0},{2,1},{3,2},{4,7},{5,4},{6,5},{7,6},{8,11},{9,8},{10,9... | collective-permute-start | bytes 1105928 | tf_op jit(solution)/shard_map/ppermute | solution.py:390
  337.8 21.4 %collective-permute-start.31 = (bf16[192,768]{1,0:T(8,128)(2,1)S(1)}, bf16[192,768]{1,0:T(8,128)(2,1)S(1)}, u32[]{:S(2)}, u32[]{:S(2)}) collective-permute-start(bf16[192,768]{1,0:T(8,128)(2,1)S(1)} %get-tuple-element.119), channel_id=1, source_target_pairs={{0,4},{4,0},{8,12},{12,8},{16,20},{20,16},{24,28},{28,24},{1,5},{5... | collective-permute-start | bytes 884744 | tf_op jit(solution)/shard_map/ppermute | solution.py:414
  357.0 20.7 %collective-permute-start.34 = (bf16[192,768]{1,0:T(8,128)(2,1)S(1)}, bf16[192,768]{1,0:T(8,128)(2,1)S(1)}, u32[]{:S(2)}, u32[]{:S(2)}) collective-permute-start(bf16[192,768]{1,0:T(8,128)(2,1)S(1)} %get-tuple-element.119), channel_id=1, source_target_pairs={{0,16},{4,20},{8,24},{12,28},{16,0},{20,4},{24,8},{28,12},{1,17},{... | collective-permute-start | bytes 884744 | tf_op jit(solution)/shard_map/ppermute | solution.py:414
  358.2 26.5 %collective-permute-start.35 = (bf16[192,768]{1,0:T(8,128)(2,1)S(1)}, bf16[192,768]{1,0:T(8,128)(2,1)S(1)}, u32[]{:S(2)}, u32[]{:S(2)}) collective-permute-start(bf16[192,768]{1,0:T(8,128)(2,1)S(1)} %get-tuple-element.119), channel_id=1, source_target_pairs={{0,20},{4,16},{8,28},{12,24},{16,4},{20,0},{24,12},{28,8},{1,21},{... | collective-permute-start | bytes 884744 | tf_op jit(solution)/shard_map/ppermute | solution.py:414
  359.2 25.6 %collective-permute-start.36 = (bf16[192,768]{1,0:T(8,128)(2,1)S(1)}, bf16[192,768]{1,0:T(8,128)(2,1)S(1)}, u32[]{:S(2)}, u32[]{:S(2)}) collective-permute-start(bf16[192,768]{1,0:T(8,128)(2,1)S(1)} %get-tuple-element.119), channel_id=1, source_target_pairs={{0,24},{4,28},{8,16},{12,20},{16,8},{20,12},{24,0},{28,4},{1,25},{... | collective-permute-start | bytes 884744 | tf_op jit(solution)/shard_map/ppermute | solution.py:414
  360.4 24.4 %collective-permute-start.37 = (bf16[192,768]{1,0:T(8,128)(2,1)S(1)}, bf16[192,768]{1,0:T(8,128)(2,1)S(1)}, u32[]{:S(2)}, u32[]{:S(2)}) collective-permute-start(bf16[192,768]{1,0:T(8,128)(2,1)S(1)} %get-tuple-element.119), channel_id=1, source_target_pairs={{0,28},{4,24},{8,20},{12,16},{16,12},{20,8},{24,4},{28,0},{1,29},{... | collective-permute-start | bytes 884744 | tf_op jit(solution)/shard_map/ppermute | solution.py:414
  (40 other events, 341.0 us)
Sparse Core Ops, SparseCore 0:
  23.8 35.9 all-gather.2
  61.6 65.3 all-gather.4
  182.0 76.6 reduce-scatter.2
  262.1 55.7 reduce-scatter.4
